TPU v7x, 32 devices: a whole 2x2x4 slice. The times are simulated.
32 devices in a mesh: dp: 8 (over y, x, core), chan: 4 (over z).
Axes of the slice: x: 2, y: 2, z: 4, core: 2. Of those that a mesh axis runs over, the one named last changes fastest.
Arguments:
- signal: bfloat16 [8, 512, 8192], P('dp', 'chan'), may hold values from -6 to 6
- signal_grad: bfloat16 [8, 512, 8192], P('dp', 'chan'), may hold values from -6 to 6
- embed_weight: float32 [64, 33], replicated, may hold values from -1 to 1
- embed_bias: float32 [64], replicated, may hold values from -3.140625 to 3.140625
- hidden_weight: float32 [64, 64], replicated, may hold values from -0.75 to 0.75
- frequency: float32 [2, 64], replicated, may hold values from 0.5 to 2
- output_weight: float32 [512, 64], replicated, may hold values from -0.75 to 0.75
- decay_rate: float32 [512], replicated, may hold values from 0.3 to 30
Outputs:
- filter_grad: float32 [512, 16384], P(None, ('dp', 'chan'))
- embed_grad: float32 [64, 33], replicated
- bias_grad: float32 [64], replicated
- hidden_grad: float32 [64, 64], replicated
- frequency_grad: float32 [2, 64], replicated
- output_grad: float32 [512, 64], replicated
- decay_grad: float32 [512], replicated
All inputs are finite; a program needn't handle non-finite values.
Results may differ from a plain program's by a relative error of at most 0.0003.
Values may be sent and summed in bfloat16 or wider, within the bound.
No kernel may reach another device: no remote copies, remote signals or barrier semaphores. Data moves between devices by JAX's collectives and lax.ppermute only.
A program may use at most 64 MiB of HBM per device.

v0:
```python
import math

import jax
import jax.numpy as jnp
from jax import lax
from jax.sharding import PartitionSpec as P


def lag_features(lag, length, bands):
    total = 2 * length
    scaled = lag.astype(jnp.float32) / length
    sines = []
    cosines = []
    for band in range(bands):
        factor = max(1, int(0.45 * total * 10000.0 ** (-band / bands)))
        phase = (lag * factor % total).astype(jnp.float32) * (2.0 * math.pi / total)
        sines.append(jnp.sin(phase))
        cosines.append(jnp.cos(phase))
    return jnp.stack([scaled] + sines + cosines)


def filter_loss(params, lag, cotangent, length):
    embed_weight, embed_bias, hidden_weight, frequency, output_weight, decay_rate = params
    bands = (embed_weight.shape[1] - 1) // 2
    exact = lax.Precision.HIGHEST
    table = lag_features(lag, length, bands)
    first = jnp.sin(
        frequency[0][:, None]
        * (
            jnp.dot(embed_weight, table, precision=exact, preferred_element_type=jnp.float32)
            + embed_bias[:, None]
        )
    )
    second = jnp.sin(
        frequency[1][:, None]
        * jnp.dot(hidden_weight, first, precision=exact, preferred_element_type=jnp.float32)
    )
    shaped = jnp.dot(output_weight, second, precision=exact, preferred_element_type=jnp.float32)
    window = jnp.exp(-decay_rate[:, None] * jnp.abs(lag).astype(jnp.float32)[None, :] / length)
    return jnp.sum(shaped * window * cotangent) / math.sqrt(2 * length)


def plan_sizes(total):
    bits = total.bit_length() - 1
    side = 2 ** min(7, bits // 2)
    return (total // (side * side), side, side)


def rotation(rows, cols, modulus, sign):
    row_index = jnp.arange(rows, dtype=jnp.int32)
    col_index = jnp.arange(cols, dtype=jnp.int32)
    product = row_index[:, None] * col_index[None, :] % modulus
    angle = product.astype(jnp.float32) * (-2.0 * math.pi / modulus)
    return (jnp.cos(angle), sign * jnp.sin(angle))


def twist(real_part, imag_part, table):
    cosine, sine = table
    return (real_part * cosine - imag_part * sine, real_part * sine + imag_part * cosine)


def table_product(spec, table, real_part, imag_part, table_first):
    cosine, sine = table
    exact = lax.Precision.HIGHEST

    def apply(matrix, values):
        if table_first:
            return jnp.einsum(
                spec, matrix, values, precision=exact, preferred_element_type=jnp.float32
            )
        return jnp.einsum(spec, values, matrix, precision=exact, preferred_element_type=jnp.float32)

    common = apply(cosine, real_part + imag_part)
    return (common - apply(cosine + sine, imag_part), common + apply(sine - cosine, real_part))


def forward(real_part, imag_part, total):
    outer, middle, inner = plan_sizes(total)
    leading = real_part.shape[:-1]
    real_part = real_part.reshape(leading + (outer, middle * inner))
    imag_part = imag_part.reshape(leading + (outer, middle * inner))
    real_part, imag_part = table_product(
        "kp,...pm->...km", rotation(outer, outer, outer, 1.0), real_part, imag_part, True
    )
    real_part, imag_part = twist(real_part, imag_part, rotation(outer, middle * inner, total, 1.0))
    real_part = real_part.reshape(leading + (outer, middle, inner))
    imag_part = imag_part.reshape(leading + (outer, middle, inner))
    real_part, imag_part = table_product(
        "aq,...kqr->...kar", rotation(middle, middle, middle, 1.0), real_part, imag_part, True
    )
    real_part, imag_part = twist(real_part, imag_part, rotation(middle, inner, middle * inner, 1.0))
    return table_product(
        "...kar,rb->...kab", rotation(inner, inner, inner, 1.0), real_part, imag_part, False
    )


def inverse(real_part, imag_part, total):
    outer, middle, inner = plan_sizes(total)
    leading = real_part.shape[:-3]
    exact = lax.Precision.HIGHEST
    real_part, imag_part = table_product(
        "...kab,rb->...kar", rotation(inner, inner, inner, -1.0), real_part, imag_part, False
    )
    real_part, imag_part = twist(
        real_part, imag_part, rotation(middle, inner, middle * inner, -1.0)
    )
    real_part, imag_part = table_product(
        "qa,...kar->...kqr", rotation(middle, middle, middle, -1.0), real_part, imag_part, True
    )
    real_part = real_part.reshape(leading + (outer, middle * inner))
    imag_part = imag_part.reshape(leading + (outer, middle * inner))
    real_part, imag_part = twist(real_part, imag_part, rotation(outer, middle * inner, total, -1.0))
    cosine, sine = rotation(outer, outer, outer, -1.0)
    result = jnp.einsum(
        "pk,...km->...pm", cosine, real_part, precision=exact, preferred_element_type=jnp.float32
    )
    result = result - jnp.einsum(
        "pk,...km->...pm", sine, imag_part, precision=exact, preferred_element_type=jnp.float32
    )
    return result.reshape(leading + (total,)) / total


def mirror(values):
    flipped = jnp.flip(values, (-3, -2, -1))
    shifted = jnp.roll(flipped, 1, axis=-3)
    head = jnp.roll(shifted[..., 0, :, :], 1, axis=-2)
    first_row = (jnp.arange(head.shape[-2]) == 0)[:, None]
    head = jnp.where(first_row, jnp.roll(head, 1, axis=-1), head)
    return jnp.concatenate([head[..., None, :, :], shifted[..., 1:, :, :]], axis=-3)


def block_spectrum(inputs, grads, total):
    padding = jnp.zeros(inputs.shape[:-1] + (total - inputs.shape[-1],), jnp.float32)
    real_part = jnp.concatenate([inputs.astype(jnp.float32), padding], axis=-1)
    imag_part = jnp.concatenate([grads.astype(jnp.float32), padding], axis=-1)
    spectrum_real, spectrum_imag = forward(real_part, imag_part, total)
    back_real = mirror(spectrum_real)
    back_imag = -mirror(spectrum_imag)
    in_real = 0.5 * (spectrum_real + back_real)
    in_imag = 0.5 * (spectrum_imag + back_imag)
    grad_real = 0.5 * (spectrum_imag - back_imag)
    grad_imag = -0.5 * (spectrum_real - back_real)
    cross_real = in_real * grad_real + in_imag * grad_imag
    cross_imag = in_real * grad_imag - in_imag * grad_real
    return (jnp.sum(cross_real, axis=0), jnp.sum(cross_imag, axis=0))


def local(
    signal,
    signal_grad,
    embed_weight,
    embed_bias,
    hidden_weight,
    frequency,
    output_weight,
    decay_rate,
):
    seq_local, chan_local, length = signal.shape
    total = 2 * length
    block = 8
    scale = 1.0 / math.sqrt(seq_local * lax.axis_size("dp") * length)
    indices = jnp.arange(chan_local // block, dtype=jnp.int32)

    def spectrum_of(index):
        start = index * block
        inputs = lax.dynamic_slice_in_dim(signal, start, block, 1)
        grads = lax.dynamic_slice_in_dim(signal_grad, start, block, 1)
        return block_spectrum(inputs, grads, total)

    def lags_of(index):
        cross_real, cross_imag = spectrum_of(index)
        return inverse(cross_real, cross_imag, total)

    correlation = lax.map(lags_of, indices).reshape(chan_local, total) * scale
    shared = lax.psum_scatter(correlation, "dp", scatter_dimension=1, tiled=True)
    filter_grad = lax.all_to_all(shared, "chan", split_axis=1, concat_axis=0, tiled=True)
    lag_count = filter_grad.shape[1]
    device_rank = lax.axis_index("dp") * lax.axis_size("chan") + lax.axis_index("chan")
    position = device_rank * lag_count + jnp.arange(lag_count, dtype=jnp.int32)
    lag = jnp.where(position < length, position, position - total)
    params = (embed_weight, embed_bias, hidden_weight, frequency, output_weight, decay_rate)
    local_grads = jax.grad(filter_loss)(params, lag, filter_grad, length)
    summed = lax.psum(
        (
            local_grads[0],
            local_grads[1],
            local_grads[2],
            local_grads[3],
            local_grads[4],
            local_grads[5],
        ),
        ("dp", "chan"),
    )
    return (filter_grad, summed[0], summed[1], summed[2], summed[3], summed[4], summed[5])


def solution(mesh):
    placed = (P("dp", "chan", None), P("dp", "chan", None), P(), P(), P(), P(), P(), P())
    return jax.shard_map(
        local,
        mesh=mesh,
        in_specs=placed,
        out_specs=(P(None, ("dp", "chan")), P(), P(), P(), P(), P(), P()),
        check_vma=False,
    )
```

profile of v0, /device:TPU:0, one launch (start us, length us, event | category | flops | bytes accessed | tf_op | source)
XLA Modules:
  0.0 587.0 jit_solution(18230572061578156664)
XLA Ops:
  7.2 325.0 %while.13 = (s32[]{:T(128)}, f32[16,8,16384]{2,1,0:T(8,128)}, s32[16]{0:T(128)S(1)}, bf16[1,128,8192]{2,1,0:T(8,128)(2,1)}, bf16[1,128,8192]{2,1,0:T(8,128)(2,1)...) while((s32[]{:T(128)}, f32[16,8,16384]{2,1,0:T(8,128)}, s32[16]{0:T(128)S(1)}, ...), condition=%wide.region_1.2_spmd, body=%wide.region_0.1_spmd.sunk | while | flops 2430353408 | bytes 44499364 | solution.py:174
  13.4 1.3 fusion.309
  33.7 1.3 fusion.309
  54.0 1.3 fusion.309
  74.4 1.3 fusion.309
  94.7 1.3 fusion.309
  115.0 1.3 fusion.309
  135.3 1.3 fusion.309
  155.6 1.3 fusion.309
  175.9 1.3 fusion.309
  196.3 1.3 fusion.309
  216.6 1.3 fusion.309
  332.3 7.4 %multiply_bitcast_fusion = f32[128,16384]{1,0:T(8,128)} fusion(f32[16,8,16384]{2,1,0:T(8,128)} %get-tuple-element.175), kind=kLoop, calls=%fused_computation.149 | loop fusion | flops 2097152 | bytes 16777216 | tf_op jit(solution)/shard_map/mul | solution.py:174
  342.0 72.2 %reduce-scatter.2.cloned.1.call-done = f32[128,2048]{1,0:T(8,128)} async-done(((f32[128,16384]{1,0:T(8,128)}), f32[128,2048]{1,0:T(8,128)}) %reduce-scatter.2.cloned.1.call-update) | async-done | bytes 1048592 | tf_op jit(solution)/shard_map/reduce_scatter | solution.py:175
  414.1 2.5 copy.73
  416.7 4.6 all-to-all-start
  423.4 23.4 %all-to-all-done = f32[128,4,512]{0,2,1:T(8,128)S(1)} async-done(((f32[128,4,512]{0,2,1:T(8,128)}), f32[128,4,512]{0,2,1:T(8,128)S(1)}, u32[]{:S(2)}, u32[]{:S(2)}) %all-to-all-start) | async-done | bytes 1048608 | tf_op jit(solution)/shard_map/all_to_all | solution.py:176
  446.8 1.8 multiply_reduce_fusion.1
  450.4 1.3 copy.75
  452.0 1.7 fusion.113
  453.7 2.2 fusion.118
  455.9 38.1 %all-reduce.4 = (f32[64,33]{0,1:T(8,128)}, f32[64]{0:T(128)}, f32[64,64]{1,0:T(8,128)}, f32[2,64]{1,0:T(2,128)}, f32[512]{0:T(512)}) all-reduce(f32[64,33]{0,1:T(8,128)S(1)} %fusion.129, f32[64]{0:T(128)S(1)} %get-tuple-element.198, f32[64,64]{1,0:T(8,128)S(1)} %fusion.131, ...), channel_id=1, replica_groups=mesh['dp'=8,'chan'=4] {'dp','chan'}, use_global_device_ids=true, to_apply=%region_3.4 | all-reduce | flops 6912 | bytes 55296 | tf_op jit(solution)/shard_map/psum | solution.py:183
  494.0 84.7 %all-reduce.7.cloned.1.call-done = f32[512,64]{0,1:T(8,128)} async-done(((f32[512,64]{0,1:T(8,128)}), f32[512,64]{0,1:T(8,128)}) %all-reduce.7.cloned.1.call-update) | async-done | bytes 131088 | tf_op jit(solution)/shard_map/psum | solution.py:183
  578.6 1.6 copy.124
  (613 shorter events, 303.4 us)
Async XLA Ops:
  7.2 439.7 %copy-start = (f32[512,64]{0,1:T(8,128)S(1)}, f32[512,64]{0,1:T(8,128)}, u32[]{:S(2)}) copy-start(f32[512,64]{0,1:T(8,128)} %param.16) | copy-start | bytes 393220
  7.2 407.0 %reduce-scatter.2.cloned.1.call-start = ((), (), s32[]{:S(2)}) async-start(), calls=%async_computation.2 | async-start | bytes 9437184 | tf_op jit(solution)/shard_map/reduce_scatter | solution.py:175
  339.7 0.7 copy-start.3
  339.7 82.6 %copy-start.4 = (f32[2,64]{1,0:T(2,128)S(1)}, f32[2,64]{1,0:T(2,128)}, u32[]{:S(2)}) copy-start(f32[2,64]{1,0:T(2,128)} %param.15) | copy-start | bytes 1540
  339.7 82.6 %copy-start.2 = (f32[64,33]{0,1:T(8,128)S(1)}, f32[64,33]{0,1:T(8,128)}, u32[]{:S(2)}) copy-start(f32[64,33]{0,1:T(8,128)} %param.12) | copy-start | bytes 25348
  339.7 82.6 %copy-start.5 = (f32[64]{0:T(128)S(1)}, f32[64]{0:T(128)}, u32[]{:S(2)}) copy-start(f32[64]{0:T(128)} %param.13) | copy-start | bytes 772
  339.7 82.9 %copy-start.1 = (f32[64,64]{1,0:T(8,128)S(1)}, f32[64,64]{1,0:T(8,128)}, u32[]{:S(2)}) copy-start(f32[64,64]{1,0:T(8,128)} %param.14) | copy-start | bytes 49156
  416.7 30.2 %all-to-all-start = ((f32[128,4,512]{0,2,1:T(8,128)}), f32[128,4,512]{0,2,1:T(8,128)S(1)}, u32[]{:S(2)}, u32[]{:S(2)}) async-start(f32[128,4,512]{0,2,1:T(8,128)} %bitcast.39), calls=%async_computation.1 | async-start | bytes 2097152 | tf_op jit(solution)/shard_map/all_to_all | solution.py:176
  421.3 157.4 %all-reduce.7.cloned.1.call-start = ((), (), s32[]{:S(2)}) async-start(), calls=%async_computation.3 | async-start | bytes 262144 | tf_op jit(solution)/shard_map/psum | solution.py:183
Sparse Core Ops, SparseCore 0:
  339.9 74.2 reduce-scatter.1
  456.0 122.5 all-reduce.6
where the time goes:
time: 588 us; the launch traced here: 587 us
  matrix products  207 us (35%)
  waiting for transfers between devices  180 us (31%)
  local copies, waits for them, and re-layouts  88.7 us (15%)
  other arithmetic  40.2 us (7%)
  blocking collectives  38.1 us (6%)
  between operations  14.2 us (2%)
  loops' own time  14 us (2%)
    dot_general x96, matrix products, apply(): jnp.einsum(spec, values, matrix, precision=exact, preferred_element_type=...  99.2 us
    dot_general x96, matrix products, apply(): jnp.einsum(spec, matrix, values, precision=exact, preferred_element_type=...  99.1 us
    psum x1, waiting for transfers between devices, local(): lax.psum((local_grads[0], local_grads[1], local_grads[2], local_grads[3],...  84.7 us
    reduce_scatter x1, waiting for transfers between devices, local(): lax.psum_scatter(correlation, 'dp', scatter_dimension=1, tiled=True)  72.2 us
    psum x1, blocking collectives, local(): lax.psum((local_grads[0], local_grads[1], local_grads[2], local_grads[3],...  38.1 us
    all_to_all x1, waiting for transfers between devices, local(): lax.all_to_all(shared, 'chan', split_axis=1, concat_axis=0, tiled=True)  23.4 us
    another operation x32, local copies, waits for them, and re-layouts  22.9 us
    dynamic_update_slice x16, local copies, waits for them, and re-layouts, local(): correlation = lax.map(lags_of, indices).reshape(chan_local, total) * scale  18 us
  transfers between devices with their start and end apart: 3, of which 3 were waited for; matrix products, arithmetic and copies ran while one was open for 1% of the time, Pallas kernels for 0%

commit v1 on v0

v1 whole, which is shorter than its diff:
```python
import functools
import math

import jax
import jax.numpy as jnp
import numpy as np
from jax import lax
from jax.experimental import pallas as pl
from jax.experimental.pallas import tpu as pltpu
from jax.sharding import PartitionSpec as P

LANES = 128
F32 = jnp.float32
BF16 = jnp.bfloat16


def lag_features(lag, length, bands):
    total = 2 * length
    scaled = lag.astype(jnp.float32) / length
    sines = []
    cosines = []
    for band in range(bands):
        factor = max(1, int(0.45 * total * 10000.0 ** (-band / bands)))
        phase = (lag * factor % total).astype(jnp.float32) * (2.0 * math.pi / total)
        sines.append(jnp.sin(phase))
        cosines.append(jnp.cos(phase))
    return jnp.stack([scaled] + sines + cosines)


def filter_loss(params, lag, cotangent, length):
    embed_weight, embed_bias, hidden_weight, frequency, output_weight, decay_rate = params
    bands = (embed_weight.shape[1] - 1) // 2
    exact = lax.Precision.HIGHEST
    table = lag_features(lag, length, bands)
    first = jnp.sin(
        frequency[0][:, None]
        * (
            jnp.dot(embed_weight, table, precision=exact, preferred_element_type=jnp.float32)
            + embed_bias[:, None]
        )
    )
    second = jnp.sin(
        frequency[1][:, None]
        * jnp.dot(hidden_weight, first, precision=exact, preferred_element_type=jnp.float32)
    )
    shaped = jnp.dot(output_weight, second, precision=exact, preferred_element_type=jnp.float32)
    window = jnp.exp(-decay_rate[:, None] * jnp.abs(lag).astype(jnp.float32)[None, :] / length)
    return jnp.sum(shaped * window * cotangent) / math.sqrt(2 * length)


def split(values):
    high = values.astype(BF16)
    return high, (values - high.astype(F32)).astype(BF16)


def split_table(values):
    high = values.astype(BF16)
    return high, (values - high.astype(np.float64)).astype(BF16)


def tables(rows, scale):
    total = 2 * rows * LANES
    odd = 2 * np.arange(rows) + 1
    angle = np.pi * (odd[:, None] * np.arange(2 * rows)[None, :] % (4 * rows)) / (2 * rows)
    first = np.concatenate([np.cos(angle[:, :rows]), -np.sin(angle[:, :rows])], axis=0)
    first = np.concatenate(split_table(first), axis=1)
    turn = np.pi * (odd[:, None] * np.arange(LANES)[None, :]) / total
    twist = np.stack([np.cos(turn), -np.sin(turn)]).astype(np.float32)
    untwist = (np.stack([np.cos(turn), np.sin(turn)]) * scale).astype(np.float32)
    fine = 2 * np.pi * (np.arange(LANES)[:, None] * np.arange(LANES)[None, :] % LANES) / LANES
    cosine, sine = np.cos(fine), np.sin(fine)
    second = np.block([[cosine, -sine], [sine, cosine]])
    sign = np.where(np.arange(2 * rows) < rows, 1.0, -1.0)[:, None]
    last = np.concatenate([np.cos(angle).T, -np.sin(angle).T], axis=1) * sign
    last_high, last_low = split_table(last)
    last = np.concatenate([last_high, last_low, last_high], axis=1)
    second_high, second_low = split_table(second)
    back_high, back_low = split_table(second.T)
    return first, twist, untwist, second_high, second_low, back_high, back_low, last


def dot(a, b):
    return jnp.dot(a, b, preferred_element_type=F32)


def correlate_kernel(
    x_ref, g_ref, first_ref, twist_ref, untwist_ref, sh_ref, sl_ref, bh_ref, bl_ref, last_ref,
    out_ref, high_ref, low_ref, spec_ref,
):
    seqs, _, rows, _ = x_ref.shape
    cosine = jnp.concatenate([twist_ref[0]] * 2, axis=1)
    sine = jnp.concatenate([twist_ref[1]] * 2, axis=1)
    first = first_ref[...]
    for s in range(seqs):
        pair = jnp.concatenate([x_ref[s, 0], g_ref[s, 0]], axis=1)
        both = dot(first, jnp.concatenate([pair, pair], axis=0))
        real, imag = both[:rows], both[rows:]
        real, imag = real * cosine - imag * sine, real * sine + imag * cosine
        for at, part in ((0, slice(0, LANES)), (1, slice(LANES, 2 * LANES))):
            line = pl.ds((at * seqs + s) * rows, rows)
            row = jnp.concatenate([real[:, part], imag[:, part]], axis=1)
            high_ref[line, :], low_ref[line, :] = split(row)
    spec_ref[...] = (
        dot(high_ref[...], sh_ref[...])
        + dot(low_ref[...], sh_ref[...])
        + dot(high_ref[...], sl_ref[...])
    )
    real = jnp.zeros((rows, LANES), F32)
    imag = jnp.zeros((rows, LANES), F32)
    for s in range(seqs):
        a = spec_ref[pl.ds(s * rows, rows), :]
        b = spec_ref[pl.ds((seqs + s) * rows, rows), :]
        a_real, a_imag, b_real, b_imag = a[:, :LANES], a[:, LANES:], b[:, :LANES], b[:, LANES:]
        real = real + (a_real * b_real + a_imag * b_imag)
        imag = imag + (a_real * b_imag - a_imag * b_real)
    high, low = split(jnp.concatenate([real, imag], axis=1))
    back = dot(high, bh_ref[...]) + dot(low, bh_ref[...]) + dot(high, bl_ref[...])
    real, imag = back[:, :LANES], back[:, LANES:]
    cosine, sine = untwist_ref[0], untwist_ref[1]
    turned = jnp.concatenate([real * cosine - imag * sine, real * sine + imag * cosine], axis=0)
    high, low = split(turned)
    out_ref[0] = dot(last_ref[...], jnp.concatenate([high, high, low], axis=0))


def correlate(x, g, scale):
    seqs, channels, rows, lanes = x.shape
    total = 2 * rows * lanes
    consts = [jnp.asarray(t) for t in tables(rows, 2.0 * scale / total)]
    block = pl.BlockSpec((seqs, 1, rows, lanes), lambda c: (0, c, 0, 0))
    whole = [
        pl.BlockSpec(t.shape, functools.partial(lambda n, c: (0,) * n, t.ndim)) for t in consts
    ]
    return pl.pallas_call(
        correlate_kernel,
        grid=(channels,),
        in_specs=[block, block] + whole,
        out_specs=pl.BlockSpec((1, 2 * rows, lanes), lambda c: (c, 0, 0)),
        out_shape=jax.ShapeDtypeStruct((channels, 2 * rows, lanes), F32),
        scratch_shapes=[
            pltpu.VMEM((2 * seqs * rows, 2 * lanes), BF16),
            pltpu.VMEM((2 * seqs * rows, 2 * lanes), BF16),
            pltpu.VMEM((2 * seqs * rows, 2 * lanes), F32),
        ],
        name="correlate",
    )(x, g, *consts)


def sum_everywhere(parts, axes, count):
    flat = jnp.concatenate([p.reshape(-1) for p in parts])
    unit = count * 8 * LANES
    padded = -(-flat.shape[0] // unit) * unit
    flat = jnp.pad(flat, (0, padded - flat.shape[0])).reshape(count, -1, LANES)
    pieces = lax.all_to_all(flat, axes, 0, 0, tiled=True)
    mine = jnp.sum(pieces, axis=0)
    sums = lax.all_to_all(
        jnp.broadcast_to(mine[None], flat.shape), axes, 0, 0, tiled=True
    ).reshape(-1)
    out, at = [], 0
    for p in parts:
        out.append(sums[at : at + p.size].reshape(p.shape))
        at += p.size
    return out


def local(
    signal,
    signal_grad,
    embed_weight,
    embed_bias,
    hidden_weight,
    frequency,
    output_weight,
    decay_rate,
):
    seq_local, chan_local, length = signal.shape
    total = 2 * length
    dp, chan = lax.axis_size("dp"), lax.axis_size("chan")
    rows = length // LANES
    own = chan_local // dp
    axes = ("dp", "chan")
    scale = 1.0 / math.sqrt(seq_local * dp * length)

    def gather(values):
        values = values.reshape(seq_local, dp, own, rows, LANES)
        values = jnp.swapaxes(values, 0, 1)
        values = lax.all_to_all(values, "dp", 0, 0, tiled=True)
        return values.reshape(dp * seq_local, own, rows, LANES)

    lags = correlate(gather(signal), gather(signal_grad), scale)
    count = dp * chan
    lag_count = total // count
    lags = jnp.swapaxes(lags.reshape(own, count, lag_count), 0, 1)
    shared = lax.all_to_all(lags, axes, 0, 0, tiled=True)
    filter_grad = jnp.swapaxes(shared.reshape(dp, chan, own, lag_count), 0, 1).reshape(
        chan * chan_local, lag_count
    )
    device_rank = lax.axis_index("dp") * chan + lax.axis_index("chan")
    position = device_rank * lag_count + jnp.arange(lag_count, dtype=jnp.int32)
    lag = jnp.where(position < length, position, position - total)
    params = (embed_weight, embed_bias, hidden_weight, frequency, output_weight, decay_rate)
    local_grads = jax.grad(filter_loss)(params, lag, filter_grad, length)
    summed = sum_everywhere(local_grads, axes, count)
    return (filter_grad, *summed)


def solution(mesh):
    placed = (P("dp", "chan", None), P("dp", "chan", None), P(), P(), P(), P(), P(), P())
    return jax.shard_map(
        local,
        mesh=mesh,
        in_specs=placed,
        out_specs=(P(None, ("dp", "chan")), P(), P(), P(), P(), P(), P()),
        check_vma=False,
    )
```

time: 588 us -> 163 us (0.28)
  matrix products: 207 us -> 8.82 us
  waiting for transfers between devices: 180 us -> 70.7 us
  local copies, waits for them, and re-layouts: 88.7 us -> 16.7 us
  other arithmetic: 40.2 us -> 2.41 us
  Pallas kernels: 0 us -> 21.9 us
  loops' own time: 14 us -> 0 us
  between operations: 14.2 us -> 0.96 us
  blocking collectives: 38.1 us -> 27.3 us
  starting transfers between devices: 4.64 us -> 13.7 us
    dot_general x192 -> x0, matrix products: 198 us -> none  [the longest x96 99.2 us: apply(): jnp.einsum(spec, values, matrix, precision=exact, preferred_element_type=...]
    psum x1 -> x0, waiting for transfers between devices: 84.7 us -> none  [local(): lax.psum((local_grads[0], local_grads[1], local_grads[2], local_grads[3],...]
    reduce_scatter x1 -> x0, waiting for transfers between devices: 72.2 us -> none  [local(): lax.psum_scatter(correlation, 'dp', scatter_dimension=1, tiled=True)]
    all_to_all x1 -> x3, waiting for transfers between devices: 23.4 us -> 70.7 us  [the longest x2 48.7 us: gather(): values = lax.all_to_all(values, 'dp', 0, 0, tiled=True)]
    psum x1 -> x0, blocking collectives: 38.1 us -> none  [local(): lax.psum((local_grads[0], local_grads[1], local_grads[2], local_grads[3],...]
    all_to_all x0 -> x2, blocking collectives: none -> 27.3 us  [the longest x1 14.6 us: sum_everywhere(): pieces = lax.all_to_all(flat, axes, 0, 0, tiled=True)]
    dynamic_slice x32 -> x0, local copies, waits for them, and re-layouts: 25.2 us -> none  [the longest x16 15.8 us: spectrum_of(): grads = lax.dynamic_slice_in_dim(signal_grad, start, block, 1)]
    another operation x32 -> x0, local copies, waits for them, and re-layouts: 22.9 us -> none
  transfers between devices with their start and end apart: 3 -> 3, of which waited for: 3 -> 3; matrix products, arithmetic and copies ran while one was open for 1% -> 4% of each run, Pallas kernels for 0% -> 0%
where the time goes in v1:
time: 163 us; the launch traced here: 162 us
  waiting for transfers between devices  70.7 us (43%)
  blocking collectives  27.3 us (17%)
  Pallas kernels  21.9 us (13%)
  local copies, waits for them, and re-layouts  16.7 us (10%)
  starting transfers between devices  13.7 us (8%)
  matrix products  8.82 us (5%)
  other arithmetic  2.41 us (1%)
    all_to_all x2, waiting for transfers between devices, gather(): values = lax.all_to_all(values, 'dp', 0, 0, tiled=True)  48.7 us
    all_to_all x1, waiting for transfers between devices, local(): shared = lax.all_to_all(lags, axes, 0, 0, tiled=True)  22 us
    pallas_call x1, Pallas kernels, correlate(): pl.pallas_call(correlate_kernel, grid=(channels,), in_specs=[block, block...  21.9 us
    all_to_all x1, blocking collectives, sum_everywhere(): pieces = lax.all_to_all(flat, axes, 0, 0, tiled=True)  14.6 us
    all_to_all x1, blocking collectives, sum_everywhere(): lax.all_to_all(jnp.broadcast_to(mine[None], flat.shape), axes, 0, 0, tile...  12.7 us
    unnamed x20, local copies, waits for them, and re-layouts  9.96 us
    all_to_all x2, starting transfers between devices, gather(): values = lax.all_to_all(values, 'dp', 0, 0, tiled=True)  9.55 us
    dot_general x3, matrix products, filter_loss(): jnp.dot(output_weight, second, precision=exact, preferred_element_type=jn...  5.9 us
  transfers between devices with their start and end apart: 3, of which 3 were waited for; matrix products, arithmetic and copies ran while one was open for 4% of the time, Pallas kernels for 0%

profile of v1, /device:TPU:0, one launch (start us, length us, event | category | flops | bytes accessed | tf_op | source)
XLA Modules:
  0.0 162.4 jit_solution(6260209341333430659)
XLA Ops:
  0.6 3.6 %copy.55 = bf16[16,8,64,128]{3,2,1,0:T(8,128)(2,1)} copy(bf16[16,8,64,128]{3,1,2,0:T(8,128)(2,1)} %bitcast.60) | data formatting | bytes 4194304
  4.2 5.2 %all-to-all-start = ((bf16[8,1,16,64,128]{4,3,2,1,0:T(8,128)(2,1)}), bf16[8,1,16,64,128]{4,3,2,1,0:T(8,128)(2,1)S(1)}, u32[]{:S(2)}, u32[]{:S(2)}) async-start(bf16[8,1,16,64,128]{4,3,2,1,0:T(8,128)(2,1)} %bitcast.56), calls=%async_computation | async-start | bytes 4194304 | tf_op jit(solution)/shard_map/all_to_all | solution.py:186
  9.4 3.5 %copy.56 = bf16[16,8,64,128]{3,2,1,0:T(8,128)(2,1)} copy(bf16[16,8,64,128]{3,1,2,0:T(8,128)(2,1)} %bitcast.61) | data formatting | bytes 4194304
  12.9 23.1 %all-to-all-done = bf16[8,1,16,64,128]{4,3,2,1,0:T(8,128)(2,1)S(1)} async-done(((bf16[8,1,16,64,128]{4,3,2,1,0:T(8,128)(2,1)}), bf16[8,1,16,64,128]{4,3,2,1,0:T(8,128)(2,1)S(1)}, u32[]{:S(2)}, u32[]{:S(2)}) %all-to-all-start) | async-done | bytes 2097184 | tf_op jit(solution)/shard_map/all_to_all | solution.py:186
  36.0 1.4 copy-done.1
  37.4 4.4 %all-to-all-start.1 = ((bf16[8,1,16,64,128]{4,3,2,1,0:T(8,128)(2,1)}), bf16[8,1,16,64,128]{4,3,2,1,0:T(8,128)(2,1)}, u32[]{:S(2)}, u32[]{:S(2)}) async-start(bf16[8,1,16,64,128]{4,3,2,1,0:T(8,128)(2,1)} %bitcast.55), calls=%async_computation.1 | async-start | bytes 4194304 | tf_op jit(solution)/shard_map/all_to_all | solution.py:186
  42.8 25.6 %all-to-all-done.1 = bf16[8,1,16,64,128]{4,3,2,1,0:T(8,128)(2,1)} async-done(((bf16[8,1,16,64,128]{4,3,2,1,0:T(8,128)(2,1)}), bf16[8,1,16,64,128]{4,3,2,1,0:T(8,128)(2,1)}, u32[]{:S(2)}, u32[]{:S(2)}) %all-to-all-start.1) | async-done | bytes 2097184 | tf_op jit(solution)/shard_map/all_to_all | solution.py:186
  68.4 21.9 %correlate.1 = f32[16,128,128]{2,1,0:T(8,128)} custom-call(bf16[8,16,64,128]{3,2,1,0:T(8,128)(2,1)} %bitcast.54, bf16[8,16,64,128]{3,2,1,0:T(8,128)(2,1)} %bitcast.1.g_ref, bf16[128,128]{1,0:T(8,128)(2,1)} %constant.167.clone.first_ref, f32[2,64,128]{2,1,0:T(8,128)} %constant.168.clone.twist_ref, f32[2,64,128]{2,1,0:T(8,128)} %constant.169.clone.untwist_ref, ...), custom_call_target="tpu_custom_call" | custom-call | tf_op jit(solution)/shard_map/correlate/pallas_call | solution.py:133
  90.2 1.4 reshape.905
  91.7 1.6 copy.58
  93.3 4.2 %all-to-all-start.2 = ((f32[32,16,512]{2,1,0:T(8,128)}), f32[32,16,512]{2,1,0:T(8,128)S(1)}, u32[]{:S(2)}, u32[]{:S(2)}) async-start(f32[32,16,512]{2,1,0:T(8,128)} %bitcast.53), calls=%async_computation.2 | async-start | bytes 2097152 | tf_op jit(solution)/shard_map/all_to_all | solution.py:193
  99.5 0.8 convolution_bitcast_fusion.2
  100.2 22.0 %all-to-all-done.2 = f32[32,16,512]{2,1,0:T(8,128)S(1)} async-done(((f32[32,16,512]{2,1,0:T(8,128)}), f32[32,16,512]{2,1,0:T(8,128)S(1)}, u32[]{:S(2)}, u32[]{:S(2)}) %all-to-all-start.2) | async-done | bytes 1048608 | tf_op jit(solution)/shard_map/all_to_all | solution.py:193
  122.7 1.8 %multiply_reduce_fusion.1 = (f32[64]{0:T(128)S(1)}, f32[64,512]{1,0:T(8,128)S(1)}) fusion(f32[64,512]{1,0:T(8,128)S(1)} %convolution_bitcast_fusion.2, f32[64]{0:T(128)S(1)} %get-tuple-element.44, f32[512,64]{0,1:T(8,128)S(1)} %copy-done, f32[512,512]{0,1:T(8,128)S(1)} %copy.48, f32[512]{0:T(512)S(1)} %fusion.32, f32[512]{0:T(512)S(1)} %neg.10), kind=kOutput, calls=%fused_computation.25 | convolution fusion | flops 202506176 | bytes 1446400 | tf_op jit(solution)/shard_map/transpose(jvp())/dot_general | solution.py:46
  124.5 0.8 multiply_reduce_fusion
  125.3 0.8 fusion.21
  126.1 2.3 %fusion.8 = f32[512,64]{1,0:T(8,128)S(1)} fusion(f32[512,512]{0,1:T(8,128)S(1)} %copy.48, f32[512]{0:T(512)S(1)} %fusion.32, f32[512]{0:T(512)S(1)} %neg.10, f32[64,512]{1,0:T(8,128)S(1)} %convolution_bitcast_fusion.2, f32[64]{0:T(128)S(1)} %get-tuple-element.44), kind=kOutput, calls=%fused_computation.15 | convolution fusion | flops 202407936 | bytes 1315072 | tf_op jit(solution)/shard_map/transpose(jvp())/dot_general | solution.py:46
  129.1 1.7 %fusion.3 = f32[512]{0:T(512)S(1)} fusion(f32[512,64]{0,1:T(8,128)S(1)} %copy-done, f32[512,512]{0,1:T(8,128)S(1)} %copy.48, f32[512]{0:T(512)S(1)} %broadcast_multiply_fusion, f32[512]{0:T(512)S(1)} %fusion.32, f32[512]{0:T(512)S(1)} %neg.10, f32[64,512]{1,0:T(8,128)S(1)} %convolution_bitcast_fusion.2, f32[64]{0:T(128)S(1)} %get-tuple-element.44), kind=kOutput, calls=%fused_computation.4 | convolution fusion | flops 203193856 | bytes 1319168 | tf_op jit(solution)/shard_map/jvp()/dot_general | solution.py:46
  131.0 14.6 %all_to_all.25 = f32[32,16,128]{2,1,0:T(8,128)S(1)} all-to-all(f32[32,16,128]{2,1,0:T(8,128)S(1)} %bitcast.65), channel_id=1, replica_groups=mesh['dp'=8,'chan'=4] {'dp','chan'}, dimensions={0} | all-to-all | bytes 524288 | tf_op jit(solution)/shard_map/all_to_all | solution.py:153
  145.6 12.7 %all_to_all.26 = f32[32,16,128]{2,1,0:T(8,128)S(1)} all-to-all(f32[32,16,128]{2,1,0:T(8,128)S(1)} %broadcast_in_dim.25), channel_id=1, replica_groups=mesh['dp'=8,'chan'=4] {'dp','chan'}, dimensions={0} | all-to-all | bytes 524288 | tf_op jit(solution)/shard_map/all_to_all | solution.py:155
  158.3 0.6 slice.39
  159.1 0.6 slice.40
  161.0 0.7 copy.51
  161.7 0.8 copy.52
  (57 shorter events, 5.6 us)
Async XLA Ops:
  0.6 122.0 %copy-start = (f32[512,64]{0,1:T(8,128)S(1)}, f32[512,64]{0,1:T(8,128)}, u32[]{:S(2)}) copy-start(f32[512,64]{0,1:T(8,128)} %param.22) | copy-start | bytes 393220
  4.2 31.8 %all-to-all-start = ((bf16[8,1,16,64,128]{4,3,2,1,0:T(8,128)(2,1)}), bf16[8,1,16,64,128]{4,3,2,1,0:T(8,128)(2,1)S(1)}, u32[]{:S(2)}, u32[]{:S(2)}) async-start(bf16[8,1,16,64,128]{4,3,2,1,0:T(8,128)(2,1)} %bitcast.56), calls=%async_computation | async-start | bytes 4194304 | tf_op jit(solution)/shard_map/all_to_all | solution.py:186
  36.0 1.4 copy-start.1
  36.0 5.7 %copy-start.5 = (f32[512]{0:T(512)S(1)}, f32[512]{0:T(512)}, u32[]{:S(2)}) copy-start(f32[512]{0:T(512)} %param.23) | copy-start | bytes 6148
  37.4 31.0 %all-to-all-start.1 = ((bf16[8,1,16,64,128]{4,3,2,1,0:T(8,128)(2,1)}), bf16[8,1,16,64,128]{4,3,2,1,0:T(8,128)(2,1)}, u32[]{:S(2)}, u32[]{:S(2)}) async-start(bf16[8,1,16,64,128]{4,3,2,1,0:T(8,128)(2,1)} %bitcast.55), calls=%async_computation.1 | async-start | bytes 4194304 | tf_op jit(solution)/shard_map/all_to_all | solution.py:186
  91.7 7.4 %copy-start.6 = (f32[2,64]{1,0:T(2,128)S(1)}, f32[2,64]{1,0:T(2,128)}, u32[]{:S(2)}) copy-start(f32[2,64]{1,0:T(2,128)} %param.21) | copy-start | bytes 1540
  91.7 7.4 %copy-start.4 = (f32[64,33]{0,1:T(8,128)S(1)}, f32[64,33]{0,1:T(8,128)}, u32[]{:S(2)}) copy-start(f32[64,33]{0,1:T(8,128)} %param.18) | copy-start | bytes 25348
  91.7 7.4 %copy-start.7 = (f32[64]{0:T(128)S(1)}, f32[64]{0:T(128)}, u32[]{:S(2)}) copy-start(f32[64]{0:T(128)} %param.19) | copy-start | bytes 772
  91.7 7.8 %copy-start.3 = (f32[64,64]{1,0:T(8,128)S(1)}, f32[64,64]{1,0:T(8,128)}, u32[]{:S(2)}) copy-start(f32[64,64]{1,0:T(8,128)} %param.20) | copy-start | bytes 49156
  93.3 28.9 %all-to-all-start.2 = ((f32[32,16,512]{2,1,0:T(8,128)}), f32[32,16,512]{2,1,0:T(8,128)S(1)}, u32[]{:S(2)}, u32[]{:S(2)}) async-start(f32[32,16,512]{2,1,0:T(8,128)} %bitcast.53), calls=%async_computation.2 | async-start | bytes 2097152 | tf_op jit(solution)/shard_map/all_to_all | solution.py:193
  122.3 2.2 %copy-start.2 = (f32[4,8,16,512]{3,2,1,0:T(8,128)}, f32[4,8,16,512]{3,2,1,0:T(8,128)S(1)}, u32[]{:S(2)}) copy-start(f32[4,8,16,512]{3,2,1,0:T(8,128)S(1)} %copy.47) | copy-start | bytes 3145732

commit v2 on v1

v2 whole, which is shorter than its diff:
```python
import functools
import math

import jax
import jax.numpy as jnp
import numpy as np
from jax import lax
from jax.experimental import pallas as pl
from jax.experimental.pallas import tpu as pltpu
from jax.sharding import PartitionSpec as P


LANES = 128
F32 = jnp.float32
BF16 = jnp.bfloat16


def split(values):
    high = values.astype(BF16)
    return high, (values - high.astype(F32)).astype(BF16)


def split_table(values):
    high = values.astype(BF16)
    return high, (values - high.astype(np.float64)).astype(BF16)


def tables(rows, scale):
    total = 2 * rows * LANES
    odd = 2 * np.arange(rows) + 1
    angle = np.pi * (odd[:, None] * np.arange(2 * rows)[None, :] % (4 * rows)) / (2 * rows)
    first = np.concatenate([np.cos(angle[:, :rows]), -np.sin(angle[:, :rows])], axis=0)
    first = np.concatenate(split_table(first), axis=1)
    turn = np.pi * (odd[:, None] * np.arange(LANES)[None, :]) / total
    twist = np.stack([np.cos(turn), -np.sin(turn)]).astype(np.float32)
    untwist = (np.stack([np.cos(turn), np.sin(turn)]) * scale).astype(np.float32)
    fine = 2 * np.pi * (np.arange(LANES)[:, None] * np.arange(LANES)[None, :] % LANES) / LANES
    cosine, sine = np.cos(fine), np.sin(fine)
    second = np.block([[cosine, -sine], [sine, cosine]])
    sign = np.where(np.arange(2 * rows) < rows, 1.0, -1.0)[:, None]
    last = np.concatenate([np.cos(angle).T, -np.sin(angle).T], axis=1) * sign
    last_high, last_low = split_table(last)
    last = np.concatenate([last_high, last_low, last_high], axis=1)
    second, back = (
        np.concatenate([high, high, low], axis=0)
        for high, low in (split_table(second), split_table(second.T))
    )
    return first, twist, untwist, second, back, last


def dot(a, b):
    return jnp.dot(a, b, preferred_element_type=F32)


def stacked(values, axis):
    high, low = split(values)
    return jnp.concatenate([high, low], axis=axis)


def narrow(values, axis):
    high = lax.reduce_precision(values, 8, 7)
    low = (values - high).astype(BF16)
    high = high.astype(BF16)
    return jnp.concatenate([high, low, high], axis=axis)


def wide(values, axis):
    high, low = split(values)
    return jnp.concatenate([high, high, low], axis=axis)


def dot_lanes(a, b):
    return lax.dot_general(a, b, (((1,), (1,)), ((), ())), preferred_element_type=F32)


def sine_cosine(angle):
    turns = jnp.round(angle * (2.0 / math.pi))
    rest = angle - turns * 1.5703125
    rest = rest - turns * 4.837512969970703125e-4
    rest = rest - turns * 7.54978995489188216e-8
    square = rest * rest
    odd = ((-1.9515295891e-4 * square + 8.3321608736e-3) * square - 1.6666654611e-1) * square
    odd = odd * rest + rest
    even = (2.443315711809948e-5 * square - 1.388731625493765e-3) * square + 4.166664568298827e-2
    even = even * square * square - 0.5 * square + 1.0
    quarter = turns.astype(jnp.int32)
    swap = (quarter & 1) != 0
    sine = jnp.where(swap, even, odd)
    cosine = jnp.where(swap, odd, even)
    sine = jnp.where((quarter & 2) != 0, -sine, sine)
    cosine = jnp.where(((quarter + 1) & 2) != 0, -cosine, cosine)
    return sine, cosine


def pick(x, g, block, own, start, count):
    first = block * own + start
    return jnp.stack([lax.dynamic_slice_in_dim(v, first, count, 1) for v in (x, g)])


def correlate_kernel(*refs, pieces):
    piece_refs = refs[:pieces]
    (
        first_ref, twist_ref, untwist_ref, second_ref, back_ref, last_ref,
        out_ref, turn_ref, high_ref, low_ref, spec_ref, lag_ref,
    ) = refs[pieces:]
    _, seqs_each, channels, length = piece_refs[0].shape
    rows = length // LANES
    seqs = pieces * seqs_each
    c = pl.program_id(0)

    @pl.when(c == 0)
    def _():
        for s in range(seqs):
            for at in range(2):
                for row in range(rows):
                    turn_ref[at * seqs + s, pl.ds(row * channels, channels), :] = piece_refs[
                        s // seqs_each
                    ][at, s % seqs_each, :, pl.ds(row * LANES, LANES)].astype(F32)

    def samples(at, s):
        return turn_ref[at * seqs + s, pl.ds(c, rows, stride=channels), :].astype(BF16)

    cosine = jnp.concatenate([twist_ref[0]] * 2, axis=1)
    sine = jnp.concatenate([twist_ref[1]] * 2, axis=1)
    first = first_ref[...]
    for s in range(seqs):
        pair = jnp.concatenate([samples(0, s), samples(1, s)], axis=1)
        both = dot(first, jnp.concatenate([pair, pair], axis=0))
        real, imag = both[:rows], both[rows:]
        real, imag = real * cosine - imag * sine, real * sine + imag * cosine
        for at, part in ((0, slice(0, LANES)), (1, slice(LANES, 2 * LANES))):
            line = pl.ds((at * seqs + s) * rows, rows)
            row = jnp.concatenate([real[:, part], imag[:, part]], axis=1)
            high_ref[line, :], low_ref[line, :] = split(row)
    spec_ref[...] = dot(
        jnp.concatenate([high_ref[...], low_ref[...], high_ref[...]], axis=1), second_ref[...]
    )
    real = jnp.zeros((rows, LANES), F32)
    imag = jnp.zeros((rows, LANES), F32)
    for s in range(seqs):
        a = spec_ref[pl.ds(s * rows, rows), :]
        b = spec_ref[pl.ds((seqs + s) * rows, rows), :]
        a_real, a_imag, b_real, b_imag = a[:, :LANES], a[:, LANES:], b[:, :LANES], b[:, LANES:]
        real = real + (a_real * b_real + a_imag * b_imag)
        imag = imag + (a_real * b_imag - a_imag * b_real)
    high, low = split(jnp.concatenate([real, imag], axis=1))
    back = dot(jnp.concatenate([high, low, high], axis=1), back_ref[...])
    real, imag = back[:, :LANES], back[:, LANES:]
    cosine, sine = untwist_ref[0], untwist_ref[1]
    turned = jnp.concatenate([real * cosine - imag * sine, real * sine + imag * cosine], axis=0)
    high, low = split(turned)
    lag_ref[pl.ds(pl.multiple_of(c * 2 * rows, 2 * rows), 2 * rows), :] = dot(
        last_ref[...], jnp.concatenate([high, high, low], axis=0)
    )

    @pl.when(c == pl.num_programs(0) - 1)
    def _():
        owners, channels, lag_count = out_ref.shape
        each = lag_count // LANES
        for owner in range(owners):
            for k in range(each):
                out_ref[owner, :, pl.ds(k * LANES, LANES)] = lag_ref[
                    pl.ds(owner * each + k, channels, stride=2 * rows), :
                ]


def correlate(pieces, scale, owners):
    _, seqs_each, channels, length = pieces[0].shape
    lanes, rows = LANES, length // LANES
    seqs = seqs_each * len(pieces)
    total = 2 * rows * lanes
    consts = [jnp.asarray(t) for t in tables(rows, 2.0 * scale / total)]
    block = pl.BlockSpec(pieces[0].shape, lambda c: (0, 0, 0, 0))
    whole = [
        pl.BlockSpec(t.shape, functools.partial(lambda n, c: (0,) * n, t.ndim)) for t in consts
    ]
    shape = (owners, channels, total // owners)
    return pl.pallas_call(
        functools.partial(correlate_kernel, pieces=len(pieces)),
        grid=(channels,),
        in_specs=[block] * len(pieces) + whole,
        out_specs=pl.BlockSpec(shape, lambda c: (0, 0, 0)),
        out_shape=jax.ShapeDtypeStruct(shape, F32),
        scratch_shapes=[
            pltpu.VMEM((2 * seqs, rows * channels, lanes), F32),
            pltpu.VMEM((2 * seqs * rows, 2 * lanes), BF16),
            pltpu.VMEM((2 * seqs * rows, 2 * lanes), BF16),
            pltpu.VMEM((2 * seqs * rows, 2 * lanes), F32),
            pltpu.VMEM((channels * 2 * rows, lanes), F32),
        ],
        cost_estimate=pl.CostEstimate(
            flops=channels * seqs * 2 * rows * lanes * lanes * 36,
            bytes_accessed=channels * (seqs * rows * lanes * 4 + total * 4),
            transcendentals=0,
        ),
        name="correlate",
    )(*pieces, *consts)


STEP = 1024
BANDS_PAD = 8


def lag_row(step, total):
    position = step * STEP + lax.broadcasted_iota(jnp.int32, (1, STEP), 1)
    return jnp.where(position < total // 2, position, position - total)


def network_kernel(
    factor_ref, embed_ref, hidden_ref, freq_ref, table_ref, first_ref, second_ref, cos1_ref, cos2_ref, *, total
):
    lag = lag_row(pl.program_id(0), total)
    length = total // 2
    phase = ((factor_ref[...] * lag) & (total - 1)).astype(F32) * (2.0 * math.pi / total)
    sine, cosine = sine_cosine(phase)
    scaled = lag.astype(F32) / length
    row = lax.broadcasted_iota(jnp.int32, (BANDS_PAD, STEP), 0)
    extra = jnp.where(row == 0, scaled, jnp.where(row == 1, 1.0, 0.0))
    table = jnp.concatenate([sine, cosine, extra], axis=0)
    table_ref[...] = stacked(table, 0)
    first, cos1 = sine_cosine(freq_ref[:, :1] * dot(embed_ref[...], wide(table, 0)))
    first_ref[...] = stacked(first, 0)
    cos1_ref[...] = cos1
    second, cos2 = sine_cosine(freq_ref[:, 1:] * dot(hidden_ref[...], wide(first, 0)))
    second_ref[...] = stacked(second, 0)
    cos2_ref[...] = cos2


def network(embed_weight, embed_bias, hidden_weight, frequency, total):
    hidden, features = embed_weight.shape
    bands = (features - 1) // 2
    factors = np.array(
        [[max(1, int(0.45 * total * 10000.0 ** (-band / bands)))] for band in range(bands)], np.int32
    )
    embed = jnp.concatenate(
        [
            embed_weight[:, 1:],
            embed_weight[:, :1],
            embed_bias[:, None],
            jnp.zeros((hidden, BANDS_PAD - 2), F32),
        ],
        axis=1,
    )
    args = (jnp.asarray(factors), narrow(embed, 1), narrow(hidden_weight, 1), frequency.T)
    whole = [pl.BlockSpec(a.shape, lambda i: (0, 0)) for a in args]
    heights = ((2 * (2 * bands + BANDS_PAD), BF16), (2 * hidden, BF16), (2 * hidden, BF16), (hidden, F32), (hidden, F32))
    return pl.pallas_call(
        functools.partial(network_kernel, total=total),
        grid=(total // STEP,),
        in_specs=whole,
        out_specs=[pl.BlockSpec((h, STEP), lambda i: (0, i)) for h, _ in heights],
        out_shape=[jax.ShapeDtypeStruct((h, total), t) for h, t in heights],
        cost_estimate=pl.CostEstimate(
            flops=total * hidden * 600, bytes_accessed=total * hidden * 20, transcendentals=0
        ),
        name="network",
    )(*args)


def backward_kernel(*refs, chunks, total):
    lag_refs = refs[:chunks]
    (
        table_ref, first_ref, second_ref, cos1_ref, cos2_ref, decay_ref, output_ref, hidden_ref,
        own_ref, net_ref, sum1_ref, sum3_ref, sum5_ref,
    ) = refs[chunks:]
    step = pl.program_id(0)

    @pl.when(step == 0)
    def _():
        for ref in (sum1_ref, sum3_ref, sum5_ref):
            ref[...] = jnp.zeros_like(ref)

    lags = jnp.concatenate(
        [
            jnp.concatenate([ref[k] for k in range(ref.shape[0])], axis=1)
            for ref in lag_refs
        ],
        axis=0,
    )
    length = total // 2
    distance = jnp.abs(lag_row(step, total)).astype(F32)
    window = jnp.exp(-decay_ref[...] * distance / length)
    shaped = lags * window * (1.0 / math.sqrt(total))
    far = shaped * (distance / length)
    sum1_ref[...] += dot_lanes(stacked(jnp.concatenate([shaped, far], axis=0), 0), second_ref[...])
    second = dot(output_ref[...], wide(shaped, 0)) * cos2_ref[...]
    high, low = split(second)
    sum3_ref[...] += dot_lanes(jnp.concatenate([high, low], axis=0), first_ref[...])
    first = dot(hidden_ref[...], jnp.concatenate([high, high, low], axis=0)) * cos1_ref[...]
    sum5_ref[...] += dot_lanes(stacked(first, 0), table_ref[...])

    @pl.when(step == pl.num_programs(0) - 1)
    def _():
        def joined(ref):
            rows, cols = ref.shape[0] // 2, ref.shape[1] // 2
            return ref[:rows, :cols] + ref[:rows, cols:] + ref[rows:, :cols]

        own_ref[...] = joined(sum1_ref)
        net = jnp.concatenate([joined(sum3_ref), joined(sum5_ref)], axis=1)
        net_ref[:, : net.shape[1]] = net
        net_ref[:, net.shape[1] :] = jnp.zeros((net.shape[0], LANES - net.shape[1]), F32)


def backward(lags, saved, decay, output_weight, hidden_weight, frequency, total):
    _, _, lag_count = lags[0].shape
    own = output_weight.shape[0]
    hidden = hidden_weight.shape[0]
    table, _, _, _, _ = saved
    args = (
        decay[:, None],
        narrow(output_weight.T, 1),
        narrow((hidden_weight * frequency[1][:, None]).T, 1),
    )
    specs = [pl.BlockSpec((STEP // lag_count, a.shape[1], lag_count), lambda i: (i, 0, 0)) for a in lags]
    specs += [pl.BlockSpec((a.shape[0], STEP), lambda i: (0, i)) for a in saved]
    specs += [pl.BlockSpec(a.shape, lambda i: (0, 0)) for a in args]
    return pl.pallas_call(
        functools.partial(backward_kernel, chunks=len(lags), total=total),
        grid=(total // STEP,),
        in_specs=specs,
        out_specs=[
            pl.BlockSpec((2 * own, hidden), lambda i: (0, 0)),
            pl.BlockSpec((hidden, LANES), lambda i: (0, 0)),
        ],
        out_shape=[
            jax.ShapeDtypeStruct((2 * own, hidden), F32),
            jax.ShapeDtypeStruct((hidden, LANES), F32),
        ],
        scratch_shapes=[
            pltpu.VMEM((4 * own, 2 * hidden), F32),
            pltpu.VMEM((2 * hidden, 2 * hidden), F32),
            pltpu.VMEM((2 * hidden, table.shape[0]), F32),
        ],
        cost_estimate=pl.CostEstimate(
            flops=total * hidden * 2000, bytes_accessed=total * hidden * 20, transcendentals=0
        ),
        name="backward",
    )(*lags, *saved, *args)


def share(net, own):
    own = own[None]
    for axis in ("chan", "dp"):
        size = lax.axis_size(axis)
        place = lax.axis_index(axis)
        bit = size // 2
        lead = own.shape[0] if axis == "dp" else 1
        own = own.reshape(lead, 1, *own.shape[-2:])
        while bit:
            swap = [(i, i ^ bit) for i in range(size)]
            got_net, got = lax.ppermute((net, own), axis, swap)
            net = net + got_net
            upper = (place & bit) != 0
            own = jnp.stack(
                [jnp.where(upper, got, own), jnp.where(upper, own, got)], axis=2
            ).reshape(lead, -1, *own.shape[-2:])
            bit //= 2
        own = own.reshape(-1, *own.shape[-2:])
    return net, own.reshape(-1, own.shape[-1])


def work(
    signal,
    signal_grad,
    embed_weight,
    embed_bias,
    hidden_weight,
    frequency,
    output_weight,
    decay_rate,
):
    seq_local, chan_local, length = signal.shape
    total = 2 * length
    dp, chan = lax.axis_size("dp"), lax.axis_size("chan")
    own = chan_local // dp
    count = dp * chan
    lag_count = total // count
    hidden, features = embed_weight.shape
    scale = 1.0 / math.sqrt(seq_local * dp * length)
    at_dp, at_chan = lax.axis_index("dp"), lax.axis_index("chan")

    chunks = 2 if own % 16 == 0 else 1
    per = own // chunks
    order = sorted(range(1, dp), key=lambda p: -bin(p).count("1"))
    lags = []
    for q in range(chunks):
        pieces = []
        for p in order:
            sent = pick(signal, signal_grad, at_dp ^ p, own, q * per, per)
            pieces.append(lax.ppermute(sent, "dp", [(i, i ^ p) for i in range(dp)]))
        pieces.append(pick(signal, signal_grad, at_dp, own, q * per, per))
        lags.append(correlate(pieces, scale, count))

    saved = network(embed_weight, embed_bias, hidden_weight, frequency, total)
    first_own = at_chan * chan_local + at_dp * own
    my_output = lax.dynamic_slice_in_dim(output_weight, first_own, own, 0)
    my_decay = lax.dynamic_slice_in_dim(decay_rate, first_own, own, 0)
    shared = []
    for q in range(chunks):
        shared.append(lax.all_to_all(lags[q], ("dp", "chan"), 0, 0, tiled=True))
    sums, net = backward(lags, saved, my_decay, my_output, hidden_weight, frequency, total)
    my_decay_grad = -jnp.sum(my_output * sums[own:], axis=1, keepdims=True)
    mine = jnp.concatenate(
        [sums[:own], my_decay_grad, jnp.zeros((own, LANES - hidden - 1), F32)], axis=1
    )
    net, rows = share(net, mine)

    shared = jnp.stack([part.reshape(dp, chan, per, lag_count) for part in shared], axis=2)
    filter_grad = jnp.swapaxes(shared, 0, 1).reshape(chan * chan_local, lag_count)

    hidden_sums = net[:, :hidden]
    table_sums = net[:, hidden : hidden + features + 1]
    embed_sums = jnp.concatenate([table_sums[:, features - 1 : features], table_sums[:, : features - 1]], axis=1)
    bias_sums = table_sums[:, features]
    embed_grad = frequency[0][:, None] * embed_sums
    bias_grad = frequency[0] * bias_sums
    hidden_grad = frequency[1][:, None] * hidden_sums
    frequency_grad = jnp.stack(
        [
            jnp.sum(embed_weight * embed_sums, axis=1) + embed_bias * bias_sums,
            jnp.sum(hidden_weight * hidden_sums, axis=1),
        ]
    )
    return (
        filter_grad,
        embed_grad,
        bias_grad,
        hidden_grad,
        frequency_grad,
        rows[:, :hidden],
        rows[:, hidden],
    )


def solution(mesh):
    placed = (P("dp", "chan", None), P("dp", "chan", None), P(), P(), P(), P(), P(), P())
    return jax.shard_map(
        work,
        mesh=mesh,
        in_specs=placed,
        out_specs=(P(None, ("dp", "chan")), P(), P(), P(), P(), P(), P()),
        check_vma=False,
    )
```

time: 163 us -> 168 us (1.031)
  Pallas kernels: 21.9 us -> 64.9 us
  waiting for transfers between devices: 70.7 us -> 39.7 us
  blocking collectives: 27.3 us -> 0 us
  starting transfers between devices: 13.7 us -> 37.1 us
  other arithmetic: 2.41 us -> 12 us
  matrix products: 8.82 us -> 0 us
  local copies, waits for them, and re-layouts: 16.7 us -> 11.2 us
    all_to_all x3 -> x2, waiting for transfers between devices: 70.7 us -> 10.2 us  [work(): shared.append(lax.all_to_all(lags[q], ('dp', 'chan'), 0, 0, tiled=True))]
    pallas_call x1 -> x4, Pallas kernels: 21.9 us -> 64.9 us  [the longest x2 27.1 us: correlate(): pl.pallas_call(functools.partial(correlate_kernel, pieces=len(pieces)), g...]
    ppermute x0 -> x24, starting transfers between devices: none -> 29.6 us  [the longest x14 15.8 us: work(): pieces.append(lax.ppermute(sent, 'dp', [(i, i ^ p) for i in range(dp)]))]
    ppermute x0 -> x24, waiting for transfers between devices: none -> 29.5 us  [the longest x10 23.5 us: share(): got_net, got = lax.ppermute((net, own), axis, swap)]
    all_to_all x2 -> x0, blocking collectives: 27.3 us -> none  [the longest x1 14.6 us: sum_everywhere(): pieces = lax.all_to_all(flat, axes, 0, 0, tiled=True)]
    dot_general x8 -> x0, matrix products: 8.82 us -> none  [the longest x3 5.9 us: filter_loss(): jnp.dot(output_weight, second, precision=exact, preferred_element_type=jn...]
    unnamed x20 -> x33, local copies, waits for them, and re-layouts: 9.96 us -> 3.09 us
    all_to_all x3 -> x2, starting transfers between devices: 13.7 us -> 7.54 us  [work(): shared.append(lax.all_to_all(lags[q], ('dp', 'chan'), 0, 0, tiled=True))]
  transfers between devices with their start and end apart: 3 -> 26, of which waited for: 3 -> 10; matrix products, arithmetic and copies ran while one was open for 4% -> 9% of each run, Pallas kernels for 0% -> 20%
where the time goes in v2:
time: 168 us; the launch traced here: 166 us
  Pallas kernels  64.9 us (39%)
  waiting for transfers between devices  39.7 us (24%)
  starting transfers between devices  37.1 us (22%)
  other arithmetic  12 us (7%)
  local copies, waits for them, and re-layouts  11.2 us (7%)
    pallas_call x2, Pallas kernels, correlate(): pl.pallas_call(functools.partial(correlate_kernel, pieces=len(pieces)), g...  27.1 us
    ppermute x10, waiting for transfers between devices, share(): got_net, got = lax.ppermute((net, own), axis, swap)  23.5 us
    pallas_call x1, Pallas kernels, network(): pl.pallas_call(functools.partial(network_kernel, total=total), grid=(tota...  19.7 us
    pallas_call x1, Pallas kernels, backward(): pl.pallas_call(functools.partial(backward_kernel, chunks=len(lags), total...  18.1 us
    ppermute x14, starting transfers between devices, work(): pieces.append(lax.ppermute(sent, 'dp', [(i, i ^ p) for i in range(dp)]))  15.8 us
    ppermute x10, starting transfers between devices, share(): got_net, got = lax.ppermute((net, own), axis, swap)  13.8 us
    all_to_all x2, waiting for transfers between devices, work(): shared.append(lax.all_to_all(lags[q], ('dp', 'chan'), 0, 0, tiled=True))  10.2 us
    all_to_all x2, starting transfers between devices, work(): shared.append(lax.all_to_all(lags[q], ('dp', 'chan'), 0, 0, tiled=True))  7.54 us
  transfers between devices with their start and end apart: 26, of which 10 were waited for; matrix products, arithmetic and copies ran while one was open for 9% of the time, Pallas kernels for 20%

profile of v2, /device:TPU:0, one launch (start us, length us, event | category | flops | bytes accessed | tf_op | source)
XLA Modules:
  0.0 166.1 jit_solution(16929225177693371044)
XLA Ops:
  0.7 2.7 %dynamic-slice_bitcast_fusion.16 = (bf16[1,1,8,8192]{3,2,1,0:T(8,128)(2,1)S(1)}, bf16[1,1,8,8192]{3,2,1,0:T(8,128)(2,1)S(1)}, bf16[1,1,8,8192]{3,2,1,0:T(8,128)(...) fusion(bf16[1,128,8192]{2,1,0:T(8,128)(2,1)} %param.22, ...), kind=kLoop, calls=%fused_computation.38 | loop fusion | bytes 8388672 | tf_op jit(solution)/shard_map/stack | solution.py:97
  4.2 3.4 %collective-permute-start = (bf16[2,1,8,8192]{3,2,1,0:T(8,128)(2,1)}, bf16[2,1,8,8192]{3,2,1,0:T(8,128)(2,1)}, u32[]{:S(2)}, u32[]{:S(2)}) collective-permute-start(bf16[2,1,8,8192]{3,2,1,0:T(8,128)(2,1)} %pad_maximum_fusion), channel_id=1, source_target_pairs={{0,28},{4,24},{8,20},{12,16},{16,12},{20,8},{24,4},{28,0},{1,29},{... | collective-permute-start | bytes 786440 | tf_op jit(solution)/shard_map/ppermute | solution.py:390
  9.9 2.4 %collective-permute-start.3 = (bf16[2,1,8,8192]{3,2,1,0:T(8,128)(2,1)S(1)}, bf16[2,1,8,8192]{3,2,1,0:T(8,128)(2,1)}, u32[]{:S(2)}, u32[]{:S(2)}) collective-permute-start(bf16[2,1,8,8192]{3,2,1,0:T(8,128)(2,1)S(1)} %pad_maximum_fusion.3), channel_id=1, source_target_pairs={{0,24},{4,28},{8,16},{12,20},{16,8},{20,12},{24,0},{28,4},{1,25},{... | collective-permute-start | bytes 786440 | tf_op jit(solution)/shard_map/ppermute | solution.py:390
  21.3 1.9 %collective-permute-start.13 = (bf16[2,1,8,8192]{3,2,1,0:T(8,128)(2,1)S(1)}, bf16[2,1,8,8192]{3,2,1,0:T(8,128)(2,1)}, u32[]{:S(2)}, u32[]{:S(2)}) collective-permute-start(bf16[2,1,8,8192]{3,2,1,0:T(8,128)(2,1)S(1)} %pad_maximum_fusion.14), channel_id=1, source_target_pairs={{0,16},{4,20},{8,24},{12,28},{16,0},{20,4},{24,8},{28,12},{1,17},{... | collective-permute-start | bytes 786440 | tf_op jit(solution)/shard_map/ppermute | solution.py:390
  23.2 3.6 %collective-permute-done.3.refs_3_ = bf16[2,1,8,8192]{3,2,1,0:T(8,128)(2,1)} collective-permute-done((bf16[2,1,8,8192]{3,2,1,0:T(8,128)(2,1)S(1)}, bf16[2,1,8,8192]{3,2,1,0:T(8,128)(2,1)}, u32[]{:S(2)}, u32[]{:S(2)}) %collective-permute-start.3) | collective-permute-done | bytes 262176 | tf_op jit(solution)/shard_map/ppermute | solution.py:390
  28.4 19.7 %network.1 = (bf16[80,16384]{1,0:T(8,128)(2,1)}, bf16[128,16384]{1,0:T(8,128)(2,1)}, bf16[128,16384]{1,0:T(8,128)(2,1)}, f32[64,16384]{1,0:T(8,128)}, f32[64,16384]{1,0:T(8,128)}) custom-call(s32[16,1]{1,0:T(8,128)} %constant.66.clone.factor_ref, bf16[64,120]{1,0:T(8,128)(2,1)} %pad_maximum_fusion.22.embed_ref, ...), custom_call_target="tpu_custom_call" | custom-call | flops 629145600 | bytes 20971520 | tf_op jit(solution)/shard_map/network/pallas_call | solution.py:247
  49.4 1.6 collective-permute-start.10
  54.0 13.6 %correlate.2.refs_0_ = f32[32,8,512]{2,1,0:T(8,128)} custom-call(bf16[2,1,8,8192]{3,2,1,0:T(8,128)(2,1)} %collective-permute-done.refs_0_, bf16[2,1,8,8192]{3,2,1,0:T(8,128)(2,1)} %collective-permute-done.1.refs_1_, bf16[2,1,8,8192]{3,2,1,0:T(8,128)(2,1)} %collective-permute-done.2.refs_2_, bf16[2,1,8,8192]{3,2,1,0:T(8,128)(2,1)} %collective-permute-done.3.refs_3_, ...), custom_call_target="tpu_custom_call" | custom-call | flops 4831838208 | bytes 2621440 | tf_op jit(solution)/shard_map/correlate/pallas_call | solution.py:178
  67.6 2.2 %collective-permute-done.7.refs_0_ = bf16[2,1,8,8192]{3,2,1,0:T(8,128)(2,1)S(1)} collective-permute-done((bf16[2,1,8,8192]{3,2,1,0:T(8,128)(2,1)S(1)}, bf16[2,1,8,8192]{3,2,1,0:T(8,128)(2,1)S(1)}, u32[]{:S(2)}, u32[]{:S(2)}) %collective-permute-start.7) | collective-permute-done | bytes 262176 | tf_op jit(solution)/shard_map/ppermute | solution.py:390
  70.5 13.5 %correlate.3.refs_1_ = f32[32,8,512]{2,1,0:T(8,128)} custom-call(bf16[2,1,8,8192]{3,2,1,0:T(8,128)(2,1)} %copy-done.13, bf16[2,1,8,8192]{3,2,1,0:T(8,128)(2,1)} %copy-done.12, bf16[2,1,8,8192]{3,2,1,0:T(8,128)(2,1)} %copy-done.11, bf16[2,1,8,8192]{3,2,1,0:T(8,128)(2,1)} %copy-done.10, bf16[2,1,8,8192]{3,2,1,0:T(8,128)(2,1)} %copy-done.9, ...), custom_call_target="tpu_custom_call" | custom-call | flops 4831838208 | bytes 2621440 | tf_op jit(solution)/shard_map/correlate/pallas_call | solution.py:178
  84.0 18.1 %backward.1 = (f32[32,64]{1,0:T(8,128)}, f32[64,128]{1,0:T(8,128)}) custom-call(f32[32,8,512]{2,1,0:T(8,128)} %correlate.2.refs_0_, f32[32,8,512]{2,1,0:T(8,128)} %correlate.3.refs_1_, bf16[80,16384]{1,0:T(8,128)(2,1)} %get-tuple-element.14.refs_2_, bf16[128,16384]{1,0:T(8,128)(2,1)} %get-tuple-element.15.refs_3_, ...), custom_call_target="tpu_custom_call" | custom-call | flops 2097152000 | bytes 20971520 | tf_op jit(solution)/shard_map/backward/pallas_call | solution.py:317
  104.7 2.6 %collective-permute-start.19 = (f32[1,1,16,128]{3,2,1,0:T(8,128)S(1)}, f32[1,1,16,128]{3,2,1,0:T(8,128)S(1)}, u32[]{:S(2)}, u32[]{:S(2)}) collective-permute-start(f32[1,1,16,128]{3,2,1,0:T(8,128)S(1)} %maximum_bitcast_fusion.3), channel_id=1, source_target_pairs={{0,2},{1,3},{2,0},{3,1},{4,6},{5,7},{6,4},{7,5},{8,10},{9,11},{10,... | collective-permute-start | bytes 24584 | tf_op jit(solution)/shard_map/ppermute | solution.py:351
  107.3 2.0 %collective-permute-done.19 = f32[1,1,16,128]{3,2,1,0:T(8,128)S(1)} collective-permute-done((f32[1,1,16,128]{3,2,1,0:T(8,128)S(1)}, f32[1,1,16,128]{3,2,1,0:T(8,128)S(1)}, u32[]{:S(2)}, u32[]{:S(2)}) %collective-permute-start.19) | collective-permute-done | bytes 8224 | tf_op jit(solution)/shard_map/ppermute | solution.py:351
  109.3 1.6 collective-permute-start.20
  110.9 3.9 %all-to-all-start = ((f32[32,8,512]{2,1,0:T(8,128)}), f32[32,8,512]{2,1,0:T(8,128)S(1)}, u32[]{:S(2)}, u32[]{:S(2)}) async-start(f32[32,8,512]{2,1,0:T(8,128)} %correlate.2.refs_0_), calls=%async_computation | async-start | bytes 1048576 | tf_op jit(solution)/shard_map/all_to_all | solution.py:400
  115.7 2.7 %collective-permute-start.14 = (f32[64,128]{0,1:T(8,128)S(1)}, f32[64,128]{0,1:T(8,128)S(1)}, u32[]{:S(2)}, u32[]{:S(2)}) collective-permute-start(f32[64,128]{0,1:T(8,128)S(1)} %copy.85), channel_id=1, source_target_pairs={{0,2},{1,3},{2,0},{3,1},{4,6},{5,7},{6,4},{7,5},{8,10},{9,11},{10,... | collective-permute-start | bytes 98312 | tf_op jit(solution)/shard_map/ppermute | solution.py:351
  118.5 1.5 collective-permute-start.21
  120.0 12.6 %collective-permute-done.14 = f32[64,128]{0,1:T(8,128)S(1)} collective-permute-done((f32[64,128]{0,1:T(8,128)S(1)}, f32[64,128]{0,1:T(8,128)S(1)}, u32[]{:S(2)}, u32[]{:S(2)}) %collective-permute-start.14) | collective-permute-done | bytes 32800 | tf_op jit(solution)/shard_map/ppermute | solution.py:351
  134.3 2.7 %collective-permute-done.15 = f32[64,128]{0,1:T(8,128)S(1)} collective-permute-done((f32[64,128]{0,1:T(8,128)S(1)}, f32[64,128]{0,1:T(8,128)S(1)}, u32[]{:S(2)}, u32[]{:S(2)}) %collective-permute-start.15) | collective-permute-done | bytes 32800 | tf_op jit(solution)/shard_map/ppermute | solution.py:351
  137.0 1.5 collective-permute-start.16
  138.5 2.8 %collective-permute-done.16 = f32[64,128]{0,1:T(8,128)S(1)} collective-permute-done((f32[64,128]{0,1:T(8,128)S(1)}, f32[64,128]{0,1:T(8,128)S(1)}, u32[]{:S(2)}, u32[]{:S(2)}) %collective-permute-start.16) | collective-permute-done | bytes 32800 | tf_op jit(solution)/shard_map/ppermute | solution.py:351
  142.9 2.8 %collective-permute-done.17 = f32[64,128]{0,1:T(8,128)S(1)} collective-permute-done((f32[64,128]{0,1:T(8,128)S(1)}, f32[64,128]{0,1:T(8,128)S(1)}, u32[]{:S(2)}, u32[]{:S(2)}) %collective-permute-start.17) | collective-permute-done | bytes 32800 | tf_op jit(solution)/shard_map/ppermute | solution.py:351
  147.1 3.6 %all-to-all-start.1 = ((f32[32,8,512]{2,1,0:T(8,128)}), f32[32,8,512]{2,1,0:T(8,128)S(1)}, u32[]{:S(2)}, u32[]{:S(2)}) async-start(f32[32,8,512]{2,1,0:T(8,128)} %correlate.3.refs_1_), calls=%async_computation.1 | async-start | bytes 1048576 | tf_op jit(solution)/shard_map/all_to_all | solution.py:400
  154.8 10.2 %all-to-all-done.1 = f32[32,8,512]{2,1,0:T(8,128)S(1)} async-done(((f32[32,8,512]{2,1,0:T(8,128)}), f32[32,8,512]{2,1,0:T(8,128)S(1)}, u32[]{:S(2)}, u32[]{:S(2)}) %all-to-all-start.1) | async-done | bytes 524320 | tf_op jit(solution)/shard_map/all_to_all | solution.py:400
  (137 shorter events, 31.8 us)
Async XLA Ops:
  4.2 16.1 %collective-permute-start = (bf16[2,1,8,8192]{3,2,1,0:T(8,128)(2,1)}, bf16[2,1,8,8192]{3,2,1,0:T(8,128)(2,1)}, u32[]{:S(2)}, u32[]{:S(2)}) collective-permute-start(bf16[2,1,8,8192]{3,2,1,0:T(8,128)(2,1)} %pad_maximum_fusion), channel_id=1, source_target_pairs={{0,28},{4,24},{8,20},{12,16},{16,12},{20,8},{24,4},{28,0},{1,29},{... | collective-permute-start | bytes 786440 | tf_op jit(solution)/shard_map/ppermute | solution.py:390
  8.3 12.9 %collective-permute-start.1 = (bf16[2,1,8,8192]{3,2,1,0:T(8,128)(2,1)}, bf16[2,1,8,8192]{3,2,1,0:T(8,128)(2,1)}, u32[]{:S(2)}, u32[]{:S(2)}) collective-permute-start(bf16[2,1,8,8192]{3,2,1,0:T(8,128)(2,1)} %pad_maximum_fusion.1), channel_id=1, source_target_pairs={{0,12},{4,8},{8,4},{12,0},{16,28},{20,24},{24,20},{28,16},{1,13},{... | collective-permute-start | bytes 786440 | tf_op jit(solution)/shard_map/ppermute | solution.py:390
  9.8 11.4 %collective-permute-start.2 = (bf16[2,1,8,8192]{3,2,1,0:T(8,128)(2,1)}, bf16[2,1,8,8192]{3,2,1,0:T(8,128)(2,1)}, u32[]{:S(2)}, u32[]{:S(2)}) collective-permute-start(bf16[2,1,8,8192]{3,2,1,0:T(8,128)(2,1)} %pad_maximum_fusion.2), channel_id=1, source_target_pairs={{0,20},{4,16},{8,28},{12,24},{16,4},{20,0},{24,12},{28,8},{1,21},{... | collective-permute-start | bytes 786440 | tf_op jit(solution)/shard_map/ppermute | solution.py:390
  9.9 16.9 %collective-permute-start.3 = (bf16[2,1,8,8192]{3,2,1,0:T(8,128)(2,1)S(1)}, bf16[2,1,8,8192]{3,2,1,0:T(8,128)(2,1)}, u32[]{:S(2)}, u32[]{:S(2)}) collective-permute-start(bf16[2,1,8,8192]{3,2,1,0:T(8,128)(2,1)S(1)} %pad_maximum_fusion.3), channel_id=1, source_target_pairs={{0,24},{4,28},{8,16},{12,20},{16,8},{20,12},{24,0},{28,4},{1,25},{... | collective-permute-start | bytes 786440 | tf_op jit(solution)/shard_map/ppermute | solution.py:390
  12.4 37.1 %collective-permute-start.4 = (bf16[2,1,8,8192]{3,2,1,0:T(8,128)(2,1)S(1)}, bf16[2,1,8,8192]{3,2,1,0:T(8,128)(2,1)}, u32[]{:S(2)}, u32[]{:S(2)}) collective-permute-start(bf16[2,1,8,8192]{3,2,1,0:T(8,128)(2,1)S(1)} %pad_maximum_fusion.4), channel_id=1, source_target_pairs={{0,4},{4,0},{8,12},{12,8},{16,20},{20,16},{24,28},{28,24},{1,5},{5... | collective-permute-start | bytes 786440 | tf_op jit(solution)/shard_map/ppermute | solution.py:390
  20.3 29.1 %collective-permute-start.5 = (bf16[2,1,8,8192]{3,2,1,0:T(8,128)(2,1)S(1)}, bf16[2,1,8,8192]{3,2,1,0:T(8,128)(2,1)}, u32[]{:S(2)}, u32[]{:S(2)}) collective-permute-start(bf16[2,1,8,8192]{3,2,1,0:T(8,128)(2,1)S(1)} %copy-done.1), channel_id=1, source_target_pairs={{0,8},{4,12},{8,0},{12,4},{16,24},{20,28},{24,16},{28,20},{1,9},{5... | collective-permute-start | bytes 786440 | tf_op jit(solution)/shard_map/ppermute | solution.py:390
  21.2 29.8 %collective-permute-start.6 = (bf16[2,1,8,8192]{3,2,1,0:T(8,128)(2,1)S(1)}, bf16[2,1,8,8192]{3,2,1,0:T(8,128)(2,1)}, u32[]{:S(2)}, u32[]{:S(2)}) collective-permute-start(bf16[2,1,8,8192]{3,2,1,0:T(8,128)(2,1)S(1)} %pad_maximum_fusion.6), channel_id=1, source_target_pairs={{0,16},{4,20},{8,24},{12,28},{16,0},{20,4},{24,8},{28,12},{1,17},{... | collective-permute-start | bytes 786440 | tf_op jit(solution)/shard_map/ppermute | solution.py:390
  21.3 29.9 %collective-permute-start.13 = (bf16[2,1,8,8192]{3,2,1,0:T(8,128)(2,1)S(1)}, bf16[2,1,8,8192]{3,2,1,0:T(8,128)(2,1)}, u32[]{:S(2)}, u32[]{:S(2)}) collective-permute-start(bf16[2,1,8,8192]{3,2,1,0:T(8,128)(2,1)S(1)} %pad_maximum_fusion.14), channel_id=1, source_target_pairs={{0,16},{4,20},{8,24},{12,28},{16,0},{20,4},{24,8},{28,12},{1,17},{... | collective-permute-start | bytes 786440 | tf_op jit(solution)/shard_map/ppermute | solution.py:390
  26.8 25.9 %collective-permute-start.12 = (bf16[2,1,8,8192]{3,2,1,0:T(8,128)(2,1)S(1)}, bf16[2,1,8,8192]{3,2,1,0:T(8,128)(2,1)S(1)}, u32[]{:S(2)}, u32[]{:S(2)}) collective-permute-start(bf16[2,1,8,8192]{3,2,1,0:T(8,128)(2,1)S(1)} %pad_maximum_fusion.13), channel_id=1, source_target_pairs={{0,8},{4,12},{8,0},{12,4},{16,24},{20,28},{24,16},{28,20},{1,9},{5... | collective-permute-start | bytes 786440 | tf_op jit(solution)/shard_map/ppermute | solution.py:390
  49.4 18.1 %collective-permute-start.11 = (bf16[2,1,8,8192]{3,2,1,0:T(8,128)(2,1)S(1)}, bf16[2,1,8,8192]{3,2,1,0:T(8,128)(2,1)S(1)}, u32[]{:S(2)}, u32[]{:S(2)}) collective-permute-start(bf16[2,1,8,8192]{3,2,1,0:T(8,128)(2,1)S(1)} %pad_maximum_fusion.12), channel_id=1, source_target_pairs={{0,4},{4,0},{8,12},{12,8},{16,20},{20,16},{24,28},{28,24},{1,5},{5... | collective-permute-start | bytes 786440 | tf_op jit(solution)/shard_map/ppermute | solution.py:390
  49.4 18.1 %collective-permute-start.10 = (bf16[2,1,8,8192]{3,2,1,0:T(8,128)(2,1)S(1)}, bf16[2,1,8,8192]{3,2,1,0:T(8,128)(2,1)S(1)}, u32[]{:S(2)}, u32[]{:S(2)}) collective-permute-start(bf16[2,1,8,8192]{3,2,1,0:T(8,128)(2,1)S(1)} %pad_maximum_fusion.11), channel_id=1, source_target_pairs={{0,24},{4,28},{8,16},{12,20},{16,8},{20,12},{24,0},{28,4},{1,25},{... | collective-permute-start | bytes 786440 | tf_op jit(solution)/shard_map/ppermute | solution.py:390
  51.0 16.6 %collective-permute-start.9 = (bf16[2,1,8,8192]{3,2,1,0:T(8,128)(2,1)S(1)}, bf16[2,1,8,8192]{3,2,1,0:T(8,128)(2,1)S(1)}, u32[]{:S(2)}, u32[]{:S(2)}) collective-permute-start(bf16[2,1,8,8192]{3,2,1,0:T(8,128)(2,1)S(1)} %pad_maximum_fusion.10), channel_id=1, source_target_pairs={{0,20},{4,16},{8,28},{12,24},{16,4},{20,0},{24,12},{28,8},{1,21},{... | collective-permute-start | bytes 786440 | tf_op jit(solution)/shard_map/ppermute | solution.py:390
  51.2 16.4 %collective-permute-start.8 = (bf16[2,1,8,8192]{3,2,1,0:T(8,128)(2,1)S(1)}, bf16[2,1,8,8192]{3,2,1,0:T(8,128)(2,1)S(1)}, u32[]{:S(2)}, u32[]{:S(2)}) collective-permute-start(bf16[2,1,8,8192]{3,2,1,0:T(8,128)(2,1)S(1)} %pad_maximum_fusion.9), channel_id=1, source_target_pairs={{0,12},{4,8},{8,4},{12,0},{16,28},{20,24},{24,20},{28,16},{1,13},{... | collective-permute-start | bytes 786440 | tf_op jit(solution)/shard_map/ppermute | solution.py:390
  52.7 17.1 %collective-permute-start.7 = (bf16[2,1,8,8192]{3,2,1,0:T(8,128)(2,1)S(1)}, bf16[2,1,8,8192]{3,2,1,0:T(8,128)(2,1)S(1)}, u32[]{:S(2)}, u32[]{:S(2)}) collective-permute-start(bf16[2,1,8,8192]{3,2,1,0:T(8,128)(2,1)S(1)} %pad_maximum_fusion.8), channel_id=1, source_target_pairs={{0,28},{4,24},{8,20},{12,16},{16,12},{20,8},{24,4},{28,0},{1,29},{... | collective-permute-start | bytes 786440 | tf_op jit(solution)/shard_map/ppermute | solution.py:390
  104.7 4.6 %collective-permute-start.19 = (f32[1,1,16,128]{3,2,1,0:T(8,128)S(1)}, f32[1,1,16,128]{3,2,1,0:T(8,128)S(1)}, u32[]{:S(2)}, u32[]{:S(2)}) collective-permute-start(f32[1,1,16,128]{3,2,1,0:T(8,128)S(1)} %maximum_bitcast_fusion.3), channel_id=1, source_target_pairs={{0,2},{1,3},{2,0},{3,1},{4,6},{5,7},{6,4},{7,5},{8,10},{9,11},{10,... | collective-permute-start | bytes 24584 | tf_op jit(solution)/shard_map/ppermute | solution.py:351
  109.3 9.1 %collective-permute-start.20 = (f32[1,2,16,128]{3,2,1,0:T(8,128)S(1)}, f32[1,2,16,128]{3,2,1,0:T(8,128)S(1)}, u32[]{:S(2)}, u32[]{:S(2)}) collective-permute-start(f32[1,2,16,128]{3,2,1,0:T(8,128)S(1)} %maximum_bitcast_fusion.2), channel_id=1, source_target_pairs={{0,1},{1,0},{2,3},{3,2},{4,5},{5,4},{6,7},{7,6},{8,9},{9,8},{10,11... | collective-permute-start | bytes 49160 | tf_op jit(solution)/shard_map/ppermute | solution.py:351
  110.9 36.1 %all-to-all-start = ((f32[32,8,512]{2,1,0:T(8,128)}), f32[32,8,512]{2,1,0:T(8,128)S(1)}, u32[]{:S(2)}, u32[]{:S(2)}) async-start(f32[32,8,512]{2,1,0:T(8,128)} %correlate.2.refs_0_), calls=%async_computation | async-start | bytes 1048576 | tf_op jit(solution)/shard_map/all_to_all | solution.py:400
  115.7 16.9 %collective-permute-start.14 = (f32[64,128]{0,1:T(8,128)S(1)}, f32[64,128]{0,1:T(8,128)S(1)}, u32[]{:S(2)}, u32[]{:S(2)}) collective-permute-start(f32[64,128]{0,1:T(8,128)S(1)} %copy.85), channel_id=1, source_target_pairs={{0,2},{1,3},{2,0},{3,1},{4,6},{5,7},{6,4},{7,5},{8,10},{9,11},{10,... | collective-permute-start | bytes 98312 | tf_op jit(solution)/shard_map/ppermute | solution.py:351
  118.5 14.2 %collective-permute-start.21 = (f32[4,1,16,128]{3,2,0,1:T(8,128)S(1)}, f32[4,1,16,128]{3,2,0,1:T(8,128)S(1)}, u32[]{:S(2)}, u32[]{:S(2)}) collective-permute-start(f32[4,1,16,128]{3,2,0,1:T(8,128)S(1)} %bitcast.143), channel_id=1, source_target_pairs={{0,16},{4,20},{8,24},{12,28},{16,0},{20,4},{24,8},{28,12},{1,17},{... | collective-permute-start | bytes 98312 | tf_op jit(solution)/shard_map/ppermute | solution.py:351
  132.8 10.1 %collective-permute-start.22 = (f32[4,2,16,128]{3,2,0,1:T(8,128)S(1)}, f32[4,2,16,128]{3,2,0,1:T(8,128)S(1)}, u32[]{:S(2)}, u32[]{:S(2)}) collective-permute-start(f32[4,2,16,128]{3,2,0,1:T(8,128)S(1)} %maximum_bitcast_fusion.1), channel_id=1, source_target_pairs={{0,8},{4,12},{8,0},{12,4},{16,24},{20,28},{24,16},{28,20},{1,9},{5... | collective-permute-start | bytes 196616 | tf_op jit(solution)/shard_map/ppermute | solution.py:351
  137.0 4.3 %collective-permute-start.16 = (f32[64,128]{0,1:T(8,128)S(1)}, f32[64,128]{0,1:T(8,128)S(1)}, u32[]{:S(2)}, u32[]{:S(2)}) collective-permute-start(f32[64,128]{0,1:T(8,128)S(1)} %add.156), channel_id=1, source_target_pairs={{0,16},{4,20},{8,24},{12,28},{16,0},{20,4},{24,8},{28,12},{1,17},{... | collective-permute-start | bytes 98312 | tf_op jit(solution)/shard_map/ppermute | solution.py:351
  141.3 4.3 %collective-permute-start.17 = (f32[64,128]{0,1:T(8,128)S(1)}, f32[64,128]{0,1:T(8,128)S(1)}, u32[]{:S(2)}, u32[]{:S(2)}) collective-permute-start(f32[64,128]{0,1:T(8,128)S(1)} %add.157), channel_id=1, source_target_pairs={{0,8},{4,12},{8,0},{12,4},{16,24},{20,28},{24,16},{28,20},{1,9},{5... | collective-permute-start | bytes 98312 | tf_op jit(solution)/shard_map/ppermute | solution.py:351
  145.8 7.3 %collective-permute-start.23 = (f32[4,4,16,128]{3,2,1,0:T(8,128)S(1)}, f32[4,4,16,128]{3,2,1,0:T(8,128)S(1)}, u32[]{:S(2)}, u32[]{:S(2)}) collective-permute-start(f32[4,4,16,128]{3,2,1,0:T(8,128)S(1)} %bitcast.141), channel_id=1, source_target_pairs={{0,4},{4,0},{8,12},{12,8},{16,20},{20,16},{24,28},{28,24},{1,5},{5... | collective-permute-start | bytes 393224 | tf_op jit(solution)/shard_map/ppermute | solution.py:351
  147.1 17.9 %all-to-all-start.1 = ((f32[32,8,512]{2,1,0:T(8,128)}), f32[32,8,512]{2,1,0:T(8,128)S(1)}, u32[]{:S(2)}, u32[]{:S(2)}) async-start(f32[32,8,512]{2,1,0:T(8,128)} %correlate.3.refs_1_), calls=%async_computation.1 | async-start | bytes 1048576 | tf_op jit(solution)/shard_map/all_to_all | solution.py:400
  (17 other events, 154.3 us)

commit v3 on v2

v3 whole, which is shorter than its diff:
```python
import functools
import math

import jax
import jax.numpy as jnp
import numpy as np
from jax import lax
from jax.experimental import pallas as pl
from jax.experimental.pallas import tpu as pltpu
from jax.sharding import PartitionSpec as P


LANES = 128
F32 = jnp.float32
BF16 = jnp.bfloat16


def split(values):
    high = values.astype(BF16)
    return high, (values - high.astype(F32)).astype(BF16)


def split_table(values):
    high = values.astype(BF16)
    return high, (values - high.astype(np.float64)).astype(BF16)


def tables(rows, scale):
    total = 2 * rows * LANES
    odd = 2 * np.arange(rows) + 1
    angle = np.pi * (odd[:, None] * np.arange(2 * rows)[None, :] % (4 * rows)) / (2 * rows)
    first = np.concatenate([np.cos(angle[:, :rows]), -np.sin(angle[:, :rows])], axis=0)
    first = np.concatenate(split_table(first), axis=1)
    turn = np.pi * (odd[:, None] * np.arange(LANES)[None, :]) / total
    twist = np.stack([np.cos(turn), -np.sin(turn)]).astype(np.float32)
    untwist = (np.stack([np.cos(turn), np.sin(turn)]) * scale).astype(np.float32)
    fine = 2 * np.pi * (np.arange(LANES)[:, None] * np.arange(LANES)[None, :] % LANES) / LANES
    cosine, sine = np.cos(fine), np.sin(fine)
    second = np.block([[cosine, -sine], [sine, cosine]])
    sign = np.where(np.arange(2 * rows) < rows, 1.0, -1.0)[:, None]
    last = np.concatenate([np.cos(angle).T, -np.sin(angle).T], axis=1) * sign
    last_high, last_low = split_table(last)
    last = np.concatenate([last_high, last_low, last_high], axis=1)
    second, back = (
        np.concatenate([high, high, low], axis=0)
        for high, low in (split_table(second), split_table(second.T))
    )
    return first, twist, untwist, second, back, last


def dot(a, b):
    return jnp.dot(a, b, preferred_element_type=F32)


def stacked(values, axis):
    high, low = split(values)
    return jnp.concatenate([high, low], axis=axis)


def narrow(values, axis):
    high, low = split(values)
    return jnp.concatenate([high, low, high], axis=axis)


def wide(values, axis):
    high, low = split(values)
    return jnp.concatenate([high, high, low], axis=axis)


def dot_lanes(a, b):
    return lax.dot_general(a, b, (((1,), (1,)), ((), ())), preferred_element_type=F32)


def sine_cosine(angle):
    turns = (angle * (1.0 / math.pi) + 12582912.0) - 12582912.0
    rest = (angle - turns * 3.140625) - turns * 9.67653589793e-4
    sign = jnp.where((turns.astype(jnp.int32) & 1) != 0, -1.0, 1.0)
    square = rest * rest
    rest = rest * sign
    sine = (2.6000244184306192e-6 * square - 1.9806601562034863e-4) * square + 8.333017104043598e-3
    sine = (sine * square - 0.1666665708890745) * square * rest + rest
    cosine = (-2.6076816602017467e-7 * square + 2.4761870623092258e-5) * square
    cosine = ((cosine - 1.3888403220356624e-3) * square + 4.1666640707487275e-2) * square
    cosine = (cosine - 0.49999999549109586) * square + 1.0
    return sine, cosine * sign


def column(row):
    size = row.shape[1]
    at = [lax.broadcasted_iota(jnp.int32, (size, size), d) for d in (0, 1)]
    return jnp.sum(jnp.where(at[0] == at[1], row, 0.0), axis=1, keepdims=True)


def pick_kernel(x_ref, g_ref, *refs, partners, own, start):
    outs, (held_ref, in_sem, out_sem) = refs[: len(partners)], refs[len(partners) :]
    per = outs[0].shape[2]
    arrivals, departures = [], []
    for k, partner in enumerate(partners):
        first = pl.multiple_of((lax.axis_index("dp") ^ partner) * own + start, per)
        for at, ref in enumerate((x_ref, g_ref)):
            arrivals.append(
                pltpu.make_async_copy(
                    ref.at[:, pl.ds(first, per), :], held_ref.at[k, at], in_sem.at[k, at]
                )
            )
            arrivals[-1].start()
    for k in range(len(partners)):
        arrivals[2 * k].wait()
        arrivals[2 * k + 1].wait()
        departures.append(pltpu.make_async_copy(held_ref.at[k], outs[k], out_sem.at[k]))
        departures[-1].start()
    for departure in departures:
        departure.wait()


def pick(x, g, partners, own, start, count):
    seqs, _, length = x.shape
    shape = (2, seqs, count, length)
    if count % 8:
        firsts = [(lax.axis_index("dp") ^ p) * own + start for p in partners]
        return [
            jnp.stack([lax.dynamic_slice_in_dim(v, first, count, 1) for v in (x, g)])
            for first in firsts
        ]
    anywhere = pl.BlockSpec(memory_space=pl.ANY)
    return pl.pallas_call(
        functools.partial(pick_kernel, partners=partners, own=own, start=start),
        in_specs=[anywhere, anywhere],
        out_specs=[anywhere] * len(partners),
        out_shape=[jax.ShapeDtypeStruct(shape, BF16)] * len(partners),
        scratch_shapes=[
            pltpu.VMEM((len(partners), *shape), BF16),
            pltpu.SemaphoreType.DMA((len(partners), 2)),
            pltpu.SemaphoreType.DMA((len(partners),)),
        ],
        cost_estimate=pl.CostEstimate(
            flops=0, bytes_accessed=4 * len(partners) * math.prod(shape), transcendentals=0
        ),
        name="pick",
    )(x, g)


def correlate_kernel(*refs, pieces, held):
    piece_refs = refs[:pieces]
    refs = refs[:pieces] + refs[pieces + held :]
    (
        first_ref, twist_ref, untwist_ref, second_ref, back_ref, last_ref,
        out_ref, turn_ref, high_ref, low_ref, spec_ref, lag_ref,
    ) = refs[pieces:]
    _, seqs_each, channels, length = piece_refs[0].shape
    rows = length // LANES
    seqs = pieces * seqs_each
    c = pl.program_id(0)

    @pl.when(c == 0)
    def _():
        for s in range(seqs):
            for at in range(2):
                for row in range(rows):
                    turn_ref[at * seqs + s, pl.ds(row * channels, channels), :] = piece_refs[
                        s // seqs_each
                    ][at, s % seqs_each, :, pl.ds(row * LANES, LANES)].astype(F32)

    def samples(at, s):
        return turn_ref[at * seqs + s, pl.ds(c, rows, stride=channels), :].astype(BF16)

    cosine = jnp.concatenate([twist_ref[0]] * 2, axis=1)
    sine = jnp.concatenate([twist_ref[1]] * 2, axis=1)
    first = first_ref[...]
    for s in range(seqs):
        pair = jnp.concatenate([samples(0, s), samples(1, s)], axis=1)
        both = dot(first, jnp.concatenate([pair, pair], axis=0))
        real, imag = both[:rows], both[rows:]
        real, imag = real * cosine - imag * sine, real * sine + imag * cosine
        for at, part in ((0, slice(0, LANES)), (1, slice(LANES, 2 * LANES))):
            line = pl.ds((at * seqs + s) * rows, rows)
            row = jnp.concatenate([real[:, part], imag[:, part]], axis=1)
            high_ref[line, :], low_ref[line, :] = split(row)
    spec_ref[...] = dot(
        jnp.concatenate([high_ref[...], low_ref[...], high_ref[...]], axis=1), second_ref[...]
    )
    real = jnp.zeros((rows, LANES), F32)
    imag = jnp.zeros((rows, LANES), F32)
    for s in range(seqs):
        a = spec_ref[pl.ds(s * rows, rows), :]
        b = spec_ref[pl.ds((seqs + s) * rows, rows), :]
        a_real, a_imag, b_real, b_imag = a[:, :LANES], a[:, LANES:], b[:, :LANES], b[:, LANES:]
        real = real + (a_real * b_real + a_imag * b_imag)
        imag = imag + (a_real * b_imag - a_imag * b_real)
    high, low = split(jnp.concatenate([real, imag], axis=1))
    back = dot(jnp.concatenate([high, low, high], axis=1), back_ref[...])
    real, imag = back[:, :LANES], back[:, LANES:]
    cosine, sine = untwist_ref[0], untwist_ref[1]
    turned = jnp.concatenate([real * cosine - imag * sine, real * sine + imag * cosine], axis=0)
    high, low = split(turned)
    lag_ref[pl.ds(pl.multiple_of(c * 2 * rows, 2 * rows), 2 * rows), :] = dot(
        last_ref[...], jnp.concatenate([high, high, low], axis=0)
    )

    @pl.when(c == pl.num_programs(0) - 1)
    def _():
        owners, channels, lag_count = out_ref.shape
        each = lag_count // LANES
        for owner in range(owners):
            for k in range(each):
                out_ref[owner, :, pl.ds(k * LANES, LANES)] = lag_ref[
                    pl.ds(owner * each + k, channels, stride=2 * rows), :
                ]


def correlate(pieces, scale, owners, held, chunk, chunks):
    _, seqs_each, channels, length = pieces[0].shape
    lanes, rows = LANES, length // LANES
    seqs = seqs_each * len(pieces)
    total = 2 * rows * lanes
    consts = [jnp.asarray(t) for t in tables(rows, 2.0 * scale / total)]
    block = pl.BlockSpec(pieces[0].shape, lambda c: (0, 0, 0, 0))
    whole = [
        pl.BlockSpec(t.shape, functools.partial(lambda n, c: (0,) * n, t.ndim)) for t in consts
    ]
    held = [] if held is None else [held]
    return pl.pallas_call(
        functools.partial(correlate_kernel, pieces=len(pieces), held=len(held)),
        grid=(channels,),
        in_specs=[block] * len(pieces) + [pl.BlockSpec(memory_space=pl.ANY)] * len(held) + whole,
        out_specs=pl.BlockSpec((owners, channels, total // owners), lambda c: (0, chunk, 0)),
        out_shape=jax.ShapeDtypeStruct((owners, channels * chunks, total // owners), F32),
        input_output_aliases={len(pieces): 0} if held else {},
        scratch_shapes=[
            pltpu.VMEM((2 * seqs, rows * channels, lanes), F32),
            pltpu.VMEM((2 * seqs * rows, 2 * lanes), BF16),
            pltpu.VMEM((2 * seqs * rows, 2 * lanes), BF16),
            pltpu.VMEM((2 * seqs * rows, 2 * lanes), F32),
            pltpu.VMEM((channels * 2 * rows, lanes), F32),
        ],
        cost_estimate=pl.CostEstimate(
            flops=channels * seqs * 2 * rows * lanes * lanes * 36,
            bytes_accessed=channels * (seqs * rows * lanes * 4 + total * 4),
            transcendentals=0,
        ),
        name="correlate",
    )(*pieces, *held, *consts)


STEP = 2048
BANDS_PAD = 8


def lag_row(step, total):
    position = step * STEP + lax.broadcasted_iota(jnp.int32, (1, STEP), 1)
    return jnp.where(position < total // 2, position, position - total)


def network_kernel(
    factor_ref, embed_ref, bias_ref, hidden_ref, freq_ref,
    table_ref, first_ref, second_ref, cos1_ref, cos2_ref,
    embed_parts, hidden_parts, freq_cols, *, total,
):
    hidden = hidden_ref.shape[0]
    step = pl.program_id(0)

    @pl.when(step == 0)
    def _():
        embed = jnp.concatenate(
            [
                embed_ref[1:],
                embed_ref[:1],
                bias_ref[...],
                jnp.zeros((BANDS_PAD - 2, hidden), F32),
            ],
            axis=0,
        )
        embed_parts[...] = narrow(embed.T, 1)
        hidden_parts[...] = narrow(hidden_ref[...], 1)
        for k in range(2):
            freq_cols[k] = column(freq_ref[k : k + 1, :])

    lag = lag_row(step, total)
    length = total // 2
    phase = ((factor_ref[...] * lag) & (total - 1)).astype(F32) * (2.0 * math.pi / total)
    sine, cosine = sine_cosine(phase)
    scaled = lag.astype(F32) / length
    row = lax.broadcasted_iota(jnp.int32, (BANDS_PAD, STEP), 0)
    extra = jnp.where(row == 0, scaled, jnp.where(row == 1, 1.0, 0.0))
    table = jnp.concatenate([sine, cosine, extra], axis=0)
    table_ref[...] = stacked(table, 0)
    first, cos1 = sine_cosine(freq_cols[0] * dot(embed_parts[...], wide(table, 0)))
    first_ref[...] = stacked(first, 0)
    cos1_ref[...] = cos1
    second, cos2 = sine_cosine(freq_cols[1] * dot(hidden_parts[...], wide(first, 0)))
    second_ref[...] = stacked(second, 0)
    cos2_ref[...] = cos2


def network(embed_weight, embed_bias, hidden_weight, frequency, total):
    hidden, features = embed_weight.shape
    bands = (features - 1) // 2
    factors = np.array(
        [[max(1, int(0.45 * total * 10000.0 ** (-band / bands)))] for band in range(bands)], np.int32
    )
    args = (jnp.asarray(factors), embed_weight.T, embed_bias[None], hidden_weight, frequency)
    whole = [pl.BlockSpec(a.shape, lambda i: (0, 0)) for a in args]
    depth = 2 * bands + BANDS_PAD
    heights = ((2 * depth, BF16), (2 * hidden, BF16), (2 * hidden, BF16), (hidden, F32), (hidden, F32))
    return pl.pallas_call(
        functools.partial(network_kernel, total=total),
        grid=(total // STEP,),
        in_specs=whole,
        out_specs=[pl.BlockSpec((h, STEP), lambda i: (0, i)) for h, _ in heights],
        out_shape=[jax.ShapeDtypeStruct((h, total), t) for h, t in heights],
        scratch_shapes=[
            pltpu.VMEM((hidden, 3 * depth), BF16),
            pltpu.VMEM((hidden, 3 * hidden), BF16),
            pltpu.VMEM((2, hidden, 1), F32),
        ],
        cost_estimate=pl.CostEstimate(
            flops=total * hidden * 600, bytes_accessed=total * hidden * 20, transcendentals=0
        ),
        name="network",
    )(*args)


def backward_kernel(
    first_ref, lags_ref, table_ref, layer1_ref, layer2_ref, cos1_ref, cos2_ref,
    decay_ref, output_ref, hidden_ref, freq_ref,
    out_ref, output_parts, hidden_parts, decay_col, own_ref, sum1_ref, sum3_ref, sum5_ref, *, total,
):
    step = pl.program_id(0)
    owners, own, _ = lags_ref.shape
    hidden = hidden_ref.shape[0]

    @pl.when(step == 0)
    def _():
        for ref in (sum1_ref, sum3_ref, sum5_ref):
            ref[...] = jnp.zeros_like(ref)
        channels = output_ref.shape[1]
        own_ref[...] = pltpu.roll(output_ref[...], channels - first_ref[0], 1)[:, :own]
        output_parts[...] = narrow(own_ref[...], 1)
        hidden_parts[...] = narrow((hidden_ref[...] * column(freq_ref[1:2, :])).T, 1)
        place = [lax.broadcasted_iota(jnp.int32, (own, channels), d) for d in (0, 1)]
        decay_col[...] = jnp.sum(
            jnp.where(place[1] == place[0] + first_ref[0], decay_ref[...], 0.0), axis=1, keepdims=True
        )

    lags = jnp.concatenate([lags_ref[k] for k in range(owners)], axis=1)
    length = total // 2
    distance = jnp.abs(lag_row(step, total)).astype(F32)
    window = jnp.exp(-decay_col[...] * distance / length)
    shaped = lags * window * (1.0 / math.sqrt(total))
    far = shaped * (distance / length)
    sum1_ref[...] += dot_lanes(stacked(jnp.concatenate([shaped, far], axis=0), 0), layer2_ref[...])
    second = dot(output_parts[...], wide(shaped, 0)) * cos2_ref[...]
    high, low = split(second)
    sum3_ref[...] += dot_lanes(jnp.concatenate([high, low], axis=0), layer1_ref[...])
    first = dot(hidden_parts[...], jnp.concatenate([high, high, low], axis=0)) * cos1_ref[...]
    sum5_ref[...] += dot_lanes(stacked(first, 0), table_ref[...])

    @pl.when(step == pl.num_programs(0) - 1)
    def _():
        def joined(ref):
            rows, cols = ref.shape[0] // 2, ref.shape[1] // 2
            return ref[:rows, :cols] + ref[:rows, cols:] + ref[rows:, :cols]

        net = jnp.concatenate([joined(sum3_ref), joined(sum5_ref)], axis=1)
        out_ref[:hidden] = jnp.concatenate(
            [net, jnp.zeros((hidden, LANES - net.shape[1]), F32)], axis=1
        )
        sums = joined(sum1_ref)
        decay_grad = -jnp.sum(own_ref[...].T * sums[own:], axis=1, keepdims=True)
        out_ref[hidden:] = jnp.concatenate(
            [sums[:own], decay_grad, jnp.zeros((own, LANES - hidden - 1), F32)], axis=1
        )


def backward(first_own, lags, saved, decay_rate, output_weight, hidden_weight, frequency, total):
    _, own, lag_count = lags.shape
    hidden = hidden_weight.shape[0]
    args = (decay_rate[None], output_weight.T, hidden_weight, frequency)
    specs = [pl.BlockSpec((STEP // lag_count, own, lag_count), lambda i, first: (i, 0, 0))]
    specs += [pl.BlockSpec((a.shape[0], STEP), lambda i, first: (0, i)) for a in saved]
    specs += [pl.BlockSpec(a.shape, lambda i, first: (0, 0)) for a in args]
    return pl.pallas_call(
        functools.partial(backward_kernel, total=total),
        grid_spec=pltpu.PrefetchScalarGridSpec(
            num_scalar_prefetch=1,
            grid=(total // STEP,),
            in_specs=specs,
            out_specs=pl.BlockSpec((hidden + own, LANES), lambda i, first: (0, 0)),
            scratch_shapes=[
                pltpu.VMEM((hidden, 3 * own), BF16),
                pltpu.VMEM((hidden, 3 * hidden), BF16),
                pltpu.VMEM((own, 1), F32),
                pltpu.VMEM((hidden, own), F32),
                pltpu.VMEM((4 * own, 2 * hidden), F32),
                pltpu.VMEM((2 * hidden, 2 * hidden), F32),
                pltpu.VMEM((2 * hidden, saved[0].shape[0]), F32),
            ],
        ),
        out_shape=jax.ShapeDtypeStruct((hidden + own, LANES), F32),
        cost_estimate=pl.CostEstimate(
            flops=total * hidden * 2000, bytes_accessed=total * hidden * 20, transcendentals=0
        ),
        name="backward",
    )(first_own.reshape(1), lags, *saved, *args)


def share(both, hidden):
    own = both.shape[0] - hidden
    count = 1
    for axis in ("chan", "dp"):
        size = lax.axis_size(axis)
        place = lax.axis_index(axis)
        lead = count
        bit = size // 2
        while bit:
            got = lax.ppermute(both, axis, [(i, i ^ bit) for i in range(size)])
            mine, theirs = (v[hidden:].reshape(lead, -1, own, LANES) for v in (both, got))
            upper = (place & bit) != 0
            rows = jnp.stack(
                [jnp.where(upper, theirs, mine), jnp.where(upper, mine, theirs)], axis=2
            )
            both = jnp.concatenate([both[:hidden] + got[:hidden], rows.reshape(-1, LANES)], axis=0)
            count *= 2
            bit //= 2
    return both


def finish_kernel(
    both_ref, embed_ref, bias_ref, hidden_ref, freq_ref,
    embed_grad, bias_grad, hidden_grad, frequency_grad, output_grad, decay_grad,
):
    hidden, features = hidden_ref.shape[0], embed_ref.shape[0]
    net = both_ref[:hidden]
    turned = net.T
    rows = both_ref[hidden:].T
    output_grad[...] = rows[:hidden]
    decay_grad[...] = rows[hidden : hidden + 1]
    table = turned[hidden:]
    embed = jnp.concatenate([table[features - 1 : features], table[: features - 1]], axis=0)
    bias = table[features : features + 1]
    embed_grad[...] = freq_ref[:1] * embed
    bias_grad[...] = freq_ref[:1] * bias
    hidden_grad[...] = column(freq_ref[1:2, :]) * net[:, :hidden]
    frequency_grad[:1] = (
        jnp.sum(embed_ref[...] * embed, axis=0, keepdims=True) + bias_ref[...] * bias
    )
    frequency_grad[1:2] = jnp.sum(hidden_ref[...].T * turned[:hidden], axis=0, keepdims=True)


def finish(both, embed_weight, embed_bias, hidden_weight, frequency, channels):
    hidden, features = embed_weight.shape
    shapes = ((features, hidden), (1, hidden), (hidden, hidden), (2, hidden), (hidden, channels), (1, channels))
    embed, bias, hid, freq, output, decay = pl.pallas_call(
        finish_kernel,
        out_shape=[jax.ShapeDtypeStruct(shape, F32) for shape in shapes],
        name="finish",
    )(both, embed_weight.T, embed_bias[None], hidden_weight, frequency)
    return embed.T, bias[0], hid, freq, output.T, decay[0]


def work(
    signal,
    signal_grad,
    embed_weight,
    embed_bias,
    hidden_weight,
    frequency,
    output_weight,
    decay_rate,
):
    seq_local, chan_local, length = signal.shape
    total = 2 * length
    dp, chan = lax.axis_size("dp"), lax.axis_size("chan")
    own = chan_local // dp
    count = dp * chan
    hidden = hidden_weight.shape[0]
    channels = chan * chan_local
    scale = 1.0 / math.sqrt(seq_local * dp * length)
    at_dp, at_chan = lax.axis_index("dp"), lax.axis_index("chan")

    chunks = 2 if own % 16 == 0 else 1
    per = own // chunks
    partners = sorted(range(1, dp), key=lambda p: -bin(p).count("1"))
    lags = None
    for q in range(chunks):
        sent = pick(signal, signal_grad, (*partners, 0), own, q * per, per)
        pieces = []
        for k, p in enumerate(partners):
            pieces.append(lax.ppermute(sent[k], "dp", [(i, i ^ p) for i in range(dp)]))
        lags = correlate([*pieces, sent[-1]], scale, count, lags, q, chunks)

    saved = network(embed_weight, embed_bias, hidden_weight, frequency, total)
    shared = lax.all_to_all(lags, ("dp", "chan"), 0, 0, tiled=True)
    first_own = at_chan * chan_local + at_dp * own
    both = backward(
        first_own, lags, saved, decay_rate, output_weight, hidden_weight, frequency, total
    )
    both = share(both, hidden)
    filter_grad = jnp.swapaxes(shared.reshape(dp, chan, own, -1), 0, 1).reshape(channels, -1)
    return (
        filter_grad,
        *finish(both, embed_weight, embed_bias, hidden_weight, frequency, channels),
    )


def solution(mesh):
    placed = (P("dp", "chan", None), P("dp", "chan", None), P(), P(), P(), P(), P(), P())
    return jax.shard_map(
        work,
        mesh=mesh,
        in_specs=placed,
        out_specs=(P(None, ("dp", "chan")), P(), P(), P(), P(), P(), P()),
        check_vma=False,
    )
```

time: 168 us -> 131 us (0.78)
  local copies, waits for them, and re-layouts: 11.2 us -> 1.16 us
  other arithmetic: 12 us -> 2.38 us
  waiting for transfers between devices: 39.7 us -> 31.1 us
  starting transfers between devices: 37.1 us -> 30 us
    ppermute x24 -> x19, waiting for transfers between devices: 29.5 us -> 21.5 us  [the longest x5 15.8 us: share(): got = lax.ppermute(both, axis, [(i, i ^ bit) for i in range(size)])]
    another operation x27 -> x6, other arithmetic: 6.01 us -> 0.75 us  [share(): jnp.stack([jnp.where(upper, theirs, mine), jnp.where(upper, mine, theirs)...]
    ppermute x24 -> x19, starting transfers between devices: 29.6 us -> 25.3 us  [the longest x14 16.9 us: work(): pieces.append(lax.ppermute(sent[k], 'dp', [(i, i ^ p) for i in range(dp)]))]
    pallas_call x1, Pallas kernels: 19.7 us -> 16 us  [network(): pl.pallas_call(functools.partial(network_kernel, total=total), grid=(tota...]
    unnamed x33 -> x30, local copies, waits for them, and re-layouts: 3.09 us -> 0.06 us
    all_to_all x2 -> x1, starting transfers between devices: 7.54 us -> 4.72 us  [work(): shared = lax.all_to_all(lags, ('dp', 'chan'), 0, 0, tiled=True)]
    another operation x4, local copies, waits for them, and re-layouts: 2.72 us -> 0.04 us  [share(): jnp.stack([jnp.where(upper, theirs, mine), jnp.where(upper, mine, theirs)...]
    pallas_call x3 -> x6, Pallas kernels: 45.2 us -> 47.3 us  [the longest x2 27.2 us: correlate(): pl.pallas_call(functools.partial(correlate_kernel, pieces=len(pieces), he...]
  transfers between devices with their start and end apart: 26 -> 20, of which waited for: 10 -> 8; matrix products, arithmetic and copies ran while one was open for 9% -> 1% of each run, Pallas kernels for 20% -> 26%
where the time goes in v3:
time: 131 us; the launch traced here: 129 us
  Pallas kernels  63.4 us (48%)
  waiting for transfers between devices  31.1 us (24%)
  starting transfers between devices  30 us (23%)
  other arithmetic  2.38 us (2%)
    pallas_call x2, Pallas kernels, correlate(): pl.pallas_call(functools.partial(correlate_kernel, pieces=len(pieces), he...  27.2 us
    ppermute x14, starting transfers between devices, work(): pieces.append(lax.ppermute(sent[k], 'dp', [(i, i ^ p) for i in range(dp)]))  16.9 us
    pallas_call x1, Pallas kernels, network(): pl.pallas_call(functools.partial(network_kernel, total=total), grid=(tota...  16 us
    ppermute x5, waiting for transfers between devices, share(): got = lax.ppermute(both, axis, [(i, i ^ bit) for i in range(size)])  15.8 us
    pallas_call x1, Pallas kernels, backward(): pl.pallas_call(functools.partial(backward_kernel, total=total), grid_spec...  13.2 us
    all_to_all x1, waiting for transfers between devices, work(): shared = lax.all_to_all(lags, ('dp', 'chan'), 0, 0, tiled=True)  9.6 us
    ppermute x5, starting transfers between devices, share(): got = lax.ppermute(both, axis, [(i, i ^ bit) for i in range(size)])  8.42 us
    ppermute x14, waiting for transfers between devices, work(): pieces.append(lax.ppermute(sent[k], 'dp', [(i, i ^ p) for i in range(dp)]))  5.79 us
  transfers between devices with their start and end apart: 20, of which 8 were waited for; matrix products, arithmetic and copies ran while one was open for 1% of the time, Pallas kernels for 26%

profile of v3, /device:TPU:0, one launch (start us, length us, event | category | flops | bytes accessed | tf_op | source)
XLA Modules:
  0.0 129.1 jit_solution(4384852082228201447)
XLA Ops:
  0.6 2.6 %pick.3 = (bf16[2,1,8,8192]{3,2,1,0:T(8,128)(2,1)}, bf16[2,1,8,8192]{3,2,1,0:T(8,128)(2,1)}, bf16[2,1,8,8192]{3,2,1,0:T(8,128)(2,1)}, bf16[2,1,8,8192]{3,2,1,0:T...) custom-call(bf16[1,128,8192]{2,1,0:T(8,128)(2,1)} %x_ref.3, ...), custom_call_target="tpu_custom_call" | custom-call | bytes 4194304 | tf_op jit(solution)/shard_map/pick/pallas_call | solution.py:126
  3.2 4.0 %collective-permute-start.10 = (bf16[2,1,8,8192]{3,2,1,0:T(8,128)(2,1)}, bf16[2,1,8,8192]{3,2,1,0:T(8,128)(2,1)S(1)}, u32[]{:S(2)}, u32[]{:S(2)}) collective-permute-start(bf16[2,1,8,8192]{3,2,1,0:T(8,128)(2,1)} %get-tuple-element.45), channel_id=1, source_target_pairs={{0,24},{4,28},{8,16},{12,20},{16,8},{20,12},{24,0},{28,4},{1,25},{... | collective-permute-start | bytes 786440 | tf_op jit(solution)/shard_map/ppermute | solution.py:489
  7.9 2.3 %collective-permute-start.7 = (bf16[2,1,8,8192]{3,2,1,0:T(8,128)(2,1)}, bf16[2,1,8,8192]{3,2,1,0:T(8,128)(2,1)S(1)}, u32[]{:S(2)}, u32[]{:S(2)}) collective-permute-start(bf16[2,1,8,8192]{3,2,1,0:T(8,128)(2,1)} %get-tuple-element.42), channel_id=1, source_target_pairs={{0,28},{4,24},{8,20},{12,16},{16,12},{20,8},{24,4},{28,0},{1,29},{... | collective-permute-start | bytes 786440 | tf_op jit(solution)/shard_map/ppermute | solution.py:489
  10.3 2.6 %pick.2 = (bf16[2,1,8,8192]{3,2,1,0:T(8,128)(2,1)}, bf16[2,1,8,8192]{3,2,1,0:T(8,128)(2,1)}, bf16[2,1,8,8192]{3,2,1,0:T(8,128)(2,1)}, bf16[2,1,8,8192]{3,2,1,0:T...) custom-call(bf16[1,128,8192]{2,1,0:T(8,128)(2,1)} %x_ref.3, ...), custom_call_target="tpu_custom_call" | custom-call | bytes 4194304 | tf_op jit(solution)/shard_map/pick/pallas_call | solution.py:126
  12.8 1.8 %collective-permute-done.10.refs_3_ = bf16[2,1,8,8192]{3,2,1,0:T(8,128)(2,1)S(1)} collective-permute-done((bf16[2,1,8,8192]{3,2,1,0:T(8,128)(2,1)}, bf16[2,1,8,8192]{3,2,1,0:T(8,128)(2,1)S(1)}, u32[]{:S(2)}, u32[]{:S(2)}) %collective-permute-start.10) | collective-permute-done | bytes 262176 | tf_op jit(solution)/shard_map/ppermute | solution.py:489
  14.7 3.2 %collective-permute-start.9 = (bf16[2,1,8,8192]{3,2,1,0:T(8,128)(2,1)S(1)}, bf16[2,1,8,8192]{3,2,1,0:T(8,128)(2,1)S(1)}, u32[]{:S(2)}, u32[]{:S(2)}) collective-permute-start(bf16[2,1,8,8192]{3,2,1,0:T(8,128)(2,1)S(1)} %copy-done.7), channel_id=1, source_target_pairs={{0,20},{4,16},{8,28},{12,24},{16,4},{20,0},{24,12},{28,8},{1,21},{... | collective-permute-start | bytes 786440 | tf_op jit(solution)/shard_map/ppermute | solution.py:489
  17.9 2.9 %collective-permute-done.12.refs_5_ = bf16[2,1,8,8192]{3,2,1,0:T(8,128)(2,1)S(1)} collective-permute-done((bf16[2,1,8,8192]{3,2,1,0:T(8,128)(2,1)}, bf16[2,1,8,8192]{3,2,1,0:T(8,128)(2,1)S(1)}, u32[]{:S(2)}, u32[]{:S(2)}) %collective-permute-start.12) | collective-permute-done | bytes 262176 | tf_op jit(solution)/shard_map/ppermute | solution.py:489
  22.0 16.0 %network.1 = (bf16[80,16384]{1,0:T(8,128)(2,1)}, bf16[128,16384]{1,0:T(8,128)(2,1)}, bf16[128,16384]{1,0:T(8,128)(2,1)}, f32[64,16384]{1,0:T(8,128)}, f32[64,16384]{1,0:T(8,128)}) custom-call(s32[16,1]{1,0:T(8,128)} %constant.41.clone.factor_ref, f32[33,64]{1,0:T(8,128)} %bitcast.49, f32[1,64]{1,0:T(1,128)} %bitcast.52, f32[64,64]{1,0:T(8,128)} %hidden_ref.5, ...), custom_call_target="tpu_custom_call" | custom-call | flops 629145600 | bytes 20971520 | tf_op jit(solution)/shard_map/network/pallas_call | solution.py:305
  38.1 1.6 %collective-permute-start.2 = (bf16[2,1,8,8192]{3,2,1,0:T(8,128)(2,1)}, bf16[2,1,8,8192]{3,2,1,0:T(8,128)(2,1)S(1)}, u32[]{:S(2)}, u32[]{:S(2)}) collective-permute-start(bf16[2,1,8,8192]{3,2,1,0:T(8,128)(2,1)} %get-tuple-element.36), channel_id=1, source_target_pairs={{0,20},{4,16},{8,28},{12,24},{16,4},{20,0},{24,12},{28,8},{1,21},{... | collective-permute-start | bytes 786440 | tf_op jit(solution)/shard_map/ppermute | solution.py:489
  39.7 1.5 %collective-permute-start.3 = (bf16[2,1,8,8192]{3,2,1,0:T(8,128)(2,1)}, bf16[2,1,8,8192]{3,2,1,0:T(8,128)(2,1)S(1)}, u32[]{:S(2)}, u32[]{:S(2)}) collective-permute-start(bf16[2,1,8,8192]{3,2,1,0:T(8,128)(2,1)} %get-tuple-element.37), channel_id=1, source_target_pairs={{0,24},{4,28},{8,16},{12,20},{16,8},{20,12},{24,0},{28,4},{1,25},{... | collective-permute-start | bytes 786440 | tf_op jit(solution)/shard_map/ppermute | solution.py:489
  41.8 1.6 %collective-permute-start.6 = (bf16[2,1,8,8192]{3,2,1,0:T(8,128)(2,1)}, bf16[2,1,8,8192]{3,2,1,0:T(8,128)(2,1)}, u32[]{:S(2)}, u32[]{:S(2)}) collective-permute-start(bf16[2,1,8,8192]{3,2,1,0:T(8,128)(2,1)} %get-tuple-element.40), channel_id=1, source_target_pairs={{0,16},{4,20},{8,24},{12,28},{16,0},{20,4},{24,8},{28,12},{1,17},{... | collective-permute-start | bytes 786440 | tf_op jit(solution)/shard_map/ppermute | solution.py:489
  43.5 13.6 %correlate.2.refs_8_ = f32[32,16,512]{2,1,0:T(8,128)} custom-call(bf16[2,1,8,8192]{3,2,1,0:T(8,128)(2,1)} %copy-done.4, bf16[2,1,8,8192]{3,2,1,0:T(8,128)(2,1)} %copy-done.9, bf16[2,1,8,8192]{3,2,1,0:T(8,128)(2,1)} %copy-done.10, bf16[2,1,8,8192]{3,2,1,0:T(8,128)(2,1)} %copy-done, bf16[2,1,8,8192]{3,2,1,0:T(8,128)(2,1)} %copy-done.1, ...), custom_call_target="tpu_custom_call" | custom-call | flops 4831838208 | bytes 2621440 | tf_op jit(solution)/shard_map/correlate/pallas_call | solution.py:222
  58.3 13.6 %correlate.3.lags_ref = f32[32,16,512]{2,1,0:T(8,128)} custom-call(bf16[2,1,8,8192]{3,2,1,0:T(8,128)(2,1)} %copy-done.5, bf16[2,1,8,8192]{3,2,1,0:T(8,128)(2,1)} %copy-done.6, bf16[2,1,8,8192]{3,2,1,0:T(8,128)(2,1)} %copy-done.11, bf16[2,1,8,8192]{3,2,1,0:T(8,128)(2,1)} %copy-done.12, ...), custom_call_target="tpu_custom_call", output_to_operand_aliasing={{}: (8, {})} | custom-call | flops 4831838208 | bytes 2621440 | tf_op jit(solution)/shard_map/correlate/pallas_call | solution.py:222
  71.9 13.2 %backward.1 = f32[80,128]{1,0:T(8,128)} custom-call(s32[1]{0:T(128)} %bitcast.3.first_ref, f32[32,16,512]{2,1,0:T(8,128)} %correlate.3.lags_ref, bf16[80,16384]{1,0:T(8,128)(2,1)} %get-tuple-element.50.table_ref, bf16[128,16384]{1,0:T(8,128)(2,1)} %get-tuple-element.51.layer1_ref, bf16[128,16384]{1,0:T(8,128)(2,1)} %get-tuple-element.52.layer2_ref, ...), custom_call_target="tpu_custom_call" | custom-call | flops 2097152000 | bytes 20971520 | tf_op jit(solution)/shard_map/backward/pallas_call | solution.py:382
  85.1 3.1 %collective-permute-start.14 = (f32[80,128]{1,0:T(8,128)}, f32[80,128]{1,0:T(8,128)S(1)}, u32[]{:S(2)}, u32[]{:S(2)}) collective-permute-start(f32[80,128]{1,0:T(8,128)} %backward.1), channel_id=1, source_target_pairs={{0,2},{1,3},{2,0},{3,1},{4,6},{5,7},{6,4},{7,5},{8,10},{9,11},{10,... | collective-permute-start | bytes 122888 | tf_op jit(solution)/shard_map/ppermute | solution.py:416
  88.1 2.6 %collective-permute-done.14 = f32[80,128]{1,0:T(8,128)S(1)} collective-permute-done((f32[80,128]{1,0:T(8,128)}, f32[80,128]{1,0:T(8,128)S(1)}, u32[]{:S(2)}, u32[]{:S(2)}) %collective-permute-start.14) | collective-permute-done | bytes 40992 | tf_op jit(solution)/shard_map/ppermute | solution.py:416
  92.2 1.5 %collective-permute-start.15 = (f32[96,128]{1,0:T(8,128)S(1)}, f32[96,128]{1,0:T(8,128)S(1)}, u32[]{:S(2)}, u32[]{:S(2)}) collective-permute-start(f32[96,128]{1,0:T(8,128)S(1)} %pad_maximum_fusion.7), channel_id=1, source_target_pairs={{0,1},{1,0},{2,3},{3,2},{4,5},{5,4},{6,7},{7,6},{8,9},{9,8},{10,11... | collective-permute-start | bytes 147464 | tf_op jit(solution)/shard_map/ppermute | solution.py:416
  93.8 2.6 %collective-permute-done.15 = f32[96,128]{1,0:T(8,128)S(1)} collective-permute-done((f32[96,128]{1,0:T(8,128)S(1)}, f32[96,128]{1,0:T(8,128)S(1)}, u32[]{:S(2)}, u32[]{:S(2)}) %collective-permute-start.15) | collective-permute-done | bytes 49184 | tf_op jit(solution)/shard_map/ppermute | solution.py:416
  96.4 1.9 %collective-permute-start.16 = (f32[128,128]{1,0:T(8,128)S(1)}, f32[128,128]{1,0:T(8,128)S(1)}, u32[]{:S(2)}, u32[]{:S(2)}) collective-permute-start(f32[128,128]{1,0:T(8,128)S(1)} %pad_maximum_fusion.5), channel_id=1, source_target_pairs={{0,16},{4,20},{8,24},{12,28},{16,0},{20,4},{24,8},{28,12},{1,17},{... | collective-permute-start | bytes 196616 | tf_op jit(solution)/shard_map/ppermute | solution.py:416
  98.4 4.7 %all-to-all-start = ((f32[32,16,512]{2,1,0:T(8,128)}), f32[32,16,512]{2,1,0:T(8,128)S(1)}, u32[]{:S(2)}, u32[]{:S(2)}) async-start(f32[32,16,512]{2,1,0:T(8,128)} %correlate.3.lags_ref), calls=%async_computation | async-start | bytes 2097152 | tf_op jit(solution)/shard_map/all_to_all | solution.py:493
  103.2 1.8 %collective-permute-start.17 = (f32[192,128]{1,0:T(8,128)S(1)}, f32[192,128]{1,0:T(8,128)S(1)}, u32[]{:S(2)}, u32[]{:S(2)}) collective-permute-start(f32[192,128]{1,0:T(8,128)S(1)} %pad_maximum_fusion.4), channel_id=1, source_target_pairs={{0,8},{4,12},{8,0},{12,4},{16,24},{20,28},{24,16},{28,20},{1,9},{5... | collective-permute-start | bytes 294920 | tf_op jit(solution)/shard_map/ppermute | solution.py:416
  105.0 9.1 %collective-permute-done.17 = f32[192,128]{1,0:T(8,128)S(1)} collective-permute-done((f32[192,128]{1,0:T(8,128)S(1)}, f32[192,128]{1,0:T(8,128)S(1)}, u32[]{:S(2)}, u32[]{:S(2)}) %collective-permute-start.17) | collective-permute-done | bytes 98336 | tf_op jit(solution)/shard_map/ppermute | solution.py:416
  116.5 1.9 %finish.1 = (f32[33,64]{1,0:T(8,128)}, f32[1,64]{1,0:T(1,128)}, f32[64,64]{1,0:T(8,128)}, f32[2,64]{1,0:T(2,128)}, f32[64,512]{1,0:T(8,128)}, /*index=5*/f32[1,512]{1,0:T(1,128)}) custom-call(f32[576,128]{1,0:T(8,128)} %pad_maximum_fusion.both_ref, f32[33,64]{1,0:T(8,128)} %bitcast.50, f32[1,64]{1,0:T(1,128)} %bitcast.53, f32[64,64]{1,0:T(8,128)} %hidden_ref.5, ...), custom_call_target="tpu_custom_call" | custom-call | tf_op jit(solution)/shard_map/finish/pallas_call | solution.py:453
  118.4 9.6 %all-to-all-done = f32[32,16,512]{2,1,0:T(8,128)S(1)} async-done(((f32[32,16,512]{2,1,0:T(8,128)}), f32[32,16,512]{2,1,0:T(8,128)S(1)}, u32[]{:S(2)}, u32[]{:S(2)}) %all-to-all-start) | async-done | bytes 1048608 | tf_op jit(solution)/shard_map/all_to_all | solution.py:493
  (81 shorter events, 8.7 us)
Async XLA Ops:
  3.2 11.4 %collective-permute-start.10 = (bf16[2,1,8,8192]{3,2,1,0:T(8,128)(2,1)}, bf16[2,1,8,8192]{3,2,1,0:T(8,128)(2,1)S(1)}, u32[]{:S(2)}, u32[]{:S(2)}) collective-permute-start(bf16[2,1,8,8192]{3,2,1,0:T(8,128)(2,1)} %get-tuple-element.45), channel_id=1, source_target_pairs={{0,24},{4,28},{8,16},{12,20},{16,8},{20,12},{24,0},{28,4},{1,25},{... | collective-permute-start | bytes 786440 | tf_op jit(solution)/shard_map/ppermute | solution.py:489
  7.2 7.4 %collective-permute-start.11 = (bf16[2,1,8,8192]{3,2,1,0:T(8,128)(2,1)}, bf16[2,1,8,8192]{3,2,1,0:T(8,128)(2,1)S(1)}, u32[]{:S(2)}, u32[]{:S(2)}) collective-permute-start(bf16[2,1,8,8192]{3,2,1,0:T(8,128)(2,1)} %get-tuple-element.46), channel_id=1, source_target_pairs={{0,4},{4,0},{8,12},{12,8},{16,20},{20,16},{24,28},{28,24},{1,5},{5... | collective-permute-start | bytes 786440 | tf_op jit(solution)/shard_map/ppermute | solution.py:489
  7.2 13.6 %collective-permute-start.12 = (bf16[2,1,8,8192]{3,2,1,0:T(8,128)(2,1)}, bf16[2,1,8,8192]{3,2,1,0:T(8,128)(2,1)S(1)}, u32[]{:S(2)}, u32[]{:S(2)}) collective-permute-start(bf16[2,1,8,8192]{3,2,1,0:T(8,128)(2,1)} %get-tuple-element.47), channel_id=1, source_target_pairs={{0,8},{4,12},{8,0},{12,4},{16,24},{20,28},{24,16},{28,20},{1,9},{5... | collective-permute-start | bytes 786440 | tf_op jit(solution)/shard_map/ppermute | solution.py:489
  7.8 13.0 %collective-permute-start.13 = (bf16[2,1,8,8192]{3,2,1,0:T(8,128)(2,1)}, bf16[2,1,8,8192]{3,2,1,0:T(8,128)(2,1)S(1)}, u32[]{:S(2)}, u32[]{:S(2)}) collective-permute-start(bf16[2,1,8,8192]{3,2,1,0:T(8,128)(2,1)} %get-tuple-element.48), channel_id=1, source_target_pairs={{0,16},{4,20},{8,24},{12,28},{16,0},{20,4},{24,8},{28,12},{1,17},{... | collective-permute-start | bytes 786440 | tf_op jit(solution)/shard_map/ppermute | solution.py:489
  7.9 30.1 %collective-permute-start.7 = (bf16[2,1,8,8192]{3,2,1,0:T(8,128)(2,1)}, bf16[2,1,8,8192]{3,2,1,0:T(8,128)(2,1)S(1)}, u32[]{:S(2)}, u32[]{:S(2)}) collective-permute-start(bf16[2,1,8,8192]{3,2,1,0:T(8,128)(2,1)} %get-tuple-element.42), channel_id=1, source_target_pairs={{0,28},{4,24},{8,20},{12,16},{16,12},{20,8},{24,4},{28,0},{1,29},{... | collective-permute-start | bytes 786440 | tf_op jit(solution)/shard_map/ppermute | solution.py:489
  14.6 28.8 %copy-start = (bf16[2,1,8,8192]{3,2,1,0:T(8,128)(2,1)}, bf16[2,1,8,8192]{3,2,1,0:T(8,128)(2,1)S(1)}, u32[]{:S(2)}) copy-start(bf16[2,1,8,8192]{3,2,1,0:T(8,128)(2,1)S(1)} %collective-permute-done.10.refs_3_) | copy-start | bytes 786436
  14.6 25.1 %collective-permute-start.8 = (bf16[2,1,8,8192]{3,2,1,0:T(8,128)(2,1)S(1)}, bf16[2,1,8,8192]{3,2,1,0:T(8,128)(2,1)S(1)}, u32[]{:S(2)}, u32[]{:S(2)}) collective-permute-start(bf16[2,1,8,8192]{3,2,1,0:T(8,128)(2,1)S(1)} %copy-done.8), channel_id=1, source_target_pairs={{0,12},{4,8},{8,4},{12,0},{16,28},{20,24},{24,20},{28,16},{1,13},{... | collective-permute-start | bytes 786440 | tf_op jit(solution)/shard_map/ppermute | solution.py:489
  14.7 28.8 %copy-start.1 = (bf16[2,1,8,8192]{3,2,1,0:T(8,128)(2,1)}, bf16[2,1,8,8192]{3,2,1,0:T(8,128)(2,1)S(1)}, u32[]{:S(2)}) copy-start(bf16[2,1,8,8192]{3,2,1,0:T(8,128)(2,1)S(1)} %collective-permute-done.11.refs_4_) | copy-start | bytes 786436
  14.7 26.5 %collective-permute-start.9 = (bf16[2,1,8,8192]{3,2,1,0:T(8,128)(2,1)S(1)}, bf16[2,1,8,8192]{3,2,1,0:T(8,128)(2,1)S(1)}, u32[]{:S(2)}, u32[]{:S(2)}) collective-permute-start(bf16[2,1,8,8192]{3,2,1,0:T(8,128)(2,1)S(1)} %copy-done.7), channel_id=1, source_target_pairs={{0,20},{4,16},{8,28},{12,24},{16,4},{20,0},{24,12},{28,8},{1,21},{... | collective-permute-start | bytes 786440 | tf_op jit(solution)/shard_map/ppermute | solution.py:489
  20.8 22.7 %copy-start.2 = (bf16[2,1,8,8192]{3,2,1,0:T(8,128)(2,1)}, bf16[2,1,8,8192]{3,2,1,0:T(8,128)(2,1)S(1)}, u32[]{:S(2)}) copy-start(bf16[2,1,8,8192]{3,2,1,0:T(8,128)(2,1)S(1)} %collective-permute-done.12.refs_5_) | copy-start | bytes 786436
  20.8 20.6 %collective-permute-start = (bf16[2,1,8,8192]{3,2,1,0:T(8,128)(2,1)}, bf16[2,1,8,8192]{3,2,1,0:T(8,128)(2,1)S(1)}, u32[]{:S(2)}, u32[]{:S(2)}) collective-permute-start(bf16[2,1,8,8192]{3,2,1,0:T(8,128)(2,1)} %get-tuple-element.34), channel_id=1, source_target_pairs={{0,28},{4,24},{8,20},{12,16},{16,12},{20,8},{24,4},{28,0},{1,29},{... | collective-permute-start | bytes 786440 | tf_op jit(solution)/shard_map/ppermute | solution.py:489
  20.8 22.7 %copy-start.3 = (bf16[2,1,8,8192]{3,2,1,0:T(8,128)(2,1)}, bf16[2,1,8,8192]{3,2,1,0:T(8,128)(2,1)S(1)}, u32[]{:S(2)}) copy-start(bf16[2,1,8,8192]{3,2,1,0:T(8,128)(2,1)S(1)} %collective-permute-done.13.refs_6_) | copy-start | bytes 786436
  20.8 21.0 %collective-permute-start.1 = (bf16[2,1,8,8192]{3,2,1,0:T(8,128)(2,1)}, bf16[2,1,8,8192]{3,2,1,0:T(8,128)(2,1)S(1)}, u32[]{:S(2)}, u32[]{:S(2)}) collective-permute-start(bf16[2,1,8,8192]{3,2,1,0:T(8,128)(2,1)} %get-tuple-element.35), channel_id=1, source_target_pairs={{0,12},{4,8},{8,4},{12,0},{16,28},{20,24},{24,20},{28,16},{1,13},{... | collective-permute-start | bytes 786440 | tf_op jit(solution)/shard_map/ppermute | solution.py:489
  38.1 19.0 %collective-permute-start.2 = (bf16[2,1,8,8192]{3,2,1,0:T(8,128)(2,1)}, bf16[2,1,8,8192]{3,2,1,0:T(8,128)(2,1)S(1)}, u32[]{:S(2)}, u32[]{:S(2)}) collective-permute-start(bf16[2,1,8,8192]{3,2,1,0:T(8,128)(2,1)} %get-tuple-element.36), channel_id=1, source_target_pairs={{0,20},{4,16},{8,28},{12,24},{16,4},{20,0},{24,12},{28,8},{1,21},{... | collective-permute-start | bytes 786440 | tf_op jit(solution)/shard_map/ppermute | solution.py:489
  39.7 17.4 %collective-permute-start.3 = (bf16[2,1,8,8192]{3,2,1,0:T(8,128)(2,1)}, bf16[2,1,8,8192]{3,2,1,0:T(8,128)(2,1)S(1)}, u32[]{:S(2)}, u32[]{:S(2)}) collective-permute-start(bf16[2,1,8,8192]{3,2,1,0:T(8,128)(2,1)} %get-tuple-element.37), channel_id=1, source_target_pairs={{0,24},{4,28},{8,16},{12,20},{16,8},{20,12},{24,0},{28,4},{1,25},{... | collective-permute-start | bytes 786440 | tf_op jit(solution)/shard_map/ppermute | solution.py:489
  41.1 16.0 %collective-permute-start.4 = (bf16[2,1,8,8192]{3,2,1,0:T(8,128)(2,1)}, bf16[2,1,8,8192]{3,2,1,0:T(8,128)(2,1)S(1)}, u32[]{:S(2)}, u32[]{:S(2)}) collective-permute-start(bf16[2,1,8,8192]{3,2,1,0:T(8,128)(2,1)} %get-tuple-element.38), channel_id=1, source_target_pairs={{0,4},{4,0},{8,12},{12,8},{16,20},{20,16},{24,28},{28,24},{1,5},{5... | collective-permute-start | bytes 786440 | tf_op jit(solution)/shard_map/ppermute | solution.py:489
  41.4 15.8 %collective-permute-start.5 = (bf16[2,1,8,8192]{3,2,1,0:T(8,128)(2,1)}, bf16[2,1,8,8192]{3,2,1,0:T(8,128)(2,1)S(1)}, u32[]{:S(2)}, u32[]{:S(2)}) collective-permute-start(bf16[2,1,8,8192]{3,2,1,0:T(8,128)(2,1)} %get-tuple-element.39), channel_id=1, source_target_pairs={{0,8},{4,12},{8,0},{12,4},{16,24},{20,28},{24,16},{28,20},{1,9},{5... | collective-permute-start | bytes 786440 | tf_op jit(solution)/shard_map/ppermute | solution.py:489
  41.8 16.5 %collective-permute-start.6 = (bf16[2,1,8,8192]{3,2,1,0:T(8,128)(2,1)}, bf16[2,1,8,8192]{3,2,1,0:T(8,128)(2,1)}, u32[]{:S(2)}, u32[]{:S(2)}) collective-permute-start(bf16[2,1,8,8192]{3,2,1,0:T(8,128)(2,1)} %get-tuple-element.40), channel_id=1, source_target_pairs={{0,16},{4,20},{8,24},{12,28},{16,0},{20,4},{24,8},{28,12},{1,17},{... | collective-permute-start | bytes 786440 | tf_op jit(solution)/shard_map/ppermute | solution.py:489
  85.1 5.7 %collective-permute-start.14 = (f32[80,128]{1,0:T(8,128)}, f32[80,128]{1,0:T(8,128)S(1)}, u32[]{:S(2)}, u32[]{:S(2)}) collective-permute-start(f32[80,128]{1,0:T(8,128)} %backward.1), channel_id=1, source_target_pairs={{0,2},{1,3},{2,0},{3,1},{4,6},{5,7},{6,4},{7,5},{8,10},{9,11},{10,... | collective-permute-start | bytes 122888 | tf_op jit(solution)/shard_map/ppermute | solution.py:416
  92.2 4.2 %collective-permute-start.15 = (f32[96,128]{1,0:T(8,128)S(1)}, f32[96,128]{1,0:T(8,128)S(1)}, u32[]{:S(2)}, u32[]{:S(2)}) collective-permute-start(f32[96,128]{1,0:T(8,128)S(1)} %pad_maximum_fusion.7), channel_id=1, source_target_pairs={{0,1},{1,0},{2,3},{3,2},{4,5},{5,4},{6,7},{7,6},{8,9},{9,8},{10,11... | collective-permute-start | bytes 147464 | tf_op jit(solution)/shard_map/ppermute | solution.py:416
  96.4 6.6 %collective-permute-start.16 = (f32[128,128]{1,0:T(8,128)S(1)}, f32[128,128]{1,0:T(8,128)S(1)}, u32[]{:S(2)}, u32[]{:S(2)}) collective-permute-start(f32[128,128]{1,0:T(8,128)S(1)} %pad_maximum_fusion.5), channel_id=1, source_target_pairs={{0,16},{4,20},{8,24},{12,28},{16,0},{20,4},{24,8},{28,12},{1,17},{... | collective-permute-start | bytes 196616 | tf_op jit(solution)/shard_map/ppermute | solution.py:416
  98.4 29.7 %all-to-all-start = ((f32[32,16,512]{2,1,0:T(8,128)}), f32[32,16,512]{2,1,0:T(8,128)S(1)}, u32[]{:S(2)}, u32[]{:S(2)}) async-start(f32[32,16,512]{2,1,0:T(8,128)} %correlate.3.lags_ref), calls=%async_computation | async-start | bytes 2097152 | tf_op jit(solution)/shard_map/all_to_all | solution.py:493
  103.2 11.0 %collective-permute-start.17 = (f32[192,128]{1,0:T(8,128)S(1)}, f32[192,128]{1,0:T(8,128)S(1)}, u32[]{:S(2)}, u32[]{:S(2)}) collective-permute-start(f32[192,128]{1,0:T(8,128)S(1)} %pad_maximum_fusion.4), channel_id=1, source_target_pairs={{0,8},{4,12},{8,0},{12,4},{16,24},{20,28},{24,16},{28,20},{1,9},{5... | collective-permute-start | bytes 294920 | tf_op jit(solution)/shard_map/ppermute | solution.py:416
  114.2 1.5 %collective-permute-start.18 = (f32[320,128]{1,0:T(8,128)S(1)}, f32[320,128]{1,0:T(8,128)S(1)}, u32[]{:S(2)}, u32[]{:S(2)}) collective-permute-start(f32[320,128]{1,0:T(8,128)S(1)} %pad_maximum_fusion.2), channel_id=1, source_target_pairs={{0,4},{4,0},{8,12},{12,8},{16,20},{20,16},{24,28},{28,24},{1,5},{5... | collective-permute-start | bytes 491528 | tf_op jit(solution)/shard_map/ppermute | solution.py:416
  (11 other events, 70.0 us)

commit v4 on v3

--- a/solution.py
+++ b/solution.py
@@ -91,7 +91,8 @@
     return jnp.sum(jnp.where(at[0] == at[1], row, 0.0), axis=1, keepdims=True)
 
 
-def pick_kernel(x_ref, g_ref, *refs, partners, own, start):
+def pick_kernel(x_ref, g_ref, *refs, partners, own, start, after):
+    refs = refs[after:]
     outs, (held_ref, in_sem, out_sem) = refs[: len(partners)], refs[len(partners) :]
     per = outs[0].shape[2]
     arrivals, departures = [], []
@@ -113,7 +114,7 @@
         departure.wait()
 
 
-def pick(x, g, partners, own, start, count):
+def pick(x, g, partners, own, start, count, after=()):
     seqs, _, length = x.shape
     shape = (2, seqs, count, length)
     if count % 8:
@@ -124,8 +125,10 @@
         ]
     anywhere = pl.BlockSpec(memory_space=pl.ANY)
     return pl.pallas_call(
-        functools.partial(pick_kernel, partners=partners, own=own, start=start),
-        in_specs=[anywhere, anywhere],
+        functools.partial(
+            pick_kernel, partners=partners, own=own, start=start, after=len(after)
+        ),
+        in_specs=[anywhere] * (2 + len(after)),
         out_specs=[anywhere] * len(partners),
         out_shape=[jax.ShapeDtypeStruct(shape, BF16)] * len(partners),
         scratch_shapes=[
@@ -137,22 +140,25 @@
             flops=0, bytes_accessed=4 * len(partners) * math.prod(shape), transcendentals=0
         ),
         name="pick",
-    )(x, g)
-
-
-def correlate_kernel(*refs, pieces, held):
-    piece_refs = refs[:pieces]
-    refs = refs[:pieces] + refs[pieces + held :]
-    (
-        first_ref, twist_ref, untwist_ref, second_ref, back_ref, last_ref,
-        out_ref, turn_ref, high_ref, low_ref, spec_ref, lag_ref,
-    ) = refs[pieces:]
+    )(x, g, *after)
+
+
+def correlate_kernel(*refs, pieces, held, last):
+    piece_refs, refs = refs[:pieces], refs[pieces:]
+    held_ref, refs = (refs[0], refs[1:]) if held else (None, refs)
+    first_ref, twist_ref, second_ref = refs[:3]
+    if last:
+        untwist_ref, back_ref, last_ref, out_ref, lag_ref, cross_ref = refs[3:9]
+    else:
+        out_ref = refs[3]
+    turn_ref, high_ref, low_ref, spec_ref = refs[-4:]
     _, seqs_each, channels, length = piece_refs[0].shape
     rows = length // LANES
     seqs = pieces * seqs_each
-    c = pl.program_id(0)
-
-    @pl.when(c == 0)
+    step = pl.program_id(0)
+    each = high_ref.shape[0] // (2 * seqs * rows)
+
+    @pl.when(step == 0)
     def _():
         for s in range(seqs):
             for at in range(2):
@@ -161,83 +167,134 @@
                         s // seqs_each
                     ][at, s % seqs_each, :, pl.ds(row * LANES, LANES)].astype(F32)
 
-    def samples(at, s):
-        return turn_ref[at * seqs + s, pl.ds(c, rows, stride=channels), :].astype(BF16)
-
     cosine = jnp.concatenate([twist_ref[0]] * 2, axis=1)
     sine = jnp.concatenate([twist_ref[1]] * 2, axis=1)
     first = first_ref[...]
-    for s in range(seqs):
-        pair = jnp.concatenate([samples(0, s), samples(1, s)], axis=1)
-        both = dot(first, jnp.concatenate([pair, pair], axis=0))
-        real, imag = both[:rows], both[rows:]
-        real, imag = real * cosine - imag * sine, real * sine + imag * cosine
-        for at, part in ((0, slice(0, LANES)), (1, slice(LANES, 2 * LANES))):
-            line = pl.ds((at * seqs + s) * rows, rows)
-            row = jnp.concatenate([real[:, part], imag[:, part]], axis=1)
-            high_ref[line, :], low_ref[line, :] = split(row)
+
+    def line(at, s, k):
+        return pl.ds(((k * 2 + at) * seqs + s) * rows, rows)
+
+    for k in range(each):
+        for s in range(seqs):
+            pair = jnp.concatenate(
+                [
+                    turn_ref[
+                        at * seqs + s, pl.ds(step * each + k, rows, stride=channels), :
+                    ].astype(BF16)
+                    for at in range(2)
+                ],
+                axis=1,
+            )
+            both = dot(first, jnp.concatenate([pair, pair], axis=0))
+            real, imag = both[:rows], both[rows:]
+            real, imag = real * cosine - imag * sine, real * sine + imag * cosine
+            for at, part in ((0, slice(0, LANES)), (1, slice(LANES, 2 * LANES))):
+                row = jnp.concatenate([real[:, part], imag[:, part]], axis=1)
+                high_ref[line(at, s, k), :], low_ref[line(at, s, k), :] = split(row)
     spec_ref[...] = dot(
         jnp.concatenate([high_ref[...], low_ref[...], high_ref[...]], axis=1), second_ref[...]
     )
-    real = jnp.zeros((rows, LANES), F32)
-    imag = jnp.zeros((rows, LANES), F32)
-    for s in range(seqs):
-        a = spec_ref[pl.ds(s * rows, rows), :]
-        b = spec_ref[pl.ds((seqs + s) * rows, rows), :]
-        a_real, a_imag, b_real, b_imag = a[:, :LANES], a[:, LANES:], b[:, :LANES], b[:, LANES:]
-        real = real + (a_real * b_real + a_imag * b_imag)
-        imag = imag + (a_real * b_imag - a_imag * b_real)
-    high, low = split(jnp.concatenate([real, imag], axis=1))
-    back = dot(jnp.concatenate([high, low, high], axis=1), back_ref[...])
-    real, imag = back[:, :LANES], back[:, LANES:]
-    cosine, sine = untwist_ref[0], untwist_ref[1]
-    turned = jnp.concatenate([real * cosine - imag * sine, real * sine + imag * cosine], axis=0)
-    high, low = split(turned)
-    lag_ref[pl.ds(pl.multiple_of(c * 2 * rows, 2 * rows), 2 * rows), :] = dot(
-        last_ref[...], jnp.concatenate([high, high, low], axis=0)
-    )
-
-    @pl.when(c == pl.num_programs(0) - 1)
+    for k in range(each):
+        if held:
+            real, imag = held_ref[k, :, :LANES], held_ref[k, :, LANES:]
+        else:
+            real = imag = jnp.zeros((rows, LANES), F32)
+        for s in range(seqs):
+            a, b = spec_ref[line(0, s, k), :], spec_ref[line(1, s, k), :]
+            a_real, a_imag, b_real, b_imag = a[:, :LANES], a[:, LANES:], b[:, :LANES], b[:, LANES:]
+            real = real + (a_real * b_real + a_imag * b_imag)
+            imag = imag + (a_real * b_imag - a_imag * b_real)
+        if last:
+            cross_line = pl.ds(pl.multiple_of((step * each + k) * rows, rows), rows)
+            cross_ref[cross_line, :LANES] = real
+            cross_ref[cross_line, LANES:] = imag
+        else:
+            out_ref[k, :, :LANES] = real
+            out_ref[k, :, LANES:] = imag
+    if not last:
+        return
+
+    @pl.when(step == pl.num_programs(0) - 1)
     def _():
         owners, channels, lag_count = out_ref.shape
-        each = lag_count // LANES
+        back_cos, back_sin = untwist_ref[0], untwist_ref[1]
+        group = math.gcd(channels, 4)
+        for start in range(0, channels, group):
+            high, low = split(cross_ref[pl.ds(start * rows, group * rows), :])
+            back = dot(jnp.concatenate([high, low, high], axis=1), back_ref[...])
+            for c in range(0, group, 2):
+                turned = []
+                for k in range(c, c + 2):
+                    real = back[k * rows : (k + 1) * rows, :LANES]
+                    imag = back[k * rows : (k + 1) * rows, LANES:]
+                    turned.append(
+                        jnp.concatenate(
+                            [real * back_cos - imag * back_sin, real * back_sin + imag * back_cos],
+                            axis=0,
+                        )
+                    )
+                lags = dot(last_ref[...], wide(jnp.concatenate(turned, axis=1), 0))
+                for k in range(2):
+                    lag_ref[pl.ds((start + c + k) * 2 * rows, 2 * rows), :] = lags[
+                        :, k * LANES : (k + 1) * LANES
+                    ]
+        wide_rows = lag_count // LANES
         for owner in range(owners):
-            for k in range(each):
+            for k in range(wide_rows):
                 out_ref[owner, :, pl.ds(k * LANES, LANES)] = lag_ref[
-                    pl.ds(owner * each + k, channels, stride=2 * rows), :
+                    pl.ds(owner * wide_rows + k, channels, stride=2 * rows), :
                 ]
 
 
-def correlate(pieces, scale, owners, held, chunk, chunks):
+def correlate(pieces, held, scale, owners):
     _, seqs_each, channels, length = pieces[0].shape
     lanes, rows = LANES, length // LANES
     seqs = seqs_each * len(pieces)
-    total = 2 * rows * lanes
-    consts = [jnp.asarray(t) for t in tables(rows, 2.0 * scale / total)]
+    total = 2 * length
+    each = max(1, min(channels, 8 // seqs))
+    first, twist, untwist, second, back, last = (
+        jnp.asarray(t) for t in tables(rows, 2.0 * scale / total)
+    )
+    consts = [first, twist, second] + ([untwist, back, last] if owners else [])
+    spectrum = pl.BlockSpec((each, rows, 2 * lanes), lambda c: (c, 0, 0))
+    held = [] if held is None else [held]
     block = pl.BlockSpec(pieces[0].shape, lambda c: (0, 0, 0, 0))
     whole = [
         pl.BlockSpec(t.shape, functools.partial(lambda n, c: (0,) * n, t.ndim)) for t in consts
     ]
-    held = [] if held is None else [held]
+    if owners:
+        shape = (owners, channels, total // owners)
+        out_spec = pl.BlockSpec(shape, lambda c: (0, 0, 0))
+    else:
+        shape = (channels, rows, 2 * lanes)
+        out_spec = spectrum
+    scratch = []
+    if owners:
+        scratch = [
+            pltpu.VMEM((channels * 2 * rows, lanes), F32),
+            pltpu.VMEM((channels * rows, 2 * lanes), F32),
+        ]
+    scratch += [
+        pltpu.VMEM((2 * seqs, rows * channels, lanes), F32),
+        pltpu.VMEM((each * 2 * seqs * rows, 2 * lanes), BF16),
+        pltpu.VMEM((each * 2 * seqs * rows, 2 * lanes), BF16),
+        pltpu.VMEM((each * 2 * seqs * rows, 2 * lanes), F32),
+    ]
     return pl.pallas_call(
-        functools.partial(correlate_kernel, pieces=len(pieces), held=len(held)),
-        grid=(channels,),
-        in_specs=[block] * len(pieces) + [pl.BlockSpec(memory_space=pl.ANY)] * len(held) + whole,
-        out_specs=pl.BlockSpec((owners, channels, total // owners), lambda c: (0, chunk, 0)),
-        out_shape=jax.ShapeDtypeStruct((owners, channels * chunks, total // owners), F32),
-        input_output_aliases={len(pieces): 0} if held else {},
-        scratch_shapes=[
-            pltpu.VMEM((2 * seqs, rows * channels, lanes), F32),
-            pltpu.VMEM((2 * seqs * rows, 2 * lanes), BF16),
-            pltpu.VMEM((2 * seqs * rows, 2 * lanes), BF16),
-            pltpu.VMEM((2 * seqs * rows, 2 * lanes), F32),
-            pltpu.VMEM((channels * 2 * rows, lanes), F32),
-        ],
+        functools.partial(
+            correlate_kernel, pieces=len(pieces), held=len(held), last=bool(owners)
+        ),
+        grid=(channels // each,),
+        in_specs=[block] * len(pieces) + [spectrum] * len(held) + whole,
+        out_specs=out_spec,
+        out_shape=jax.ShapeDtypeStruct(shape, F32),
+        scratch_shapes=scratch,
         cost_estimate=pl.CostEstimate(
             flops=channels * seqs * 2 * rows * lanes * lanes * 36,
             bytes_accessed=channels * (seqs * rows * lanes * 4 + total * 4),
             transcendentals=0,
         ),
+        compiler_params=pltpu.CompilerParams(vmem_limit_bytes=24 * 2**20),
         name="correlate",
     )(*pieces, *held, *consts)
 
@@ -323,7 +380,7 @@
 def backward_kernel(
     first_ref, lags_ref, table_ref, layer1_ref, layer2_ref, cos1_ref, cos2_ref,
     decay_ref, output_ref, hidden_ref, freq_ref,
-    out_ref, output_parts, hidden_parts, decay_col, own_ref, sum1_ref, sum3_ref, sum5_ref, *, total,
+    out_ref, output_parts, hidden_parts, decay_col, own_ref, sum1_ref, sum3_ref, sum5_ref, *, total, pack,
 ):
     step = pl.program_id(0)
     owners, own, _ = lags_ref.shape
@@ -367,25 +424,43 @@
         )
         sums = joined(sum1_ref)
         decay_grad = -jnp.sum(own_ref[...].T * sums[own:], axis=1, keepdims=True)
-        out_ref[hidden:] = jnp.concatenate(
-            [sums[:own], decay_grad, jnp.zeros((own, LANES - hidden - 1), F32)], axis=1
-        )
+        height = out_ref.shape[0] - hidden - own // pack
+        place = lax.broadcasted_iota(jnp.int32, (height, LANES), 0) * LANES
+        place = place + lax.broadcasted_iota(jnp.int32, (height, LANES), 1) - first_ref[0]
+        decays = jnp.zeros((height, LANES), F32)
+        for c in range(own):
+            decays = jnp.where(place == c, decay_grad[c : c + 1], decays)
+        out_ref[pl.ds(hidden, height), :] = decays
+        per = own // pack
+        parts = [sums[k * per : (k + 1) * per] for k in range(pack)]
+        parts += [jnp.zeros((per, LANES - pack * hidden), F32)] if pack * hidden < LANES else []
+        out_ref[hidden + height :] = jnp.concatenate(parts, axis=1)
+
+
+def packing(own, hidden):
+    return 2 if own % 16 == 0 and 2 * hidden <= LANES else 1
+
+
+def summed_rows(hidden, channels):
+    return hidden + -(-channels // (8 * LANES)) * 8
 
 
 def backward(first_own, lags, saved, decay_rate, output_weight, hidden_weight, frequency, total):
     _, own, lag_count = lags.shape
     hidden = hidden_weight.shape[0]
+    pack = packing(own, hidden)
+    height = summed_rows(hidden, decay_rate.shape[0]) + own // pack
     args = (decay_rate[None], output_weight.T, hidden_weight, frequency)
     specs = [pl.BlockSpec((STEP // lag_count, own, lag_count), lambda i, first: (i, 0, 0))]
     specs += [pl.BlockSpec((a.shape[0], STEP), lambda i, first: (0, i)) for a in saved]
     specs += [pl.BlockSpec(a.shape, lambda i, first: (0, 0)) for a in args]
     return pl.pallas_call(
-        functools.partial(backward_kernel, total=total),
+        functools.partial(backward_kernel, total=total, pack=pack),
         grid_spec=pltpu.PrefetchScalarGridSpec(
             num_scalar_prefetch=1,
             grid=(total // STEP,),
             in_specs=specs,
-            out_specs=pl.BlockSpec((hidden + own, LANES), lambda i, first: (0, 0)),
+            out_specs=pl.BlockSpec((height, LANES), lambda i, first: (0, 0)),
             scratch_shapes=[
                 pltpu.VMEM((hidden, 3 * own), BF16),
                 pltpu.VMEM((hidden, 3 * hidden), BF16),
@@ -396,7 +471,7 @@
                 pltpu.VMEM((2 * hidden, saved[0].shape[0]), F32),
             ],
         ),
-        out_shape=jax.ShapeDtypeStruct((hidden + own, LANES), F32),
+        out_shape=jax.ShapeDtypeStruct((height, LANES), F32),
         cost_estimate=pl.CostEstimate(
             flops=total * hidden * 2000, bytes_accessed=total * hidden * 20, transcendentals=0
         ),
@@ -404,37 +479,46 @@
     )(first_own.reshape(1), lags, *saved, *args)
 
 
-def share(both, hidden):
-    own = both.shape[0] - hidden
-    count = 1
-    for axis in ("chan", "dp"):
+def rounds():
+    sizes = ((axis, lax.axis_size(axis)) for axis in ("dp", "chan"))
+    return [(axis, 1 << b) for axis, size in sizes for b in reversed(range(size.bit_length() - 1))]
+
+
+def share(both, summed):
+    for axis, bit in rounds():
         size = lax.axis_size(axis)
-        place = lax.axis_index(axis)
-        lead = count
-        bit = size // 2
-        while bit:
-            got = lax.ppermute(both, axis, [(i, i ^ bit) for i in range(size)])
-            mine, theirs = (v[hidden:].reshape(lead, -1, own, LANES) for v in (both, got))
-            upper = (place & bit) != 0
-            rows = jnp.stack(
-                [jnp.where(upper, theirs, mine), jnp.where(upper, mine, theirs)], axis=2
-            )
-            both = jnp.concatenate([both[:hidden] + got[:hidden], rows.reshape(-1, LANES)], axis=0)
-            count *= 2
-            bit //= 2
-    return both
+        got = lax.ppermute(both, axis, [(i, i ^ bit) for i in range(size)])
+        last = both, got
+        both = jnp.concatenate([both[:summed] + got[:summed], both[summed:], got[summed:]], axis=0)
+    return last
 
 
 def finish_kernel(
-    both_ref, embed_ref, bias_ref, hidden_ref, freq_ref,
-    embed_grad, bias_grad, hidden_grad, frequency_grad, output_grad, decay_grad,
+    both_ref, got_ref, embed_ref, bias_ref, hidden_ref, freq_ref,
+    embed_grad, bias_grad, hidden_grad, frequency_grad, output_grad, decay_grad, rows_ref, *, own, pack,
 ):
     hidden, features = hidden_ref.shape[0], embed_ref.shape[0]
-    net = both_ref[:hidden]
+    summed = summed_rows(hidden, output_grad.shape[1])
+    total = both_ref[:summed] + got_ref[:summed]
+    net = total[:hidden]
     turned = net.T
-    rows = both_ref[hidden:].T
-    output_grad[...] = rows[:hidden]
-    decay_grad[...] = rows[hidden : hidden + 1]
+    decay_grad[...] = total[hidden : hidden + decay_grad.shape[0]]
+    unit = own // pack
+    count = output_grad.shape[1] // own
+    here = {axis: lax.axis_index(axis) for axis in ("dp", "chan")}
+    steps = rounds()
+    for k in range(count):
+        there = dict(here)
+        for n, (axis, bit) in enumerate(steps):
+            if k >> n & 1:
+                there[axis] = there[axis] ^ bit
+        place = there["chan"] * lax.axis_size("dp") + there["dp"]
+        ref, at = (both_ref, k) if k < count // 2 else (got_ref, k - count // 2)
+        for n in range(pack):
+            rows_ref[pl.ds(pl.multiple_of(place * own + n * unit, unit), unit), :] = ref[
+                pl.ds(summed + at * unit, unit), n * hidden : (n + 1) * hidden
+            ]
+    output_grad[...] = rows_ref[...].T
     table = turned[hidden:]
     embed = jnp.concatenate([table[features - 1 : features], table[: features - 1]], axis=0)
     bias = table[features : features + 1]
@@ -447,15 +531,20 @@
     frequency_grad[1:2] = jnp.sum(hidden_ref[...].T * turned[:hidden], axis=0, keepdims=True)
 
 
-def finish(both, embed_weight, embed_bias, hidden_weight, frequency, channels):
+def finish(both, got, embed_weight, embed_bias, hidden_weight, frequency, channels, own):
     hidden, features = embed_weight.shape
-    shapes = ((features, hidden), (1, hidden), (hidden, hidden), (2, hidden), (hidden, channels), (1, channels))
+    shapes = (
+        (features, hidden), (1, hidden), (hidden, hidden), (2, hidden), (hidden, channels),
+        (-(-channels // LANES), LANES),
+    )
     embed, bias, hid, freq, output, decay = pl.pallas_call(
-        finish_kernel,
+        functools.partial(finish_kernel, own=own, pack=packing(own, hidden)),
         out_shape=[jax.ShapeDtypeStruct(shape, F32) for shape in shapes],
+        scratch_shapes=[pltpu.VMEM((channels, hidden), F32)],
+        compiler_params=pltpu.CompilerParams(vmem_limit_bytes=8 * 2**20),
         name="finish",
-    )(both, embed_weight.T, embed_bias[None], hidden_weight, frequency)
-    return embed.T, bias[0], hid, freq, output.T, decay[0]
+    )(both, got, embed_weight.T, embed_bias[None], hidden_weight, frequency)
+    return embed.T, bias[0], hid, freq, output.T, decay.reshape(-1)[:channels]
 
 
 def work(
@@ -478,16 +567,22 @@
     scale = 1.0 / math.sqrt(seq_local * dp * length)
     at_dp, at_chan = lax.axis_index("dp"), lax.axis_index("chan")
 
-    chunks = 2 if own % 16 == 0 else 1
-    per = own // chunks
-    partners = sorted(range(1, dp), key=lambda p: -bin(p).count("1"))
-    lags = None
-    for q in range(chunks):
-        sent = pick(signal, signal_grad, (*partners, 0), own, q * per, per)
-        pieces = []
-        for k, p in enumerate(partners):
-            pieces.append(lax.ppermute(sent[k], "dp", [(i, i ^ p) for i in range(dp)]))
-        lags = correlate([*pieces, sent[-1]], scale, count, lags, q, chunks)
+    partners = sorted(
+        range(1, dp), key=lambda p: (p != 1, -bin(p >> 1).count("1"), p & 1, p)
+    )
+    pieces = [None] * dp
+    made = []
+    for some in (tuple(partners[1:3]), (partners[0], *partners[3:], 0)):
+        made = pick(signal, signal_grad, some, own, 0, own, made[:1])
+        for p, sent in zip(some, made):
+            pieces[p] = lax.ppermute(sent, "dp", [(i, i ^ p) for i in range(dp)]) if p else sent
+    order = [0, *partners]
+    spectrum = None
+    cuts = (*range(0, dp, max(2, dp // 4)), dp)
+    for q in range(len(cuts) - 1):
+        some = [pieces[p] for p in order[cuts[q] : cuts[q + 1]]]
+        spectrum = correlate(some, spectrum, scale, count if q == len(cuts) - 2 else 0)
+    lags = spectrum
 
     saved = network(embed_weight, embed_bias, hidden_weight, frequency, total)
     shared = lax.all_to_all(lags, ("dp", "chan"), 0, 0, tiled=True)
@@ -495,11 +590,12 @@
     both = backward(
         first_own, lags, saved, decay_rate, output_weight, hidden_weight, frequency, total
     )
-    both = share(both, hidden)
-    filter_grad = jnp.swapaxes(shared.reshape(dp, chan, own, -1), 0, 1).reshape(channels, -1)
+    both, got = share(both, summed_rows(hidden, channels))
+    filter_grad = jnp.swapaxes(shared.reshape(dp, chan, own, -1), 0, 1)
+    filter_grad = filter_grad.reshape(channels, -1)
     return (
         filter_grad,
-        *finish(both, embed_weight, embed_bias, hidden_weight, frequency, channels),
+        *finish(both, got, embed_weight, embed_bias, hidden_weight, frequency, channels, own),
     )
 
 

time: 131 us -> 130 us (level)
  waiting for transfers between devices: 31.1 us -> 47.8 us
  starting transfers between devices: 30 us -> 20.3 us
  Pallas kernels: 63.4 us -> 55 us
  local copies, waits for them, and re-layouts: 1.16 us -> 4.27 us
  other arithmetic: 2.38 us -> 0.81 us
    ppermute x5, waiting for transfers between devices: 15.8 us -> 34.6 us  [share(): got = lax.ppermute(both, axis, [(i, i ^ bit) for i in range(size)])]
    all_to_all x1, waiting for transfers between devices: 9.6 us -> 0.01 us  [work(): shared = lax.all_to_all(lags, ('dp', 'chan'), 0, 0, tiled=True)]
    ppermute x14 -> x7, starting transfers between devices: 16.9 us -> 7.93 us  [work(): lax.ppermute(sent, 'dp', [(i, i ^ p) for i in range(dp)])]
    pallas_call x2 -> x4, Pallas kernels: 27.2 us -> 19.5 us  [correlate(): pl.pallas_call(functools.partial(correlate_kernel, pieces=len(pieces), he...]
    ppermute x14 -> x7, waiting for transfers between devices: 5.79 us -> 13.2 us  [work(): lax.ppermute(sent, 'dp', [(i, i ^ p) for i in range(dp)])]
    unnamed x30 -> x29, local copies, waits for them, and re-layouts: 0.06 us -> 2.49 us
    ppermute x5, starting transfers between devices: 8.42 us -> 6.27 us  [share(): got = lax.ppermute(both, axis, [(i, i ^ bit) for i in range(size)])]
    all_to_all x1, starting transfers between devices: 4.72 us -> 6.14 us  [work(): shared = lax.all_to_all(lags, ('dp', 'chan'), 0, 0, tiled=True)]
  transfers between devices with their start and end apart: 20 -> 13, of which waited for: 8 -> 7; matrix products, arithmetic and copies ran while one was open for 1% -> 2% of each run, Pallas kernels for 26% -> 23%
where the time goes in v4:
time: 130 us; the launch traced here: 129 us
  Pallas kernels  55 us (42%)
  waiting for transfers between devices  47.8 us (37%)
  starting transfers between devices  20.3 us (16%)
  local copies, waits for them, and re-layouts  4.27 us (3%)
    ppermute x5, waiting for transfers between devices, share(): got = lax.ppermute(both, axis, [(i, i ^ bit) for i in range(size)])  34.6 us
    pallas_call x4, Pallas kernels, correlate(): pl.pallas_call(functools.partial(correlate_kernel, pieces=len(pieces), he...  19.5 us
    pallas_call x1, Pallas kernels, network(): pl.pallas_call(functools.partial(network_kernel, total=total), grid=(tota...  16.1 us
    pallas_call x1, Pallas kernels, backward(): pl.pallas_call(functools.partial(backward_kernel, total=total, pack=pack)...  13.6 us
    ppermute x7, waiting for transfers between devices, work(): lax.ppermute(sent, 'dp', [(i, i ^ p) for i in range(dp)])  13.2 us
    ppermute x7, starting transfers between devices, work(): lax.ppermute(sent, 'dp', [(i, i ^ p) for i in range(dp)])  7.93 us
    ppermute x5, starting transfers between devices, share(): got = lax.ppermute(both, axis, [(i, i ^ bit) for i in range(size)])  6.27 us
    all_to_all x1, starting transfers between devices, work(): shared = lax.all_to_all(lags, ('dp', 'chan'), 0, 0, tiled=True)  6.14 us
  transfers between devices with their start and end apart: 13, of which 7 were waited for; matrix products, arithmetic and copies ran while one was open for 2% of the time, Pallas kernels for 23%

profile of v4, /device:TPU:0, one launch (start us, length us, event | category | flops | bytes accessed | tf_op | source)
XLA Modules:
  0.0 129.1 jit_solution(1189877683665148095)
XLA Ops:
  0.6 2.1 %pick.2 = (bf16[2,1,16,8192]{3,2,1,0:T(8,128)(2,1)}, bf16[2,1,16,8192]{3,2,1,0:T(8,128)(2,1)}) custom-call(bf16[1,128,8192]{2,1,0:T(8,128)(2,1)} %x_ref.3, bf16[1,128,8192]{2,1,0:T(8,128)(2,1)} %g_ref.3), custom_call_target="tpu_custom_call" | custom-call | bytes 2097152 | tf_op jit(solution)/shard_map/pick/pallas_call | solution.py:127
  2.7 2.9 %pick.3 = (bf16[2,1,16,8192]{3,2,1,0:T(8,128)(2,1)}, bf16[2,1,16,8192]{3,2,1,0:T(8,128)(2,1)}, bf16[2,1,16,8192]{3,2,1,0:T(8,128)(2,1)}, bf16[2,1,16,8192]{3,2,1...) custom-call(bf16[1,128,8192]{2,1,0:T(8,128)(2,1)} %x_ref.3, ...), custom_call_target="tpu_custom_call" | custom-call | bytes 6291456 | tf_op jit(solution)/shard_map/pick/pallas_call | solution.py:127
  6.2 3.5 %collective-permute-start.4 = (bf16[2,1,16,8192]{3,2,1,0:T(8,128)(2,1)}, bf16[2,1,16,8192]{3,2,1,0:T(8,128)(2,1)S(1)}, u32[]{:S(2)}, u32[]{:S(2)}) collective-permute-start(bf16[2,1,16,8192]{3,2,1,0:T(8,128)(2,1)} %get-tuple-element.26.refs_0_), channel_id=1, source_target_pairs={{0,24},{4,28},{8,16},{12,20},{16,8},{20,12},{24,0},{28,4},{1,25},{... | collective-permute-start | bytes 1572872 | tf_op jit(solution)/shard_map/ppermute | solution.py:578
  9.8 1.7 %collective-permute-start.2 = (bf16[2,1,16,8192]{3,2,1,0:T(8,128)(2,1)}, bf16[2,1,16,8192]{3,2,1,0:T(8,128)(2,1)S(1)}, u32[]{:S(2)}, u32[]{:S(2)}) collective-permute-start(bf16[2,1,16,8192]{3,2,1,0:T(8,128)(2,1)} %get-tuple-element.29), channel_id=1, source_target_pairs={{0,8},{4,12},{8,0},{12,4},{16,24},{20,28},{24,16},{28,20},{1,9},{5... | collective-permute-start | bytes 1572872 | tf_op jit(solution)/shard_map/ppermute | solution.py:578
  11.5 1.5 %collective-permute-start.3 = (bf16[2,1,16,8192]{3,2,1,0:T(8,128)(2,1)}, bf16[2,1,16,8192]{3,2,1,0:T(8,128)(2,1)S(1)}, u32[]{:S(2)}, u32[]{:S(2)}) collective-permute-start(bf16[2,1,16,8192]{3,2,1,0:T(8,128)(2,1)} %get-tuple-element.30), channel_id=1, source_target_pairs={{0,16},{4,20},{8,24},{12,28},{16,0},{20,4},{24,8},{28,12},{1,17},{... | collective-permute-start | bytes 1572872 | tf_op jit(solution)/shard_map/ppermute | solution.py:578
  13.0 16.1 %network.1 = (bf16[80,16384]{1,0:T(8,128)(2,1)}, bf16[128,16384]{1,0:T(8,128)(2,1)}, bf16[128,16384]{1,0:T(8,128)(2,1)}, f32[64,16384]{1,0:T(8,128)}, f32[64,16384]{1,0:T(8,128)}) custom-call(s32[16,1]{1,0:T(8,128)} %constant.33.clone.factor_ref, f32[33,64]{1,0:T(8,128)} %bitcast.13, f32[1,64]{1,0:T(1,128)} %bitcast.15, f32[64,64]{1,0:T(8,128)} %hidden_ref.5, ...), custom_call_target="tpu_custom_call" | custom-call | flops 629145600 | bytes 20971520 | tf_op jit(solution)/shard_map/network/pallas_call | solution.py:362
  29.7 1.0 copy-done.4
  30.7 4.0 %correlate.4.refs_2_ = f32[16,64,256]{2,1,0:T(8,128)S(1)} custom-call(bf16[2,1,16,8192]{3,2,1,0:T(8,128)(2,1)S(1)} %copy-done.4, bf16[2,1,16,8192]{3,2,1,0:T(8,128)(2,1)S(1)} %collective-permute-done.6.refs_1_, bf16[128,128]{1,0:T(8,128)(2,1)S(1)} %copy-done.10, f32[2,64,128]{2,1,0:T(8,128)S(1)} %copy-done.8, bf16[768,256]{1,0:T(8,128)(2,1)S(1)} %copy-done.5), custom_call_target="tpu_custom_call" | custom-call | flops 2415919104 | bytes 2097152 | tf_op jit(solution)/shard_map/correlate/pallas_call | solution.py:283
  34.8 4.0 %correlate.5.refs_2_ = f32[16,64,256]{2,1,0:T(8,128)S(1)} custom-call(bf16[2,1,16,8192]{3,2,1,0:T(8,128)(2,1)S(1)} %collective-permute-done.4.refs_0_, bf16[2,1,16,8192]{3,2,1,0:T(8,128)(2,1)S(1)} %collective-permute-done.5.refs_1_, f32[16,64,256]{2,1,0:T(8,128)S(1)} %correlate.4.refs_2_, bf16[128,128]{1,0:T(8,128)(2,1)S(1)} %copy-done.10, ...), custom_call_target="tpu_custom_call" | custom-call | flops 2415919104 | bytes 2097152 | tf_op jit(solution)/shard_map/correlate/pallas_call | solution.py:283
  38.9 6.9 %collective-permute-done.2.refs_0_ = bf16[2,1,16,8192]{3,2,1,0:T(8,128)(2,1)S(1)} collective-permute-done((bf16[2,1,16,8192]{3,2,1,0:T(8,128)(2,1)}, bf16[2,1,16,8192]{3,2,1,0:T(8,128)(2,1)S(1)}, u32[]{:S(2)}, u32[]{:S(2)}) %collective-permute-start.2) | collective-permute-done | bytes 524320 | tf_op jit(solution)/shard_map/ppermute | solution.py:578
  45.8 4.0 %correlate.6.refs_2_ = f32[16,64,256]{2,1,0:T(8,128)S(1)} custom-call(bf16[2,1,16,8192]{3,2,1,0:T(8,128)(2,1)S(1)} %collective-permute-done.2.refs_0_, bf16[2,1,16,8192]{3,2,1,0:T(8,128)(2,1)S(1)} %collective-permute-done.3.refs_1_, f32[16,64,256]{2,1,0:T(8,128)S(1)} %correlate.5.refs_2_, bf16[128,128]{1,0:T(8,128)(2,1)S(1)} %copy-done.10, ...), custom_call_target="tpu_custom_call" | custom-call | flops 2415919104 | bytes 2097152 | tf_op jit(solution)/shard_map/correlate/pallas_call | solution.py:283
  49.8 6.1 %collective-permute-done.refs_0_ = bf16[2,1,16,8192]{3,2,1,0:T(8,128)(2,1)S(1)} collective-permute-done((bf16[2,1,16,8192]{3,2,1,0:T(8,128)(2,1)}, bf16[2,1,16,8192]{3,2,1,0:T(8,128)(2,1)S(1)}, u32[]{:S(2)}, u32[]{:S(2)}) %collective-permute-start) | collective-permute-done | bytes 524320 | tf_op jit(solution)/shard_map/ppermute | solution.py:578
  56.1 7.4 %correlate.7.lags_ref = f32[32,16,512]{2,1,0:T(8,128)} custom-call(bf16[2,1,16,8192]{3,2,1,0:T(8,128)(2,1)S(1)} %collective-permute-done.refs_0_, bf16[2,1,16,8192]{3,2,1,0:T(8,128)(2,1)S(1)} %collective-permute-done.1.refs_1_, f32[16,64,256]{2,1,0:T(8,128)S(1)} %correlate.6.refs_2_, bf16[128,128]{1,0:T(8,128)(2,1)S(1)} %copy-done.10, ...), custom_call_target="tpu_custom_call" | custom-call | flops 2415919104 | bytes 2097152 | tf_op jit(solution)/shard_map/correlate/pallas_call | solution.py:283
  63.5 13.6 %backward.1 = f32[80,128]{1,0:T(8,128)} custom-call(s32[1]{0:T(128)} %bitcast.3.first_ref, f32[32,16,512]{2,1,0:T(8,128)} %correlate.7.lags_ref, bf16[80,16384]{1,0:T(8,128)(2,1)} %get-tuple-element.34.table_ref, bf16[128,16384]{1,0:T(8,128)(2,1)} %get-tuple-element.35.layer1_ref, bf16[128,16384]{1,0:T(8,128)(2,1)} %get-tuple-element.36.layer2_ref, ...), custom_call_target="tpu_custom_call" | custom-call | flops 2097152000 | bytes 20971520 | tf_op jit(solution)/shard_map/backward/pallas_call | solution.py:457
  77.1 1.7 %collective-permute-start.7 = (f32[80,128]{1,0:T(8,128)}, f32[80,128]{1,0:T(8,128)S(1)}, u32[]{:S(2)}, u32[]{:S(2)}) collective-permute-start(f32[80,128]{1,0:T(8,128)} %backward.1), channel_id=1, source_target_pairs={{0,16},{4,20},{8,24},{12,28},{16,0},{20,4},{24,8},{28,12},{1,17},{... | collective-permute-start | bytes 122888 | tf_op jit(solution)/shard_map/ppermute | solution.py:490
  79.5 1.8 %collective-permute-done.7 = f32[80,128]{1,0:T(8,128)S(1)} collective-permute-done((f32[80,128]{1,0:T(8,128)}, f32[80,128]{1,0:T(8,128)S(1)}, u32[]{:S(2)}, u32[]{:S(2)}) %collective-permute-start.7) | collective-permute-done | bytes 40992 | tf_op jit(solution)/shard_map/ppermute | solution.py:490
  82.1 1.7 %collective-permute-start.8 = (f32[88,128]{1,0:T(8,128)S(1)}, f32[88,128]{1,0:T(8,128)S(1)}, u32[]{:S(2)}, u32[]{:S(2)}) collective-permute-start(f32[88,128]{1,0:T(8,128)S(1)} %pad_maximum_fusion.1), channel_id=1, source_target_pairs={{0,8},{4,12},{8,0},{12,4},{16,24},{20,28},{24,16},{28,20},{1,9},{5... | collective-permute-start | bytes 135176 | tf_op jit(solution)/shard_map/ppermute | solution.py:490
  83.8 2.4 %collective-permute-done.8 = f32[88,128]{1,0:T(8,128)S(1)} collective-permute-done((f32[88,128]{1,0:T(8,128)S(1)}, f32[88,128]{1,0:T(8,128)S(1)}, u32[]{:S(2)}, u32[]{:S(2)}) %collective-permute-start.8) | collective-permute-done | bytes 45088 | tf_op jit(solution)/shard_map/ppermute | solution.py:490
  86.3 6.1 %all-to-all-start = ((f32[32,16,512]{2,1,0:T(8,128)}), f32[32,16,512]{2,1,0:T(8,128)S(1)}, u32[]{:S(2)}, u32[]{:S(2)}) async-start(f32[32,16,512]{2,1,0:T(8,128)} %correlate.7.lags_ref), calls=%async_computation | async-start | bytes 2097152 | tf_op jit(solution)/shard_map/all_to_all | solution.py:588
  93.2 2.7 %collective-permute-start.10 = (f32[136,128]{1,0:T(8,128)S(1)}, f32[136,128]{1,0:T(8,128)S(1)}, u32[]{:S(2)}, u32[]{:S(2)}) collective-permute-start(f32[136,128]{1,0:T(8,128)S(1)} %constant_dynamic-update-slice_fusion), channel_id=1, source_target_pairs={{0,2},{1,3},{2,0},{3,1},{4,6},{5,7},{6,4},{7,5},{8,10},{9,11},{10,... | collective-permute-start | bytes 208904 | tf_op jit(solution)/shard_map/ppermute | solution.py:490
  95.8 25.8 %collective-permute-done.10 = f32[136,128]{1,0:T(8,128)S(1)} collective-permute-done((f32[136,128]{1,0:T(8,128)S(1)}, f32[136,128]{1,0:T(8,128)S(1)}, u32[]{:S(2)}, u32[]{:S(2)}) %collective-permute-start.10) | collective-permute-done | bytes 69664 | tf_op jit(solution)/shard_map/ppermute | solution.py:490
  122.4 4.6 %collective-permute-done.11.got_ref = f32[200,128]{1,0:T(8,128)S(1)} collective-permute-done((f32[200,128]{1,0:T(8,128)S(1)}, f32[200,128]{1,0:T(8,128)S(1)}, u32[]{:S(2)}, u32[]{:S(2)}) %collective-permute-start.11) | collective-permute-done | bytes 102432 | tf_op jit(solution)/shard_map/ppermute | solution.py:490
  127.1 1.0 finish.1
  128.1 1.0 copy.31
  (52 shorter events, 4.5 us)
Async XLA Ops:
  2.7 27.0 %copy-start.5 = (bf16[768,256]{1,0:T(8,128)(2,1)S(1)}, bf16[768,256]{1,0:T(8,128)(2,1)}, u32[]{:S(2)}) copy-start(bf16[768,256]{1,0:T(8,128)(2,1)} %constant.29.clone.refs_4_.refs_5_) | copy-start | bytes 1179652
  2.7 27.0 %copy-start.8 = (f32[2,64,128]{2,1,0:T(8,128)S(1)}, f32[2,64,128]{2,1,0:T(8,128)}, u32[]{:S(2)}) copy-start(f32[2,64,128]{2,1,0:T(8,128)} %constant.28.clone.refs_3_.refs_4_) | copy-start | bytes 196612
  2.7 27.0 %copy-start.10 = (bf16[128,128]{1,0:T(8,128)(2,1)S(1)}, bf16[128,128]{1,0:T(8,128)(2,1)}, u32[]{:S(2)}) copy-start(bf16[128,128]{1,0:T(8,128)(2,1)} %constant.27.clone.refs_2_.refs_3_) | copy-start | bytes 98308
  5.7 23.4 %collective-permute-start.6 = (bf16[2,1,16,8192]{3,2,1,0:T(8,128)(2,1)}, bf16[2,1,16,8192]{3,2,1,0:T(8,128)(2,1)S(1)}, u32[]{:S(2)}, u32[]{:S(2)}) collective-permute-start(bf16[2,1,16,8192]{3,2,1,0:T(8,128)(2,1)} %get-tuple-element.33), channel_id=1, source_target_pairs={{0,4},{4,0},{8,12},{12,8},{16,20},{20,16},{24,28},{28,24},{1,5},{5... | collective-permute-start | bytes 1572872 | tf_op jit(solution)/shard_map/ppermute | solution.py:578
  6.2 22.9 %collective-permute-start.4 = (bf16[2,1,16,8192]{3,2,1,0:T(8,128)(2,1)}, bf16[2,1,16,8192]{3,2,1,0:T(8,128)(2,1)S(1)}, u32[]{:S(2)}, u32[]{:S(2)}) collective-permute-start(bf16[2,1,16,8192]{3,2,1,0:T(8,128)(2,1)} %get-tuple-element.26.refs_0_), channel_id=1, source_target_pairs={{0,24},{4,28},{8,16},{12,20},{16,8},{20,12},{24,0},{28,4},{1,25},{... | collective-permute-start | bytes 1572872 | tf_op jit(solution)/shard_map/ppermute | solution.py:578
  9.7 25.0 %collective-permute-start.5 = (bf16[2,1,16,8192]{3,2,1,0:T(8,128)(2,1)}, bf16[2,1,16,8192]{3,2,1,0:T(8,128)(2,1)S(1)}, u32[]{:S(2)}, u32[]{:S(2)}) collective-permute-start(bf16[2,1,16,8192]{3,2,1,0:T(8,128)(2,1)} %get-tuple-element.31), channel_id=1, source_target_pairs={{0,28},{4,24},{8,20},{12,16},{16,12},{20,8},{24,4},{28,0},{1,29},{... | collective-permute-start | bytes 1572872 | tf_op jit(solution)/shard_map/ppermute | solution.py:578
  9.8 36.0 %collective-permute-start.2 = (bf16[2,1,16,8192]{3,2,1,0:T(8,128)(2,1)}, bf16[2,1,16,8192]{3,2,1,0:T(8,128)(2,1)S(1)}, u32[]{:S(2)}, u32[]{:S(2)}) collective-permute-start(bf16[2,1,16,8192]{3,2,1,0:T(8,128)(2,1)} %get-tuple-element.29), channel_id=1, source_target_pairs={{0,8},{4,12},{8,0},{12,4},{16,24},{20,28},{24,16},{28,20},{1,9},{5... | collective-permute-start | bytes 1572872 | tf_op jit(solution)/shard_map/ppermute | solution.py:578
  11.5 34.3 %collective-permute-start.3 = (bf16[2,1,16,8192]{3,2,1,0:T(8,128)(2,1)}, bf16[2,1,16,8192]{3,2,1,0:T(8,128)(2,1)S(1)}, u32[]{:S(2)}, u32[]{:S(2)}) collective-permute-start(bf16[2,1,16,8192]{3,2,1,0:T(8,128)(2,1)} %get-tuple-element.30), channel_id=1, source_target_pairs={{0,16},{4,20},{8,24},{12,28},{16,0},{20,4},{24,8},{28,12},{1,17},{... | collective-permute-start | bytes 1572872 | tf_op jit(solution)/shard_map/ppermute | solution.py:578
  29.1 26.9 %collective-permute-start = (bf16[2,1,16,8192]{3,2,1,0:T(8,128)(2,1)}, bf16[2,1,16,8192]{3,2,1,0:T(8,128)(2,1)S(1)}, u32[]{:S(2)}, u32[]{:S(2)}) collective-permute-start(bf16[2,1,16,8192]{3,2,1,0:T(8,128)(2,1)} %get-tuple-element.27), channel_id=1, source_target_pairs={{0,12},{4,8},{8,4},{12,0},{16,28},{20,24},{24,20},{28,16},{1,13},{... | collective-permute-start | bytes 1572872 | tf_op jit(solution)/shard_map/ppermute | solution.py:578
  29.1 26.9 %collective-permute-start.1 = (bf16[2,1,16,8192]{3,2,1,0:T(8,128)(2,1)}, bf16[2,1,16,8192]{3,2,1,0:T(8,128)(2,1)S(1)}, u32[]{:S(2)}, u32[]{:S(2)}) collective-permute-start(bf16[2,1,16,8192]{3,2,1,0:T(8,128)(2,1)} %get-tuple-element.28), channel_id=1, source_target_pairs={{0,20},{4,16},{8,28},{12,24},{16,4},{20,0},{24,12},{28,8},{1,21},{... | collective-permute-start | bytes 1572872 | tf_op jit(solution)/shard_map/ppermute | solution.py:578
  29.7 1.0 copy-start.4
  38.8 17.3 %copy-start.6 = (bf16[768,256]{1,0:T(8,128)(2,1)S(1)}, bf16[768,256]{1,0:T(8,128)(2,1)}, u32[]{:S(2)}) copy-start(bf16[768,256]{1,0:T(8,128)(2,1)} %constant.31.clone.refs_7_) | copy-start | bytes 1179652
  38.8 17.3 %copy-start.7 = (bf16[128,384]{1,0:T(8,128)(2,1)S(1)}, bf16[128,384]{1,0:T(8,128)(2,1)}, u32[]{:S(2)}) copy-start(bf16[128,384]{1,0:T(8,128)(2,1)} %constant.32.clone.refs_8_) | copy-start | bytes 294916
  38.8 17.2 %copy-start.9 = (f32[2,64,128]{2,1,0:T(8,128)S(1)}, f32[2,64,128]{2,1,0:T(8,128)}, u32[]{:S(2)}) copy-start(f32[2,64,128]{2,1,0:T(8,128)} %constant.30.clone.refs_6_) | copy-start | bytes 196612
  63.5 63.6 %copy-start = (f32[64,64]{1,0:T(8,128)S(1)}, f32[64,64]{1,0:T(8,128)}, u32[]{:S(2)}) copy-start(f32[64,64]{1,0:T(8,128)} %hidden_ref.5) | copy-start | bytes 49156
  63.5 63.6 %copy-start.1 = (f32[64,33]{0,1:T(8,128)S(1)}, f32[64,33]{0,1:T(8,128)}, u32[]{:S(2)}) copy-start(f32[64,33]{0,1:T(8,128)} %param.26) | copy-start | bytes 25348
  63.5 63.6 %copy-start.2 = (f32[2,64]{1,0:T(2,128)S(1)}, f32[2,64]{1,0:T(2,128)}, u32[]{:S(2)}) copy-start(f32[2,64]{1,0:T(2,128)} %freq_ref.5) | copy-start | bytes 1540
  63.5 63.6 %copy-start.3 = (f32[64]{0:T(128)S(1)}, f32[64]{0:T(128)}, u32[]{:S(2)}) copy-start(f32[64]{0:T(128)} %param.27) | copy-start | bytes 772
  77.1 4.2 %collective-permute-start.7 = (f32[80,128]{1,0:T(8,128)}, f32[80,128]{1,0:T(8,128)S(1)}, u32[]{:S(2)}, u32[]{:S(2)}) collective-permute-start(f32[80,128]{1,0:T(8,128)} %backward.1), channel_id=1, source_target_pairs={{0,16},{4,20},{8,24},{12,28},{16,0},{20,4},{24,8},{28,12},{1,17},{... | collective-permute-start | bytes 122888 | tf_op jit(solution)/shard_map/ppermute | solution.py:490
  82.1 4.1 %collective-permute-start.8 = (f32[88,128]{1,0:T(8,128)S(1)}, f32[88,128]{1,0:T(8,128)S(1)}, u32[]{:S(2)}, u32[]{:S(2)}) collective-permute-start(f32[88,128]{1,0:T(8,128)S(1)} %pad_maximum_fusion.1), channel_id=1, source_target_pairs={{0,8},{4,12},{8,0},{12,4},{16,24},{20,28},{24,16},{28,20},{1,9},{5... | collective-permute-start | bytes 135176 | tf_op jit(solution)/shard_map/ppermute | solution.py:490
  86.2 6.2 %collective-permute-start.9 = (f32[104,128]{1,0:T(8,128)S(1)}, f32[104,128]{1,0:T(8,128)S(1)}, u32[]{:S(2)}, u32[]{:S(2)}) collective-permute-start(f32[104,128]{1,0:T(8,128)S(1)} %pad_maximum_fusion), channel_id=1, source_target_pairs={{0,4},{4,0},{8,12},{12,8},{16,20},{20,16},{24,28},{28,24},{1,5},{5... | collective-permute-start | bytes 159752 | tf_op jit(solution)/shard_map/ppermute | solution.py:490
  86.3 41.8 %all-to-all-start = ((f32[32,16,512]{2,1,0:T(8,128)}), f32[32,16,512]{2,1,0:T(8,128)S(1)}, u32[]{:S(2)}, u32[]{:S(2)}) async-start(f32[32,16,512]{2,1,0:T(8,128)} %correlate.7.lags_ref), calls=%async_computation | async-start | bytes 2097152 | tf_op jit(solution)/shard_map/all_to_all | solution.py:588
  93.2 28.5 %collective-permute-start.10 = (f32[136,128]{1,0:T(8,128)S(1)}, f32[136,128]{1,0:T(8,128)S(1)}, u32[]{:S(2)}, u32[]{:S(2)}) collective-permute-start(f32[136,128]{1,0:T(8,128)S(1)} %constant_dynamic-update-slice_fusion), channel_id=1, source_target_pairs={{0,2},{1,3},{2,0},{3,1},{4,6},{5,7},{6,4},{7,5},{8,10},{9,11},{10,... | collective-permute-start | bytes 208904 | tf_op jit(solution)/shard_map/ppermute | solution.py:490
  122.3 4.7 %collective-permute-start.11 = (f32[200,128]{1,0:T(8,128)S(1)}, f32[200,128]{1,0:T(8,128)S(1)}, u32[]{:S(2)}, u32[]{:S(2)}) collective-permute-start(f32[200,128]{1,0:T(8,128)S(1)} %slice_dynamic-update-slice_fusion.both_ref), channel_id=1, source_target_pairs={{0,1},{1,0},{2,3},{3,2},{4,5},{5,4},{6,7},{7,6},{8,9},{9,8},{10,11... | collective-permute-start | bytes 307208 | tf_op jit(solution)/shard_map/ppermute | solution.py:490

commit v5 on v4

--- a/solution.py
+++ b/solution.py
@@ -91,61 +91,66 @@
     return jnp.sum(jnp.where(at[0] == at[1], row, 0.0), axis=1, keepdims=True)
 
 
-def pick_kernel(x_ref, g_ref, *refs, partners, own, start, after):
+def pick_kernel(x_ref, g_ref, *refs, items, own, after):
     refs = refs[after:]
-    outs, (held_ref, in_sem, out_sem) = refs[: len(partners)], refs[len(partners) :]
-    per = outs[0].shape[2]
+    outs, held = refs[: len(items)], refs[len(items) : 2 * len(items)]
+    in_sem, out_sem = refs[2 * len(items) :]
     arrivals, departures = [], []
-    for k, partner in enumerate(partners):
-        first = pl.multiple_of((lax.axis_index("dp") ^ partner) * own + start, per)
+    for k, (partner, start, count) in enumerate(items):
+        first = pl.multiple_of((lax.axis_index("dp") ^ partner) * own + start, count)
         for at, ref in enumerate((x_ref, g_ref)):
             arrivals.append(
                 pltpu.make_async_copy(
-                    ref.at[:, pl.ds(first, per), :], held_ref.at[k, at], in_sem.at[k, at]
+                    ref.at[:, pl.ds(first, count), :], held[k].at[at], in_sem.at[k, at]
                 )
             )
             arrivals[-1].start()
-    for k in range(len(partners)):
+    for k in range(len(items)):
         arrivals[2 * k].wait()
         arrivals[2 * k + 1].wait()
-        departures.append(pltpu.make_async_copy(held_ref.at[k], outs[k], out_sem.at[k]))
+        departures.append(pltpu.make_async_copy(held[k], outs[k], out_sem.at[k]))
         departures[-1].start()
     for departure in departures:
         departure.wait()
 
 
-def pick(x, g, partners, own, start, count, after=()):
+def pick(x, g, items, own, after=()):
     seqs, _, length = x.shape
-    shape = (2, seqs, count, length)
-    if count % 8:
-        firsts = [(lax.axis_index("dp") ^ p) * own + start for p in partners]
+    if own % 8:
         return [
-            jnp.stack([lax.dynamic_slice_in_dim(v, first, count, 1) for v in (x, g)])
-            for first in firsts
+            jnp.stack(
+                [
+                    lax.dynamic_slice_in_dim(
+                        v, (lax.axis_index("dp") ^ partner) * own + start, count, 1
+                    )
+                    for v in (x, g)
+                ]
+            )
+            for partner, start, count in items
         ]
+    shapes = [(2, seqs, count, length) for _, _, count in items]
     anywhere = pl.BlockSpec(memory_space=pl.ANY)
     return pl.pallas_call(
-        functools.partial(
-            pick_kernel, partners=partners, own=own, start=start, after=len(after)
-        ),
+        functools.partial(pick_kernel, items=items, own=own, after=len(after)),
         in_specs=[anywhere] * (2 + len(after)),
-        out_specs=[anywhere] * len(partners),
-        out_shape=[jax.ShapeDtypeStruct(shape, BF16)] * len(partners),
+        out_specs=[anywhere] * len(items),
+        out_shape=[jax.ShapeDtypeStruct(shape, BF16) for shape in shapes],
         scratch_shapes=[
-            pltpu.VMEM((len(partners), *shape), BF16),
-            pltpu.SemaphoreType.DMA((len(partners), 2)),
-            pltpu.SemaphoreType.DMA((len(partners),)),
+            *[pltpu.VMEM(shape, BF16) for shape in shapes],
+            pltpu.SemaphoreType.DMA((len(items), 2)),
+            pltpu.SemaphoreType.DMA((len(items),)),
         ],
         cost_estimate=pl.CostEstimate(
-            flops=0, bytes_accessed=4 * len(partners) * math.prod(shape), transcendentals=0
+            flops=0, bytes_accessed=4 * sum(math.prod(shape) for shape in shapes), transcendentals=0
         ),
         name="pick",
     )(x, g, *after)
 
 
-def correlate_kernel(*refs, pieces, held, last):
+def correlate_kernel(*refs, pieces, held, lags, last):
     piece_refs, refs = refs[:pieces], refs[pieces:]
     held_ref, refs = (refs[0], refs[1:]) if held else (None, refs)
+    refs = refs[lags:]
     first_ref, twist_ref, second_ref = refs[:3]
     if last:
         untwist_ref, back_ref, last_ref, out_ref, lag_ref, cross_ref = refs[3:9]
@@ -246,7 +251,7 @@
                 ]
 
 
-def correlate(pieces, held, scale, owners):
+def correlate(pieces, held, scale, owners, lags=None, chunk=0, chunks=1):
     _, seqs_each, channels, length = pieces[0].shape
     lanes, rows = LANES, length // LANES
     seqs = seqs_each * len(pieces)
@@ -256,15 +261,17 @@
         jnp.asarray(t) for t in tables(rows, 2.0 * scale / total)
     )
     consts = [first, twist, second] + ([untwist, back, last] if owners else [])
-    spectrum = pl.BlockSpec((each, rows, 2 * lanes), lambda c: (c, 0, 0))
+    skip = chunk * (channels // each)
+    spectrum = pl.BlockSpec((each, rows, 2 * lanes), lambda c: (c + skip, 0, 0))
+    lags = [] if lags is None else [lags]
     held = [] if held is None else [held]
     block = pl.BlockSpec(pieces[0].shape, lambda c: (0, 0, 0, 0))
     whole = [
         pl.BlockSpec(t.shape, functools.partial(lambda n, c: (0,) * n, t.ndim)) for t in consts
     ]
     if owners:
-        shape = (owners, channels, total // owners)
-        out_spec = pl.BlockSpec(shape, lambda c: (0, 0, 0))
+        shape = (owners, channels * chunks, total // owners)
+        out_spec = pl.BlockSpec((owners, channels, total // owners), lambda c: (0, chunk, 0))
     else:
         shape = (channels, rows, 2 * lanes)
         out_spec = spectrum
@@ -282,10 +289,18 @@
     ]
     return pl.pallas_call(
         functools.partial(
-            correlate_kernel, pieces=len(pieces), held=len(held), last=bool(owners)
+            correlate_kernel,
+            pieces=len(pieces),
+            held=len(held),
+            lags=len(lags),
+            last=bool(owners),
         ),
         grid=(channels // each,),
-        in_specs=[block] * len(pieces) + [spectrum] * len(held) + whole,
+        in_specs=[block] * len(pieces)
+        + [spectrum] * len(held)
+        + [pl.BlockSpec(memory_space=pl.ANY)] * len(lags)
+        + whole,
+        input_output_aliases={len(pieces) + len(held): 0} if lags else {},
         out_specs=out_spec,
         out_shape=jax.ShapeDtypeStruct(shape, F32),
         scratch_shapes=scratch,
@@ -296,7 +311,7 @@
         ),
         compiler_params=pltpu.CompilerParams(vmem_limit_bytes=24 * 2**20),
         name="correlate",
-    )(*pieces, *held, *consts)
+    )(*pieces, *held, *lags, *consts)
 
 
 STEP = 2048
@@ -480,44 +495,56 @@
 
 
 def rounds():
-    sizes = ((axis, lax.axis_size(axis)) for axis in ("dp", "chan"))
-    return [(axis, 1 << b) for axis, size in sizes for b in reversed(range(size.bit_length() - 1))]
+    steps = []
+    for axis in ("dp", "chan"):
+        bits = [1 << b for b in range(lax.axis_size(axis).bit_length() - 1)]
+        alone = 1 if axis == "dp" else 0
+        for group in [bits[:alone]] + [bits[b : b + 2] for b in range(alone, len(bits), 2)]:
+            masks = [0]
+            for bit in group:
+                masks += [mask | bit for mask in masks]
+            if len(masks) > 1:
+                steps.append((axis, masks))
+    return steps
 
 
 def share(both, summed):
-    for axis, bit in rounds():
+    steps = rounds()
+    for axis, masks in steps:
         size = lax.axis_size(axis)
-        got = lax.ppermute(both, axis, [(i, i ^ bit) for i in range(size)])
-        last = both, got
-        both = jnp.concatenate([both[:summed] + got[:summed], both[summed:], got[summed:]], axis=0)
-    return last
-
-
-def finish_kernel(
-    both_ref, got_ref, embed_ref, bias_ref, hidden_ref, freq_ref,
-    embed_grad, bias_grad, hidden_grad, frequency_grad, output_grad, decay_grad, rows_ref, *, own, pack,
-):
+        parts = [both]
+        for mask in masks[1:]:
+            parts.append(lax.ppermute(both, axis, [(i, i ^ mask) for i in range(size)]))
+        total = sum(part[:summed] for part in parts)
+        both = jnp.concatenate([total, *(part[summed:] for part in parts)], axis=0)
+    return parts
+
+
+def finish_kernel(*refs, own, pack):
+    steps = rounds()
+    part_refs, refs = refs[: len(steps[-1][1])], refs[len(steps[-1][1]) :]
+    embed_ref, bias_ref, hidden_ref, freq_ref = refs[:4]
+    embed_grad, bias_grad, hidden_grad, frequency_grad, output_grad, decay_grad, rows_ref = refs[4:]
     hidden, features = hidden_ref.shape[0], embed_ref.shape[0]
     summed = summed_rows(hidden, output_grad.shape[1])
-    total = both_ref[:summed] + got_ref[:summed]
+    total = sum(ref[:summed] for ref in part_refs)
     net = total[:hidden]
     turned = net.T
     decay_grad[...] = total[hidden : hidden + decay_grad.shape[0]]
     unit = own // pack
     count = output_grad.shape[1] // own
     here = {axis: lax.axis_index(axis) for axis in ("dp", "chan")}
-    steps = rounds()
+    each = count // len(part_refs)
     for k in range(count):
-        there = dict(here)
-        for n, (axis, bit) in enumerate(steps):
-            if k >> n & 1:
-                there[axis] = there[axis] ^ bit
+        there, rest = dict(here), k
+        for axis, masks in steps:
+            there[axis] = there[axis] ^ masks[rest % len(masks)]
+            rest //= len(masks)
         place = there["chan"] * lax.axis_size("dp") + there["dp"]
-        ref, at = (both_ref, k) if k < count // 2 else (got_ref, k - count // 2)
         for n in range(pack):
-            rows_ref[pl.ds(pl.multiple_of(place * own + n * unit, unit), unit), :] = ref[
-                pl.ds(summed + at * unit, unit), n * hidden : (n + 1) * hidden
-            ]
+            rows_ref[pl.ds(pl.multiple_of(place * own + n * unit, unit), unit), :] = part_refs[
+                k // each
+            ][pl.ds(summed + k % each * unit, unit), n * hidden : (n + 1) * hidden]
     output_grad[...] = rows_ref[...].T
     table = turned[hidden:]
     embed = jnp.concatenate([table[features - 1 : features], table[: features - 1]], axis=0)
@@ -531,7 +558,7 @@
     frequency_grad[1:2] = jnp.sum(hidden_ref[...].T * turned[:hidden], axis=0, keepdims=True)
 
 
-def finish(both, got, embed_weight, embed_bias, hidden_weight, frequency, channels, own):
+def finish(parts, embed_weight, embed_bias, hidden_weight, frequency, channels, own):
     hidden, features = embed_weight.shape
     shapes = (
         (features, hidden), (1, hidden), (hidden, hidden), (2, hidden), (hidden, channels),
@@ -543,7 +570,7 @@
         scratch_shapes=[pltpu.VMEM((channels, hidden), F32)],
         compiler_params=pltpu.CompilerParams(vmem_limit_bytes=8 * 2**20),
         name="finish",
-    )(both, got, embed_weight.T, embed_bias[None], hidden_weight, frequency)
+    )(*parts, embed_weight.T, embed_bias[None], hidden_weight, frequency)
     return embed.T, bias[0], hid, freq, output.T, decay.reshape(-1)[:channels]
 
 
@@ -570,19 +597,30 @@
     partners = sorted(
         range(1, dp), key=lambda p: (p != 1, -bin(p >> 1).count("1"), p & 1, p)
     )
-    pieces = [None] * dp
-    made = []
-    for some in (tuple(partners[1:3]), (partners[0], *partners[3:], 0)):
-        made = pick(signal, signal_grad, some, own, 0, own, made[:1])
-        for p, sent in zip(some, made):
-            pieces[p] = lax.ppermute(sent, "dp", [(i, i ^ p) for i in range(dp)]) if p else sent
-    order = [0, *partners]
-    spectrum = None
-    cuts = (*range(0, dp, max(2, dp // 4)), dp)
-    for q in range(len(cuts) - 1):
-        some = [pieces[p] for p in order[cuts[q] : cuts[q + 1]]]
-        spectrum = correlate(some, spectrum, scale, count if q == len(cuts) - 2 else 0)
+    chunks = 2 if own % 16 == 0 and dp > 2 else 1
+    per = own // chunks
+    late = partners[-2:] if chunks > 1 else []
+    soon = [p for p in (0, *partners) if p not in late]
+    items = [(p, 0, own) for p in (*partners[1:3], partners[0], *soon[4:], 0)]
+    items += [(p, q * per, per) for q in range(chunks) for p in late]
+    made, pieces = [], {}
+    for some in (tuple(items[:2]), tuple(items[2:])):
+        made = pick(signal, signal_grad, some, own, made[:1])
+        for (p, start, _), sent in zip(some, made):
+            swap = [(i, i ^ p) for i in range(dp)]
+            pieces[p, start] = lax.ppermute(sent, "dp", swap) if p else sent
+    lags = spectrum = None
+    step = max(2, dp // 4)
+    for at in range(0, len(soon), step):
+        end = not late and at + step >= len(soon)
+        spectrum = correlate(
+            [pieces[p, 0] for p in soon[at : at + step]], spectrum, scale, count if end else 0
+        )
     lags = spectrum
+    for q in range(chunks if late else 0):
+        lags = correlate(
+            [pieces[p, q * per] for p in late], spectrum, scale, count, lags if q else None, q, chunks
+        )
 
     saved = network(embed_weight, embed_bias, hidden_weight, frequency, total)
     shared = lax.all_to_all(lags, ("dp", "chan"), 0, 0, tiled=True)
@@ -590,12 +628,12 @@
     both = backward(
         first_own, lags, saved, decay_rate, output_weight, hidden_weight, frequency, total
     )
-    both, got = share(both, summed_rows(hidden, channels))
+    parts = share(both, summed_rows(hidden, channels))
     filter_grad = jnp.swapaxes(shared.reshape(dp, chan, own, -1), 0, 1)
     filter_grad = filter_grad.reshape(channels, -1)
     return (
         filter_grad,
-        *finish(both, got, embed_weight, embed_bias, hidden_weight, frequency, channels, own),
+        *finish(parts, embed_weight, embed_bias, hidden_weight, frequency, channels, own),
     )
 
 

time: 130 us -> 104 us (0.80)
  waiting for transfers between devices: 47.8 us -> 19 us
  starting transfers between devices: 20.3 us -> 23.6 us
    ppermute x12 -> x16, waiting for transfers between devices: 47.8 us -> 19 us  [the longest x7 10.9 us: share(): parts.append(lax.ppermute(both, axis, [(i, i ^ mask) for i in range(size)]))]
    ppermute x12 -> x16, starting transfers between devices: 14.2 us -> 17.6 us  [the longest x9 9.33 us: work(): pieces[p, start] = lax.ppermute(sent, 'dp', swap) if p else sent]
    pallas_call x4 -> x5, Pallas kernels: 19.5 us -> 19.7 us  [correlate(): pl.pallas_call(functools.partial(correlate_kernel, pieces=len(pieces), he...]
  transfers between devices with their start and end apart: 13 -> 17, of which waited for: 7 -> 11; matrix products, arithmetic and copies ran while one was open for 2% -> 2% of each run, Pallas kernels for 23% -> 45%
where the time goes in v5:
time: 104 us; the launch traced here: 103 us
  Pallas kernels  55.1 us (53%)
  starting transfers between devices  23.6 us (23%)
  waiting for transfers between devices  19 us (18%)
  local copies, waits for them, and re-layouts  3.54 us (3%)
    pallas_call x5, Pallas kernels, correlate(): pl.pallas_call(functools.partial(correlate_kernel, pieces=len(pieces), he...  19.7 us
    pallas_call x1, Pallas kernels, network(): pl.pallas_call(functools.partial(network_kernel, total=total), grid=(tota...  16 us
    pallas_call x1, Pallas kernels, backward(): pl.pallas_call(functools.partial(backward_kernel, total=total, pack=pack)...  13.5 us
    ppermute x7, waiting for transfers between devices, share(): parts.append(lax.ppermute(both, axis, [(i, i ^ mask) for i in range(size)]))  10.9 us
    ppermute x9, starting transfers between devices, work(): pieces[p, start] = lax.ppermute(sent, 'dp', swap) if p else sent  9.33 us
    ppermute x7, starting transfers between devices, share(): parts.append(lax.ppermute(both, axis, [(i, i ^ mask) for i in range(size)]))  8.24 us
    ppermute x9, waiting for transfers between devices, work(): pieces[p, start] = lax.ppermute(sent, 'dp', swap) if p else sent  8.06 us
    all_to_all x1, starting transfers between devices, work(): shared = lax.all_to_all(lags, ('dp', 'chan'), 0, 0, tiled=True)  6.05 us
  transfers between devices with their start and end apart: 17, of which 11 were waited for; matrix products, arithmetic and copies ran while one was open for 2% of the time, Pallas kernels for 45%

profile of v5, /device:TPU:0, one launch (start us, length us, event | category | flops | bytes accessed | tf_op | source)
XLA Modules:
  0.0 102.9 jit_solution(5911017375546820233)
XLA Ops:
  0.6 2.1 %pick.2 = (bf16[2,1,16,8192]{3,2,1,0:T(8,128)(2,1)}, bf16[2,1,16,8192]{3,2,1,0:T(8,128)(2,1)}) custom-call(bf16[1,128,8192]{2,1,0:T(8,128)(2,1)} %x_ref.3, bf16[1,128,8192]{2,1,0:T(8,128)(2,1)} %g_ref.3), custom_call_target="tpu_custom_call" | custom-call | bytes 2097152 | tf_op jit(solution)/shard_map/pick/pallas_call | solution.py:133
  2.7 3.0 %pick.3 = (bf16[2,1,16,8192]{3,2,1,0:T(8,128)(2,1)}, bf16[2,1,16,8192]{3,2,1,0:T(8,128)(2,1)}, bf16[2,1,16,8192]{3,2,1,0:T(8,128)(2,1)}, bf16[2,1,16,8192]{3,2,1...) custom-call(bf16[1,128,8192]{2,1,0:T(8,128)(2,1)} %x_ref.3, ...), custom_call_target="tpu_custom_call" | custom-call | bytes 6291456 | tf_op jit(solution)/shard_map/pick/pallas_call | solution.py:133
  6.3 3.5 %collective-permute-start.4 = (bf16[2,1,16,8192]{3,2,1,0:T(8,128)(2,1)}, bf16[2,1,16,8192]{3,2,1,0:T(8,128)(2,1)S(1)}, u32[]{:S(2)}, u32[]{:S(2)}) collective-permute-start(bf16[2,1,16,8192]{3,2,1,0:T(8,128)(2,1)} %get-tuple-element.28.refs_0_), channel_id=1, source_target_pairs={{0,24},{4,28},{8,16},{12,20},{16,8},{20,12},{24,0},{28,4},{1,25},{... | collective-permute-start | bytes 1572872 | tf_op jit(solution)/shard_map/ppermute | solution.py:611
  9.8 1.7 %collective-permute-start.2 = (bf16[2,1,16,8192]{3,2,1,0:T(8,128)(2,1)}, bf16[2,1,16,8192]{3,2,1,0:T(8,128)(2,1)S(1)}, u32[]{:S(2)}, u32[]{:S(2)}) collective-permute-start(bf16[2,1,16,8192]{3,2,1,0:T(8,128)(2,1)} %get-tuple-element.31), channel_id=1, source_target_pairs={{0,8},{4,12},{8,0},{12,4},{16,24},{20,28},{24,16},{28,20},{1,9},{5... | collective-permute-start | bytes 1572872 | tf_op jit(solution)/shard_map/ppermute | solution.py:611
  11.5 1.5 %collective-permute-start.3 = (bf16[2,1,16,8192]{3,2,1,0:T(8,128)(2,1)}, bf16[2,1,16,8192]{3,2,1,0:T(8,128)(2,1)S(1)}, u32[]{:S(2)}, u32[]{:S(2)}) collective-permute-start(bf16[2,1,16,8192]{3,2,1,0:T(8,128)(2,1)} %get-tuple-element.32), channel_id=1, source_target_pairs={{0,16},{4,20},{8,24},{12,28},{16,0},{20,4},{24,8},{28,12},{1,17},{... | collective-permute-start | bytes 1572872 | tf_op jit(solution)/shard_map/ppermute | solution.py:611
  13.0 16.0 %network.1 = (bf16[80,16384]{1,0:T(8,128)(2,1)}, bf16[128,16384]{1,0:T(8,128)(2,1)}, bf16[128,16384]{1,0:T(8,128)(2,1)}, f32[64,16384]{1,0:T(8,128)}, f32[64,16384]{1,0:T(8,128)}) custom-call(s32[16,1]{1,0:T(8,128)} %constant.33.clone.factor_ref, f32[33,64]{1,0:T(8,128)} %bitcast.13, f32[1,64]{1,0:T(1,128)} %bitcast.15, f32[64,64]{1,0:T(8,128)} %refs_6_.3, ...), custom_call_target="tpu_custom_call" | custom-call | flops 629145600 | bytes 20971520 | tf_op jit(solution)/shard_map/network/pallas_call | solution.py:377
  30.1 4.0 %correlate.5.refs_2_ = f32[16,64,256]{2,1,0:T(8,128)S(1)} custom-call(bf16[2,1,16,8192]{3,2,1,0:T(8,128)(2,1)S(1)} %copy-done.10, bf16[2,1,16,8192]{3,2,1,0:T(8,128)(2,1)S(1)} %collective-permute-done.6.refs_1_, bf16[128,128]{1,0:T(8,128)(2,1)S(1)} %copy-done.6, f32[2,64,128]{2,1,0:T(8,128)S(1)} %copy-done.4, bf16[768,256]{1,0:T(8,128)(2,1)S(1)} %copy-done), custom_call_target="tpu_custom_call" | custom-call | flops 2415919104 | bytes 2097152 | tf_op jit(solution)/shard_map/correlate/pallas_call | solution.py:290
  34.8 1.3 %collective-permute-start = (bf16[2,1,8,8192]{3,2,1,0:T(8,128)(2,1)S(1)}, bf16[2,1,8,8192]{3,2,1,0:T(8,128)(2,1)S(1)}, u32[]{:S(2)}, u32[]{:S(2)}) collective-permute-start(bf16[2,1,8,8192]{3,2,1,0:T(8,128)(2,1)S(1)} %copy-done.12), channel_id=1, source_target_pairs={{0,12},{4,8},{8,4},{12,0},{16,28},{20,24},{24,20},{28,16},{1,13},{... | collective-permute-start | bytes 786440 | tf_op jit(solution)/shard_map/ppermute | solution.py:611
  36.1 4.0 %correlate.6.refs_2_ = f32[16,64,256]{2,1,0:T(8,128)S(1)} custom-call(bf16[2,1,16,8192]{3,2,1,0:T(8,128)(2,1)S(1)} %collective-permute-done.4.refs_0_, bf16[2,1,16,8192]{3,2,1,0:T(8,128)(2,1)S(1)} %collective-permute-done.5.refs_1_, f32[16,64,256]{2,1,0:T(8,128)S(1)} %correlate.5.refs_2_, bf16[128,128]{1,0:T(8,128)(2,1)S(1)} %copy-done.6, ...), custom_call_target="tpu_custom_call" | custom-call | flops 2415919104 | bytes 2097152 | tf_op jit(solution)/shard_map/correlate/pallas_call | solution.py:290
  40.1 5.7 %collective-permute-done.2.refs_0_ = bf16[2,1,16,8192]{3,2,1,0:T(8,128)(2,1)S(1)} collective-permute-done((bf16[2,1,16,8192]{3,2,1,0:T(8,128)(2,1)}, bf16[2,1,16,8192]{3,2,1,0:T(8,128)(2,1)S(1)}, u32[]{:S(2)}, u32[]{:S(2)}) %collective-permute-start.2) | collective-permute-done | bytes 524320 | tf_op jit(solution)/shard_map/ppermute | solution.py:611
  45.9 4.0 %correlate.7.refs_2_ = f32[16,64,256]{2,1,0:T(8,128)S(1)} custom-call(bf16[2,1,16,8192]{3,2,1,0:T(8,128)(2,1)S(1)} %collective-permute-done.2.refs_0_, bf16[2,1,16,8192]{3,2,1,0:T(8,128)(2,1)S(1)} %collective-permute-done.3.refs_1_, f32[16,64,256]{2,1,0:T(8,128)S(1)} %correlate.6.refs_2_, bf16[128,128]{1,0:T(8,128)(2,1)S(1)} %copy-done.6, ...), custom_call_target="tpu_custom_call" | custom-call | flops 2415919104 | bytes 2097152 | tf_op jit(solution)/shard_map/correlate/pallas_call | solution.py:290
  50.6 3.8 %correlate.8.refs_3_ = f32[32,16,512]{2,1,0:T(8,128)} custom-call(bf16[2,1,8,8192]{3,2,1,0:T(8,128)(2,1)S(1)} %collective-permute-done.7.refs_0_, bf16[2,1,8,8192]{3,2,1,0:T(8,128)(2,1)S(1)} %collective-permute-done.8.refs_1_, f32[16,64,256]{2,1,0:T(8,128)S(1)} %correlate.7.refs_2_, bf16[128,128]{1,0:T(8,128)(2,1)S(1)} %copy-done.6, ...), custom_call_target="tpu_custom_call" | custom-call | flops 1207959552 | bytes 1048576 | tf_op jit(solution)/shard_map/correlate/pallas_call | solution.py:290
  54.4 1.6 %collective-permute-done.refs_0_ = bf16[2,1,8,8192]{3,2,1,0:T(8,128)(2,1)S(1)} collective-permute-done((bf16[2,1,8,8192]{3,2,1,0:T(8,128)(2,1)S(1)}, bf16[2,1,8,8192]{3,2,1,0:T(8,128)(2,1)S(1)}, u32[]{:S(2)}, u32[]{:S(2)}) %collective-permute-start) | collective-permute-done | bytes 262176 | tf_op jit(solution)/shard_map/ppermute | solution.py:611
  56.1 3.8 %correlate.9.lags_ref = f32[32,16,512]{2,1,0:T(8,128)} custom-call(bf16[2,1,8,8192]{3,2,1,0:T(8,128)(2,1)S(1)} %collective-permute-done.refs_0_, bf16[2,1,8,8192]{3,2,1,0:T(8,128)(2,1)S(1)} %collective-permute-done.1.refs_1_, f32[16,64,256]{2,1,0:T(8,128)S(1)} %correlate.7.refs_2_, f32[32,16,512]{2,1,0:T(8,128)} %correlate.8.refs_3_, ...), custom_call_target="tpu_custom_call", output_to_operand_aliasing={{}: (3, {})} | custom-call | flops 1207959552 | bytes 1048576 | tf_op jit(solution)/shard_map/correlate/pallas_call | solution.py:290
  59.9 6.0 %all-to-all-start = ((f32[32,16,512]{2,1,0:T(8,128)}), f32[32,16,512]{2,1,0:T(8,128)S(1)}, u32[]{:S(2)}, u32[]{:S(2)}) async-start(f32[32,16,512]{2,1,0:T(8,128)} %correlate.9.lags_ref), calls=%async_computation | async-start | bytes 2097152 | tf_op jit(solution)/shard_map/all_to_all | solution.py:626
  66.0 13.5 %backward.1 = f32[80,128]{1,0:T(8,128)} custom-call(s32[1]{0:T(128)} %bitcast.3.first_ref, f32[32,16,512]{2,1,0:T(8,128)} %correlate.9.lags_ref, bf16[80,16384]{1,0:T(8,128)(2,1)} %get-tuple-element.38.table_ref, bf16[128,16384]{1,0:T(8,128)(2,1)} %get-tuple-element.39.layer1_ref, bf16[128,16384]{1,0:T(8,128)(2,1)} %get-tuple-element.40.layer2_ref, ...), custom_call_target="tpu_custom_call" | custom-call | flops 2097152000 | bytes 20971520 | tf_op jit(solution)/shard_map/backward/pallas_call | solution.py:472
  81.7 1.8 %collective-permute-start.10 = (f32[88,128]{1,0:T(8,128)S(1)}, f32[88,128]{1,0:T(8,128)S(1)}, u32[]{:S(2)}, u32[]{:S(2)}) collective-permute-start(f32[88,128]{1,0:T(8,128)S(1)} %pad_maximum_fusion), channel_id=1, source_target_pairs={{0,8},{4,12},{8,0},{12,4},{16,24},{20,28},{24,16},{28,20},{1,9},{5... | collective-permute-start | bytes 135176 | tf_op jit(solution)/shard_map/ppermute | solution.py:517
  83.6 1.5 %collective-permute-start.11 = (f32[88,128]{1,0:T(8,128)S(1)}, f32[88,128]{1,0:T(8,128)S(1)}, u32[]{:S(2)}, u32[]{:S(2)}) collective-permute-start(f32[88,128]{1,0:T(8,128)S(1)} %pad_maximum_fusion), channel_id=1, source_target_pairs={{0,16},{4,20},{8,24},{12,28},{16,0},{20,4},{24,8},{28,12},{1,17},{... | collective-permute-start | bytes 135176 | tf_op jit(solution)/shard_map/ppermute | solution.py:517
  86.0 1.7 %collective-permute-done.11 = f32[88,128]{1,0:T(8,128)S(1)} collective-permute-done((f32[88,128]{1,0:T(8,128)S(1)}, f32[88,128]{1,0:T(8,128)S(1)}, u32[]{:S(2)}, u32[]{:S(2)}) %collective-permute-start.11) | collective-permute-done | bytes 45088 | tf_op jit(solution)/shard_map/ppermute | solution.py:517
  87.6 2.4 %collective-permute-done.12 = f32[88,128]{1,0:T(8,128)S(1)} collective-permute-done((f32[88,128]{1,0:T(8,128)S(1)}, f32[88,128]{1,0:T(8,128)S(1)}, u32[]{:S(2)}, u32[]{:S(2)}) %collective-permute-start.12) | collective-permute-done | bytes 45088 | tf_op jit(solution)/shard_map/ppermute | solution.py:517
  90.7 1.6 %collective-permute-start.13 = (f32[136,128]{1,0:T(8,128)S(1)}, f32[136,128]{1,0:T(8,128)S(1)}, u32[]{:S(2)}, u32[]{:S(2)}) collective-permute-start(f32[136,128]{1,0:T(8,128)S(1)} %constant_dynamic-update-slice_fusion.refs_0_), channel_id=1, source_target_pairs={{0,1},{1,0},{2,3},{3,2},{4,5},{5,4},{6,7},{7,6},{8,9},{9,8},{10,11... | collective-permute-start | bytes 208904 | tf_op jit(solution)/shard_map/ppermute | solution.py:517
  92.3 2.4 %collective-permute-start.14 = (f32[136,128]{1,0:T(8,128)S(1)}, f32[136,128]{1,0:T(8,128)S(1)}, u32[]{:S(2)}, u32[]{:S(2)}) collective-permute-start(f32[136,128]{1,0:T(8,128)S(1)} %constant_dynamic-update-slice_fusion.refs_0_), channel_id=1, source_target_pairs={{0,2},{1,3},{2,0},{3,1},{4,6},{5,7},{6,4},{7,5},{8,10},{9,11},{10,... | collective-permute-start | bytes 208904 | tf_op jit(solution)/shard_map/ppermute | solution.py:517
  95.8 3.2 %collective-permute-done.14.refs_2_ = f32[136,128]{1,0:T(8,128)S(1)} collective-permute-done((f32[136,128]{1,0:T(8,128)S(1)}, f32[136,128]{1,0:T(8,128)S(1)}, u32[]{:S(2)}, u32[]{:S(2)}) %collective-permute-start.14) | collective-permute-done | bytes 69664 | tf_op jit(solution)/shard_map/ppermute | solution.py:517
  99.0 1.8 %collective-permute-done.15.refs_3_ = f32[136,128]{1,0:T(8,128)S(1)} collective-permute-done((f32[136,128]{1,0:T(8,128)S(1)}, f32[136,128]{1,0:T(8,128)S(1)}, u32[]{:S(2)}, u32[]{:S(2)}) %collective-permute-start.15) | collective-permute-done | bytes 69664 | tf_op jit(solution)/shard_map/ppermute | solution.py:517
  (59 shorter events, 10.1 us)
Async XLA Ops:
  2.7 26.4 %copy-start = (bf16[768,256]{1,0:T(8,128)(2,1)S(1)}, bf16[768,256]{1,0:T(8,128)(2,1)}, u32[]{:S(2)}) copy-start(bf16[768,256]{1,0:T(8,128)(2,1)} %constant.29.clone.refs_4_.refs_5_.refs_6_) | copy-start | bytes 1179652
  2.7 26.4 %copy-start.4 = (f32[2,64,128]{2,1,0:T(8,128)S(1)}, f32[2,64,128]{2,1,0:T(8,128)}, u32[]{:S(2)}) copy-start(f32[2,64,128]{2,1,0:T(8,128)} %constant.28.clone.refs_3_.refs_4_.refs_5_) | copy-start | bytes 196612
  2.7 26.4 %copy-start.6 = (bf16[128,128]{1,0:T(8,128)(2,1)S(1)}, bf16[128,128]{1,0:T(8,128)(2,1)}, u32[]{:S(2)}) copy-start(bf16[128,128]{1,0:T(8,128)(2,1)} %constant.27.clone.refs_2_.refs_3_.refs_4_) | copy-start | bytes 98308
  5.7 23.3 %collective-permute-start.6 = (bf16[2,1,16,8192]{3,2,1,0:T(8,128)(2,1)}, bf16[2,1,16,8192]{3,2,1,0:T(8,128)(2,1)S(1)}, u32[]{:S(2)}, u32[]{:S(2)}) collective-permute-start(bf16[2,1,16,8192]{3,2,1,0:T(8,128)(2,1)} %get-tuple-element.35), channel_id=1, source_target_pairs={{0,4},{4,0},{8,12},{12,8},{16,20},{20,16},{24,28},{28,24},{1,5},{5... | collective-permute-start | bytes 1572872 | tf_op jit(solution)/shard_map/ppermute | solution.py:611
  6.3 27.9 %collective-permute-start.4 = (bf16[2,1,16,8192]{3,2,1,0:T(8,128)(2,1)}, bf16[2,1,16,8192]{3,2,1,0:T(8,128)(2,1)S(1)}, u32[]{:S(2)}, u32[]{:S(2)}) collective-permute-start(bf16[2,1,16,8192]{3,2,1,0:T(8,128)(2,1)} %get-tuple-element.28.refs_0_), channel_id=1, source_target_pairs={{0,24},{4,28},{8,16},{12,20},{16,8},{20,12},{24,0},{28,4},{1,25},{... | collective-permute-start | bytes 1572872 | tf_op jit(solution)/shard_map/ppermute | solution.py:611
  9.8 25.0 %collective-permute-start.5 = (bf16[2,1,16,8192]{3,2,1,0:T(8,128)(2,1)}, bf16[2,1,16,8192]{3,2,1,0:T(8,128)(2,1)S(1)}, u32[]{:S(2)}, u32[]{:S(2)}) collective-permute-start(bf16[2,1,16,8192]{3,2,1,0:T(8,128)(2,1)} %get-tuple-element.33), channel_id=1, source_target_pairs={{0,28},{4,24},{8,20},{12,16},{16,12},{20,8},{24,4},{28,0},{1,29},{... | collective-permute-start | bytes 1572872 | tf_op jit(solution)/shard_map/ppermute | solution.py:611
  9.8 36.0 %collective-permute-start.2 = (bf16[2,1,16,8192]{3,2,1,0:T(8,128)(2,1)}, bf16[2,1,16,8192]{3,2,1,0:T(8,128)(2,1)S(1)}, u32[]{:S(2)}, u32[]{:S(2)}) collective-permute-start(bf16[2,1,16,8192]{3,2,1,0:T(8,128)(2,1)} %get-tuple-element.31), channel_id=1, source_target_pairs={{0,8},{4,12},{8,0},{12,4},{16,24},{20,28},{24,16},{28,20},{1,9},{5... | collective-permute-start | bytes 1572872 | tf_op jit(solution)/shard_map/ppermute | solution.py:611
  11.5 34.4 %collective-permute-start.3 = (bf16[2,1,16,8192]{3,2,1,0:T(8,128)(2,1)}, bf16[2,1,16,8192]{3,2,1,0:T(8,128)(2,1)S(1)}, u32[]{:S(2)}, u32[]{:S(2)}) collective-permute-start(bf16[2,1,16,8192]{3,2,1,0:T(8,128)(2,1)} %get-tuple-element.32), channel_id=1, source_target_pairs={{0,16},{4,20},{8,24},{12,28},{16,0},{20,4},{24,8},{28,12},{1,17},{... | collective-permute-start | bytes 1572872 | tf_op jit(solution)/shard_map/ppermute | solution.py:611
  29.0 21.6 %collective-permute-start.7 = (bf16[2,1,8,8192]{3,2,1,0:T(8,128)(2,1)}, bf16[2,1,8,8192]{3,2,1,0:T(8,128)(2,1)S(1)}, u32[]{:S(2)}, u32[]{:S(2)}) collective-permute-start(bf16[2,1,8,8192]{3,2,1,0:T(8,128)(2,1)} %get-tuple-element.36), channel_id=1, source_target_pairs={{0,12},{4,8},{8,4},{12,0},{16,28},{20,24},{24,20},{28,16},{1,13},{... | collective-permute-start | bytes 786440 | tf_op jit(solution)/shard_map/ppermute | solution.py:611
  34.2 16.3 %collective-permute-start.8 = (bf16[2,1,8,8192]{3,2,1,0:T(8,128)(2,1)S(1)}, bf16[2,1,8,8192]{3,2,1,0:T(8,128)(2,1)S(1)}, u32[]{:S(2)}, u32[]{:S(2)}) collective-permute-start(bf16[2,1,8,8192]{3,2,1,0:T(8,128)(2,1)S(1)} %copy-done.13), channel_id=1, source_target_pairs={{0,20},{4,16},{8,28},{12,24},{16,4},{20,0},{24,12},{28,8},{1,21},{... | collective-permute-start | bytes 786440 | tf_op jit(solution)/shard_map/ppermute | solution.py:611
  34.8 21.2 %collective-permute-start = (bf16[2,1,8,8192]{3,2,1,0:T(8,128)(2,1)S(1)}, bf16[2,1,8,8192]{3,2,1,0:T(8,128)(2,1)S(1)}, u32[]{:S(2)}, u32[]{:S(2)}) collective-permute-start(bf16[2,1,8,8192]{3,2,1,0:T(8,128)(2,1)S(1)} %copy-done.12), channel_id=1, source_target_pairs={{0,12},{4,8},{8,4},{12,0},{16,28},{20,24},{24,20},{28,16},{1,13},{... | collective-permute-start | bytes 786440 | tf_op jit(solution)/shard_map/ppermute | solution.py:611
  45.8 10.3 %collective-permute-start.1 = (bf16[2,1,8,8192]{3,2,1,0:T(8,128)(2,1)S(1)}, bf16[2,1,8,8192]{3,2,1,0:T(8,128)(2,1)S(1)}, u32[]{:S(2)}, u32[]{:S(2)}) collective-permute-start(bf16[2,1,8,8192]{3,2,1,0:T(8,128)(2,1)S(1)} %copy-done.11), channel_id=1, source_target_pairs={{0,20},{4,16},{8,28},{12,24},{16,4},{20,0},{24,12},{28,8},{1,21},{... | collective-permute-start | bytes 786440 | tf_op jit(solution)/shard_map/ppermute | solution.py:611
  59.9 41.9 %all-to-all-start = ((f32[32,16,512]{2,1,0:T(8,128)}), f32[32,16,512]{2,1,0:T(8,128)S(1)}, u32[]{:S(2)}, u32[]{:S(2)}) async-start(f32[32,16,512]{2,1,0:T(8,128)} %correlate.9.lags_ref), calls=%async_computation | async-start | bytes 2097152 | tf_op jit(solution)/shard_map/all_to_all | solution.py:626
  66.0 34.9 %copy-start.2 = (f32[64,64]{1,0:T(8,128)S(1)}, f32[64,64]{1,0:T(8,128)}, u32[]{:S(2)}) copy-start(f32[64,64]{1,0:T(8,128)} %refs_6_.3) | copy-start | bytes 49156
  66.0 34.9 %copy-start.7 = (f32[64,33]{0,1:T(8,128)S(1)}, f32[64,33]{0,1:T(8,128)}, u32[]{:S(2)}) copy-start(f32[64,33]{0,1:T(8,128)} %param.32) | copy-start | bytes 25348
  66.0 34.9 %copy-start.8 = (f32[2,64]{1,0:T(2,128)S(1)}, f32[2,64]{1,0:T(2,128)}, u32[]{:S(2)}) copy-start(f32[2,64]{1,0:T(2,128)} %refs_7_.3) | copy-start | bytes 1540
  66.0 34.9 %copy-start.9 = (f32[64]{0:T(128)S(1)}, f32[64]{0:T(128)}, u32[]{:S(2)}) copy-start(f32[64]{0:T(128)} %param.33) | copy-start | bytes 772
  79.5 1.4 %collective-permute-start.9 = (f32[80,128]{1,0:T(8,128)}, f32[80,128]{1,0:T(8,128)S(1)}, u32[]{:S(2)}, u32[]{:S(2)}) collective-permute-start(f32[80,128]{1,0:T(8,128)} %backward.1), channel_id=1, source_target_pairs={{0,4},{4,0},{8,12},{12,8},{16,20},{20,16},{24,28},{28,24},{1,5},{5... | collective-permute-start | bytes 122888 | tf_op jit(solution)/shard_map/ppermute | solution.py:517
  81.7 4.2 %collective-permute-start.10 = (f32[88,128]{1,0:T(8,128)S(1)}, f32[88,128]{1,0:T(8,128)S(1)}, u32[]{:S(2)}, u32[]{:S(2)}) collective-permute-start(f32[88,128]{1,0:T(8,128)S(1)} %pad_maximum_fusion), channel_id=1, source_target_pairs={{0,8},{4,12},{8,0},{12,4},{16,24},{20,28},{24,16},{28,20},{1,9},{5... | collective-permute-start | bytes 135176 | tf_op jit(solution)/shard_map/ppermute | solution.py:517
  83.6 4.0 %collective-permute-start.11 = (f32[88,128]{1,0:T(8,128)S(1)}, f32[88,128]{1,0:T(8,128)S(1)}, u32[]{:S(2)}, u32[]{:S(2)}) collective-permute-start(f32[88,128]{1,0:T(8,128)S(1)} %pad_maximum_fusion), channel_id=1, source_target_pairs={{0,16},{4,20},{8,24},{12,28},{16,0},{20,4},{24,8},{28,12},{1,17},{... | collective-permute-start | bytes 135176 | tf_op jit(solution)/shard_map/ppermute | solution.py:517
  85.0 4.9 %collective-permute-start.12 = (f32[88,128]{1,0:T(8,128)S(1)}, f32[88,128]{1,0:T(8,128)S(1)}, u32[]{:S(2)}, u32[]{:S(2)}) collective-permute-start(f32[88,128]{1,0:T(8,128)S(1)} %pad_maximum_fusion), channel_id=1, source_target_pairs={{0,24},{4,28},{8,16},{12,20},{16,8},{20,12},{24,0},{28,4},{1,25},{... | collective-permute-start | bytes 135176 | tf_op jit(solution)/shard_map/ppermute | solution.py:517
  90.7 5.1 %collective-permute-start.13 = (f32[136,128]{1,0:T(8,128)S(1)}, f32[136,128]{1,0:T(8,128)S(1)}, u32[]{:S(2)}, u32[]{:S(2)}) collective-permute-start(f32[136,128]{1,0:T(8,128)S(1)} %constant_dynamic-update-slice_fusion.refs_0_), channel_id=1, source_target_pairs={{0,1},{1,0},{2,3},{3,2},{4,5},{5,4},{6,7},{7,6},{8,9},{9,8},{10,11... | collective-permute-start | bytes 208904 | tf_op jit(solution)/shard_map/ppermute | solution.py:517
  92.3 6.7 %collective-permute-start.14 = (f32[136,128]{1,0:T(8,128)S(1)}, f32[136,128]{1,0:T(8,128)S(1)}, u32[]{:S(2)}, u32[]{:S(2)}) collective-permute-start(f32[136,128]{1,0:T(8,128)S(1)} %constant_dynamic-update-slice_fusion.refs_0_), channel_id=1, source_target_pairs={{0,2},{1,3},{2,0},{3,1},{4,6},{5,7},{6,4},{7,5},{8,10},{9,11},{10,... | collective-permute-start | bytes 208904 | tf_op jit(solution)/shard_map/ppermute | solution.py:517
  94.7 6.1 %collective-permute-start.15 = (f32[136,128]{1,0:T(8,128)S(1)}, f32[136,128]{1,0:T(8,128)S(1)}, u32[]{:S(2)}, u32[]{:S(2)}) collective-permute-start(f32[136,128]{1,0:T(8,128)S(1)} %constant_dynamic-update-slice_fusion.refs_0_), channel_id=1, source_target_pairs={{0,3},{1,2},{2,1},{3,0},{4,7},{5,6},{6,5},{7,4},{8,11},{9,10},{10,... | collective-permute-start | bytes 208904 | tf_op jit(solution)/shard_map/ppermute | solution.py:517
  (7 other events, 35.0 us)

commit v6 on v5

--- a/solution.py
+++ b/solution.py
@@ -153,7 +153,7 @@
     refs = refs[lags:]
     first_ref, twist_ref, second_ref = refs[:3]
     if last:
-        untwist_ref, back_ref, last_ref, out_ref, lag_ref, cross_ref = refs[3:9]
+        untwist_ref, back_ref, last_ref, out_ref, other_ref, lag_ref, cross_ref = refs[3:10]
     else:
         out_ref = refs[3]
     turn_ref, high_ref, low_ref, spec_ref = refs[-4:]
@@ -249,6 +249,12 @@
                 out_ref[owner, :, pl.ds(k * LANES, LANES)] = lag_ref[
                     pl.ds(owner * wide_rows + k, channels, stride=2 * rows), :
                 ]
+        skip = (1 - (lax.axis_index("dp") & 1)) * (owners // 2 * wide_rows)
+        for owner in range(owners // 2):
+            for k in range(wide_rows):
+                other_ref[owner, :, pl.ds(k * LANES, LANES)] = lag_ref[
+                    pl.ds(skip + owner * wide_rows + k, channels, stride=2 * rows), :
+                ]
 
 
 def correlate(pieces, held, scale, owners, lags=None, chunk=0, chunks=1):
@@ -271,10 +277,16 @@
     ]
     if owners:
         shape = (owners, channels * chunks, total // owners)
-        out_spec = pl.BlockSpec((owners, channels, total // owners), lambda c: (0, chunk, 0))
+        part = (owners // 2, channels, total // owners)
+        out_spec = [
+            pl.BlockSpec((owners, channels, total // owners), lambda c: (0, chunk, 0)),
+            pl.BlockSpec(part, lambda c: (0, 0, 0)),
+        ]
+        out_shape = [jax.ShapeDtypeStruct(shape, F32), jax.ShapeDtypeStruct(part, F32)]
     else:
         shape = (channels, rows, 2 * lanes)
         out_spec = spectrum
+        out_shape = jax.ShapeDtypeStruct(shape, F32)
     scratch = []
     if owners:
         scratch = [
@@ -302,7 +314,7 @@
         + whole,
         input_output_aliases={len(pieces) + len(held): 0} if lags else {},
         out_specs=out_spec,
-        out_shape=jax.ShapeDtypeStruct(shape, F32),
+        out_shape=out_shape,
         scratch_shapes=scratch,
         cost_estimate=pl.CostEstimate(
             flops=channels * seqs * 2 * rows * lanes * lanes * 36,
@@ -318,9 +330,8 @@
 BANDS_PAD = 8
 
 
-def lag_row(step, total):
-    position = step * STEP + lax.broadcasted_iota(jnp.int32, (1, STEP), 1)
-    return jnp.where(position < total // 2, position, position - total)
+def lag_row(step, second, total):
+    return step * STEP + lax.broadcasted_iota(jnp.int32, (1, STEP), 1) - second * (total // 2)
 
 
 def network_kernel(
@@ -347,7 +358,7 @@
         for k in range(2):
             freq_cols[k] = column(freq_ref[k : k + 1, :])
 
-    lag = lag_row(step, total)
+    lag = lag_row(step, lax.axis_index("dp") & 1, total)
     length = total // 2
     phase = ((factor_ref[...] * lag) & (total - 1)).astype(F32) * (2.0 * math.pi / total)
     sine, cosine = sine_cosine(phase)
@@ -376,10 +387,10 @@
     heights = ((2 * depth, BF16), (2 * hidden, BF16), (2 * hidden, BF16), (hidden, F32), (hidden, F32))
     return pl.pallas_call(
         functools.partial(network_kernel, total=total),
-        grid=(total // STEP,),
+        grid=(total // 2 // STEP,),
         in_specs=whole,
         out_specs=[pl.BlockSpec((h, STEP), lambda i: (0, i)) for h, _ in heights],
-        out_shape=[jax.ShapeDtypeStruct((h, total), t) for h, t in heights],
+        out_shape=[jax.ShapeDtypeStruct((h, total // 2), t) for h, t in heights],
         scratch_shapes=[
             pltpu.VMEM((hidden, 3 * depth), BF16),
             pltpu.VMEM((hidden, 3 * hidden), BF16),
@@ -392,31 +403,45 @@
     )(*args)
 
 
-def backward_kernel(
-    first_ref, lags_ref, table_ref, layer1_ref, layer2_ref, cos1_ref, cos2_ref,
+def backward_kernel(place_ref, second_ref, lags_ref, *refs, others, total, pack):
+    other_refs, refs = refs[:others], refs[others:]
+    backward_body(place_ref, second_ref, lags_ref, other_refs, *refs, total=total, pack=pack)
+
+
+def backward_body(
+    place_ref, second_ref, lags_ref, other_refs, table_ref, layer1_ref, layer2_ref, cos1_ref, cos2_ref,
     decay_ref, output_ref, hidden_ref, freq_ref,
     out_ref, output_parts, hidden_parts, decay_col, own_ref, sum1_ref, sum3_ref, sum5_ref, *, total, pack,
 ):
     step = pl.program_id(0)
     owners, own, _ = lags_ref.shape
+    own = 2 * own
     hidden = hidden_ref.shape[0]
+    first, second_of_pair = place_ref[0], second_ref[0]
 
     @pl.when(step == 0)
     def _():
         for ref in (sum1_ref, sum3_ref, sum5_ref):
             ref[...] = jnp.zeros_like(ref)
         channels = output_ref.shape[1]
-        own_ref[...] = pltpu.roll(output_ref[...], channels - first_ref[0], 1)[:, :own]
+        own_ref[...] = pltpu.roll(output_ref[...], channels - first, 1)[:, :own]
         output_parts[...] = narrow(own_ref[...], 1)
         hidden_parts[...] = narrow((hidden_ref[...] * column(freq_ref[1:2, :])).T, 1)
         place = [lax.broadcasted_iota(jnp.int32, (own, channels), d) for d in (0, 1)]
         decay_col[...] = jnp.sum(
-            jnp.where(place[1] == place[0] + first_ref[0], decay_ref[...], 0.0), axis=1, keepdims=True
+            jnp.where(place[1] == place[0] + first, decay_ref[...], 0.0), axis=1, keepdims=True
         )
 
-    lags = jnp.concatenate([lags_ref[k] for k in range(owners)], axis=1)
+    mine = jnp.concatenate([lags_ref[k] for k in range(owners)], axis=1)
+    others = jnp.concatenate(
+        [jnp.concatenate([ref[k] for k in range(owners)], axis=1) for ref in other_refs], axis=0
+    )
+    upper = second_of_pair != 0
+    lags = jnp.concatenate(
+        [jnp.where(upper, others, mine), jnp.where(upper, mine, others)], axis=0
+    )
     length = total // 2
-    distance = jnp.abs(lag_row(step, total)).astype(F32)
+    distance = jnp.abs(lag_row(step, second_of_pair, total)).astype(F32)
     window = jnp.exp(-decay_col[...] * distance / length)
     shaped = lags * window * (1.0 / math.sqrt(total))
     far = shaped * (distance / length)
@@ -424,8 +449,8 @@
     second = dot(output_parts[...], wide(shaped, 0)) * cos2_ref[...]
     high, low = split(second)
     sum3_ref[...] += dot_lanes(jnp.concatenate([high, low], axis=0), layer1_ref[...])
-    first = dot(hidden_parts[...], jnp.concatenate([high, high, low], axis=0)) * cos1_ref[...]
-    sum5_ref[...] += dot_lanes(stacked(first, 0), table_ref[...])
+    below = dot(hidden_parts[...], jnp.concatenate([high, high, low], axis=0)) * cos1_ref[...]
+    sum5_ref[...] += dot_lanes(stacked(below, 0), table_ref[...])
 
     @pl.when(step == pl.num_programs(0) - 1)
     def _():
@@ -441,7 +466,7 @@
         decay_grad = -jnp.sum(own_ref[...].T * sums[own:], axis=1, keepdims=True)
         height = out_ref.shape[0] - hidden - own // pack
         place = lax.broadcasted_iota(jnp.int32, (height, LANES), 0) * LANES
-        place = place + lax.broadcasted_iota(jnp.int32, (height, LANES), 1) - first_ref[0]
+        place = place + lax.broadcasted_iota(jnp.int32, (height, LANES), 1) - first
         decays = jnp.zeros((height, LANES), F32)
         for c in range(own):
             decays = jnp.where(place == c, decay_grad[c : c + 1], decays)
@@ -460,22 +485,29 @@
     return hidden + -(-channels // (8 * LANES)) * 8
 
 
-def backward(first_own, lags, saved, decay_rate, output_weight, hidden_weight, frequency, total):
+def backward(first, second, lags, others, saved, decay_rate, output_weight, hidden_weight, frequency, total):
     _, own, lag_count = lags.shape
+    own = 2 * own
     hidden = hidden_weight.shape[0]
     pack = packing(own, hidden)
     height = summed_rows(hidden, decay_rate.shape[0]) + own // pack
+    steps = total // 2 // STEP
     args = (decay_rate[None], output_weight.T, hidden_weight, frequency)
-    specs = [pl.BlockSpec((STEP // lag_count, own, lag_count), lambda i, first: (i, 0, 0))]
-    specs += [pl.BlockSpec((a.shape[0], STEP), lambda i, first: (0, i)) for a in saved]
-    specs += [pl.BlockSpec(a.shape, lambda i, first: (0, 0)) for a in args]
+    specs = [
+        pl.BlockSpec((STEP // lag_count, own // 2, lag_count), lambda i, at, second: (i + second[0] * steps, 0, 0))
+    ]
+    specs += [
+        pl.BlockSpec((STEP // lag_count, *a.shape[1:]), lambda i, at, second: (i, 0, 0)) for a in others
+    ]
+    specs += [pl.BlockSpec((a.shape[0], STEP), lambda i, at, second: (0, i)) for a in saved]
+    specs += [pl.BlockSpec(a.shape, lambda i, at, second: (0, 0)) for a in args]
     return pl.pallas_call(
-        functools.partial(backward_kernel, total=total, pack=pack),
+        functools.partial(backward_kernel, others=len(others), total=total, pack=pack),
         grid_spec=pltpu.PrefetchScalarGridSpec(
-            num_scalar_prefetch=1,
-            grid=(total // STEP,),
+            num_scalar_prefetch=2,
+            grid=(steps,),
             in_specs=specs,
-            out_specs=pl.BlockSpec((height, LANES), lambda i, first: (0, 0)),
+            out_specs=pl.BlockSpec((height, LANES), lambda i, at, second: (0, 0)),
             scratch_shapes=[
                 pltpu.VMEM((hidden, 3 * own), BF16),
                 pltpu.VMEM((hidden, 3 * hidden), BF16),
@@ -488,18 +520,17 @@
         ),
         out_shape=jax.ShapeDtypeStruct((height, LANES), F32),
         cost_estimate=pl.CostEstimate(
-            flops=total * hidden * 2000, bytes_accessed=total * hidden * 20, transcendentals=0
+            flops=total * hidden * 1000, bytes_accessed=total * hidden * 10, transcendentals=0
         ),
         name="backward",
-    )(first_own.reshape(1), lags, *saved, *args)
+    )(first.reshape(1), second.reshape(1), lags, *others, *saved, *args)
 
 
 def rounds():
     steps = []
     for axis in ("dp", "chan"):
         bits = [1 << b for b in range(lax.axis_size(axis).bit_length() - 1)]
-        alone = 1 if axis == "dp" else 0
-        for group in [bits[:alone]] + [bits[b : b + 2] for b in range(alone, len(bits), 2)]:
+        for group in [bits[b : b + 2] for b in range(axis == "dp", len(bits), 2)]:
             masks = [0]
             for bit in group:
                 masks += [mask | bit for mask in masks]
@@ -510,6 +541,8 @@
 
 def share(both, summed):
     steps = rounds()
+    size = lax.axis_size("dp")
+    both = both + lax.ppermute(both, "dp", [(i, i ^ 1) for i in range(size)])
     for axis, masks in steps:
         size = lax.axis_size(axis)
         parts = [both]
@@ -540,7 +573,7 @@
         for axis, masks in steps:
             there[axis] = there[axis] ^ masks[rest % len(masks)]
             rest //= len(masks)
-        place = there["chan"] * lax.axis_size("dp") + there["dp"]
+        place = there["chan"] * (lax.axis_size("dp") // 2) + (there["dp"] >> 1)
         for n in range(pack):
             rows_ref[pl.ds(pl.multiple_of(place * own + n * unit, unit), unit), :] = part_refs[
                 k // each
@@ -616,24 +649,25 @@
         spectrum = correlate(
             [pieces[p, 0] for p in soon[at : at + step]], spectrum, scale, count if end else 0
         )
-    lags = spectrum
+    lags, others = (None, []) if late else (spectrum[0], [spectrum[1]])
     for q in range(chunks if late else 0):
-        lags = correlate(
-            [pieces[p, q * per] for p in late], spectrum, scale, count, lags if q else None, q, chunks
+        lags, other = correlate(
+            [pieces[p, q * per] for p in late], spectrum, scale, count, lags, q, chunks
         )
+        others.append(other)
+    for q, other in enumerate(others):
+        others[q] = lax.ppermute(other, "dp", [(i, i ^ 1) for i in range(dp)])
 
     saved = network(embed_weight, embed_bias, hidden_weight, frequency, total)
     shared = lax.all_to_all(lags, ("dp", "chan"), 0, 0, tiled=True)
-    first_own = at_chan * chan_local + at_dp * own
-    both = backward(
-        first_own, lags, saved, decay_rate, output_weight, hidden_weight, frequency, total
-    )
+    first = at_chan * chan_local + (at_dp & -2) * own
+    both = backward(first, at_dp & 1, lags, others, saved, decay_rate, output_weight, hidden_weight, frequency, total)
     parts = share(both, summed_rows(hidden, channels))
     filter_grad = jnp.swapaxes(shared.reshape(dp, chan, own, -1), 0, 1)
     filter_grad = filter_grad.reshape(channels, -1)
     return (
         filter_grad,
-        *finish(parts, embed_weight, embed_bias, hidden_weight, frequency, channels, own),
+        *finish(parts, embed_weight, embed_bias, hidden_weight, frequency, channels, 2 * own),
     )
 
 

time: 104 us -> 108 us (1.038)
  waiting for transfers between devices: 19 us -> 34.7 us
  Pallas kernels: 55.1 us -> 43.3 us
    ppermute x9, waiting for transfers between devices: 8.06 us -> 23.1 us  [work(): pieces[p, start] = lax.ppermute(sent, 'dp', swap) if p else sent]
    pallas_call x1, Pallas kernels: 16 us -> 8.93 us  [network(): pl.pallas_call(functools.partial(network_kernel, total=total), grid=(tota...]
    pallas_call x1, Pallas kernels: 13.5 us -> 8.3 us  [backward(): pl.pallas_call(functools.partial(backward_kernel, others=len(others), tot...]
    ppermute x0 -> x3, waiting for transfers between devices: none -> 1.36 us  [the longest x1 1.35 us: share(): both = both + lax.ppermute(both, 'dp', [(i, i ^ 1) for i in range(size)])]
    ppermute x7 -> x6, waiting for transfers between devices: 10.9 us -> 10.2 us  [share(): parts.append(lax.ppermute(both, axis, [(i, i ^ mask) for i in range(size)]))]
    ppermute x7 -> x6, starting transfers between devices: 8.24 us -> 7.94 us  [share(): parts.append(lax.ppermute(both, axis, [(i, i ^ mask) for i in range(size)]))]
  transfers between devices with their start and end apart: 17 -> 19, of which waited for: 11 -> 13; matrix products, arithmetic and copies ran while one was open for 2% -> 1% of each run, Pallas kernels for 45% -> 32%
where the time goes in v6:
time: 108 us; the launch traced here: 107 us
  Pallas kernels  43.3 us (40%)
  waiting for transfers between devices  34.7 us (32%)
  starting transfers between devices  24.6 us (23%)
  local copies, waits for them, and re-layouts  2.99 us (3%)
    ppermute x9, waiting for transfers between devices, work(): pieces[p, start] = lax.ppermute(sent, 'dp', swap) if p else sent  23.1 us
    pallas_call x5, Pallas kernels, correlate(): pl.pallas_call(functools.partial(correlate_kernel, pieces=len(pieces), he...  20.1 us
    ppermute x6, waiting for transfers between devices, share(): parts.append(lax.ppermute(both, axis, [(i, i ^ mask) for i in range(size)]))  10.2 us
    ppermute x9, starting transfers between devices, work(): pieces[p, start] = lax.ppermute(sent, 'dp', swap) if p else sent  9.8 us
    pallas_call x1, Pallas kernels, network(): pl.pallas_call(functools.partial(network_kernel, total=total), grid=(tota...  8.93 us
    pallas_call x1, Pallas kernels, backward(): pl.pallas_call(functools.partial(backward_kernel, others=len(others), tot...  8.3 us
    ppermute x6, starting transfers between devices, share(): parts.append(lax.ppermute(both, axis, [(i, i ^ mask) for i in range(size)]))  7.94 us
    all_to_all x1, starting transfers between devices, work(): shared = lax.all_to_all(lags, ('dp', 'chan'), 0, 0, tiled=True)  6.22 us
  transfers between devices with their start and end apart: 19, of which 13 were waited for; matrix products, arithmetic and copies ran while one was open for 1% of the time, Pallas kernels for 32%

profile of v6, /device:TPU:0, one launch (start us, length us, event | category | flops | bytes accessed | tf_op | source)
XLA Modules:
  0.0 107.3 jit_solution(2571764635380387754)
XLA Ops:
  0.6 2.0 %pick.2 = (bf16[2,1,16,8192]{3,2,1,0:T(8,128)(2,1)}, bf16[2,1,16,8192]{3,2,1,0:T(8,128)(2,1)}) custom-call(bf16[1,128,8192]{2,1,0:T(8,128)(2,1)} %x_ref.3, bf16[1,128,8192]{2,1,0:T(8,128)(2,1)} %g_ref.3), custom_call_target="tpu_custom_call" | custom-call | bytes 2097152 | tf_op jit(solution)/shard_map/pick/pallas_call | solution.py:133
  2.7 3.0 %pick.3 = (bf16[2,1,16,8192]{3,2,1,0:T(8,128)(2,1)}, bf16[2,1,16,8192]{3,2,1,0:T(8,128)(2,1)}, bf16[2,1,16,8192]{3,2,1,0:T(8,128)(2,1)}, bf16[2,1,16,8192]{3,2,1...) custom-call(bf16[1,128,8192]{2,1,0:T(8,128)(2,1)} %x_ref.3, ...), custom_call_target="tpu_custom_call" | custom-call | bytes 6291456 | tf_op jit(solution)/shard_map/pick/pallas_call | solution.py:133
  6.3 3.5 %collective-permute-start.4 = (bf16[2,1,16,8192]{3,2,1,0:T(8,128)(2,1)S(1)}, bf16[2,1,16,8192]{3,2,1,0:T(8,128)(2,1)S(1)}, u32[]{:S(2)}, u32[]{:S(2)}) collective-permute-start(bf16[2,1,16,8192]{3,2,1,0:T(8,128)(2,1)S(1)} %copy-done.11), channel_id=1, source_target_pairs={{0,24},{4,28},{8,16},{12,20},{16,8},{20,12},{24,0},{28,4},{1,25},{... | collective-permute-start | bytes 1572872 | tf_op jit(solution)/shard_map/ppermute | solution.py:644
  9.9 1.6 %collective-permute-start.2 = (bf16[2,1,16,8192]{3,2,1,0:T(8,128)(2,1)}, bf16[2,1,16,8192]{3,2,1,0:T(8,128)(2,1)S(1)}, u32[]{:S(2)}, u32[]{:S(2)}) collective-permute-start(bf16[2,1,16,8192]{3,2,1,0:T(8,128)(2,1)} %get-tuple-element.35), channel_id=1, source_target_pairs={{0,8},{4,12},{8,0},{12,4},{16,24},{20,28},{24,16},{28,20},{1,9},{5... | collective-permute-start | bytes 1572872 | tf_op jit(solution)/shard_map/ppermute | solution.py:644
  11.6 1.5 %collective-permute-start.3 = (bf16[2,1,16,8192]{3,2,1,0:T(8,128)(2,1)}, bf16[2,1,16,8192]{3,2,1,0:T(8,128)(2,1)S(1)}, u32[]{:S(2)}, u32[]{:S(2)}) collective-permute-start(bf16[2,1,16,8192]{3,2,1,0:T(8,128)(2,1)} %get-tuple-element.36), channel_id=1, source_target_pairs={{0,16},{4,20},{8,24},{12,28},{16,0},{20,4},{24,8},{28,12},{1,17},{... | collective-permute-start | bytes 1572872 | tf_op jit(solution)/shard_map/ppermute | solution.py:644
  14.2 4.0 %correlate.5.refs_2_ = f32[16,64,256]{2,1,0:T(8,128)S(1)} custom-call(bf16[2,1,16,8192]{3,2,1,0:T(8,128)(2,1)S(1)} %copy-done.4, bf16[2,1,16,8192]{3,2,1,0:T(8,128)(2,1)S(1)} %collective-permute-done.6.refs_1_, bf16[128,128]{1,0:T(8,128)(2,1)S(1)} %copy-done.10, f32[2,64,128]{2,1,0:T(8,128)S(1)} %copy-done.8, bf16[768,256]{1,0:T(8,128)(2,1)S(1)} %copy-done.5), custom_call_target="tpu_custom_call" | custom-call | flops 2415919104 | bytes 2097152 | tf_op jit(solution)/shard_map/correlate/pallas_call | solution.py:302
  18.2 4.5 %collective-permute-done.4.refs_0_ = bf16[2,1,16,8192]{3,2,1,0:T(8,128)(2,1)S(1)} collective-permute-done((bf16[2,1,16,8192]{3,2,1,0:T(8,128)(2,1)S(1)}, bf16[2,1,16,8192]{3,2,1,0:T(8,128)(2,1)S(1)}, u32[]{:S(2)}, u32[]{:S(2)}) %collective-permute-start.4) | collective-permute-done | bytes 524320 | tf_op jit(solution)/shard_map/ppermute | solution.py:644
  23.3 10.2 %collective-permute-done.5.refs_1_ = bf16[2,1,16,8192]{3,2,1,0:T(8,128)(2,1)S(1)} collective-permute-done((bf16[2,1,16,8192]{3,2,1,0:T(8,128)(2,1)S(1)}, bf16[2,1,16,8192]{3,2,1,0:T(8,128)(2,1)S(1)}, u32[]{:S(2)}, u32[]{:S(2)}) %collective-permute-start.5) | collective-permute-done | bytes 524320 | tf_op jit(solution)/shard_map/ppermute | solution.py:644
  33.4 1.9 %collective-permute-start = (bf16[2,1,8,8192]{3,2,1,0:T(8,128)(2,1)S(1)}, bf16[2,1,8,8192]{3,2,1,0:T(8,128)(2,1)S(1)}, u32[]{:S(2)}, u32[]{:S(2)}) collective-permute-start(bf16[2,1,8,8192]{3,2,1,0:T(8,128)(2,1)S(1)} %copy-done.16), channel_id=1, source_target_pairs={{0,12},{4,8},{8,4},{12,0},{16,28},{20,24},{24,20},{28,16},{1,13},{... | collective-permute-start | bytes 786440 | tf_op jit(solution)/shard_map/ppermute | solution.py:644
  35.3 4.0 %correlate.6.refs_2_ = f32[16,64,256]{2,1,0:T(8,128)S(1)} custom-call(bf16[2,1,16,8192]{3,2,1,0:T(8,128)(2,1)S(1)} %collective-permute-done.4.refs_0_, bf16[2,1,16,8192]{3,2,1,0:T(8,128)(2,1)S(1)} %collective-permute-done.5.refs_1_, f32[16,64,256]{2,1,0:T(8,128)S(1)} %correlate.5.refs_2_, bf16[128,128]{1,0:T(8,128)(2,1)S(1)} %copy-done.10, ...), custom_call_target="tpu_custom_call" | custom-call | flops 2415919104 | bytes 2097152 | tf_op jit(solution)/shard_map/correlate/pallas_call | solution.py:302
  39.3 6.3 %collective-permute-done.2.refs_0_ = bf16[2,1,16,8192]{3,2,1,0:T(8,128)(2,1)S(1)} collective-permute-done((bf16[2,1,16,8192]{3,2,1,0:T(8,128)(2,1)}, bf16[2,1,16,8192]{3,2,1,0:T(8,128)(2,1)S(1)}, u32[]{:S(2)}, u32[]{:S(2)}) %collective-permute-start.2) | collective-permute-done | bytes 524320 | tf_op jit(solution)/shard_map/ppermute | solution.py:644
  45.8 4.0 %correlate.7.refs_2_ = f32[16,64,256]{2,1,0:T(8,128)S(1)} custom-call(bf16[2,1,16,8192]{3,2,1,0:T(8,128)(2,1)S(1)} %collective-permute-done.2.refs_0_, bf16[2,1,16,8192]{3,2,1,0:T(8,128)(2,1)S(1)} %collective-permute-done.3.refs_1_, f32[16,64,256]{2,1,0:T(8,128)S(1)} %correlate.6.refs_2_, bf16[128,128]{1,0:T(8,128)(2,1)S(1)} %copy-done.10, ...), custom_call_target="tpu_custom_call" | custom-call | flops 2415919104 | bytes 2097152 | tf_op jit(solution)/shard_map/correlate/pallas_call | solution.py:302
  50.4 4.0 %correlate.8 = (f32[32,16,512]{2,1,0:T(8,128)}, f32[16,8,512]{2,1,0:T(8,128)S(1)}) custom-call(bf16[2,1,8,8192]{3,2,1,0:T(8,128)(2,1)S(1)} %collective-permute-done.7.refs_0_, bf16[2,1,8,8192]{3,2,1,0:T(8,128)(2,1)S(1)} %collective-permute-done.8.refs_1_, f32[16,64,256]{2,1,0:T(8,128)S(1)} %correlate.7.refs_2_, bf16[128,128]{1,0:T(8,128)(2,1)S(1)} %copy-done.10, ...), custom_call_target="tpu_custom_call" | custom-call | flops 1207959552 | bytes 1048576 | tf_op jit(solution)/shard_map/correlate/pallas_call | solution.py:302
  56.0 4.0 %correlate.9 = (f32[32,16,512]{2,1,0:T(8,128)}, f32[16,8,512]{2,1,0:T(8,128)S(1)}) custom-call(bf16[2,1,8,8192]{3,2,1,0:T(8,128)(2,1)S(1)} %collective-permute-done.refs_0_, bf16[2,1,8,8192]{3,2,1,0:T(8,128)(2,1)S(1)} %collective-permute-done.1.refs_1_, f32[16,64,256]{2,1,0:T(8,128)S(1)} %correlate.7.refs_2_, ...), custom_call_target="tpu_custom_call", output_to_operand_aliasing={{0}: (3, {})} | custom-call | flops 1207959552 | bytes 1048576 | tf_op jit(solution)/shard_map/correlate/pallas_call | solution.py:302
  60.0 6.2 %all-to-all-start = ((f32[32,16,512]{2,1,0:T(8,128)}), f32[32,16,512]{2,1,0:T(8,128)S(1)}, u32[]{:S(2)}, u32[]{:S(2)}) async-start(f32[32,16,512]{2,1,0:T(8,128)} %get-tuple-element.43.lags_ref), calls=%async_computation | async-start | bytes 2097152 | tf_op jit(solution)/shard_map/all_to_all | solution.py:662
  66.8 8.9 %network.1 = (bf16[80,8192]{1,0:T(8,128)(2,1)}, bf16[128,8192]{1,0:T(8,128)(2,1)}, bf16[128,8192]{1,0:T(8,128)(2,1)}, f32[64,8192]{1,0:T(8,128)}, f32[64,8192]{1,0:T(8,128)}) custom-call(s32[16,1]{1,0:T(8,128)} %constant.37.clone.factor_ref, f32[33,64]{1,0:T(8,128)} %bitcast.14, f32[1,64]{1,0:T(1,128)} %bitcast.16, f32[64,64]{1,0:T(8,128)} %refs_6_.3, ...), custom_call_target="tpu_custom_call" | custom-call | flops 629145600 | bytes 20971520 | tf_op jit(solution)/shard_map/network/pallas_call | solution.py:388
  76.5 8.3 %backward.1 = f32[88,128]{1,0:T(8,128)} custom-call(s32[1]{0:T(128)} %bitcast.3.place_ref, s32[1]{0:T(128)} %bitcast.4.second_ref, f32[32,16,512]{2,1,0:T(8,128)} %get-tuple-element.43.lags_ref, f32[16,8,512]{2,1,0:T(8,128)} %copy-done.13, f32[16,8,512]{2,1,0:T(8,128)} %copy-done.12, bf16[80,8192]{1,0:T(8,128)(2,1)} %get-tuple-element.46.refs_2_, ...), custom_call_target="tpu_custom_call" | custom-call | flops 1048576000 | bytes 10485760 | tf_op jit(solution)/shard_map/backward/pallas_call | solution.py:504
  87.1 1.6 %collective-permute-start.12 = (f32[88,128]{1,0:T(8,128)S(1)}, f32[88,128]{1,0:T(8,128)S(1)}, u32[]{:S(2)}, u32[]{:S(2)}) collective-permute-start(f32[88,128]{1,0:T(8,128)S(1)} %add.16), channel_id=1, source_target_pairs={{0,8},{4,12},{8,0},{12,4},{16,24},{20,28},{24,16},{28,20},{1,9},{5... | collective-permute-start | bytes 135176 | tf_op jit(solution)/shard_map/ppermute | solution.py:550
  88.6 1.5 %collective-permute-start.13 = (f32[88,128]{1,0:T(8,128)S(1)}, f32[88,128]{1,0:T(8,128)S(1)}, u32[]{:S(2)}, u32[]{:S(2)}) collective-permute-start(f32[88,128]{1,0:T(8,128)S(1)} %add.16), channel_id=1, source_target_pairs={{0,16},{4,20},{8,24},{12,28},{16,0},{20,4},{24,8},{28,12},{1,17},{... | collective-permute-start | bytes 135176 | tf_op jit(solution)/shard_map/ppermute | solution.py:550
  92.7 2.4 %collective-permute-done.14 = f32[88,128]{1,0:T(8,128)S(1)} collective-permute-done((f32[88,128]{1,0:T(8,128)S(1)}, f32[88,128]{1,0:T(8,128)S(1)}, u32[]{:S(2)}, u32[]{:S(2)}) %collective-permute-start.14) | collective-permute-done | bytes 45088 | tf_op jit(solution)/shard_map/ppermute | solution.py:550
  95.1 1.5 %collective-permute-start.15 = (f32[136,128]{1,0:T(8,128)S(1)}, f32[136,128]{1,0:T(8,128)S(1)}, u32[]{:S(2)}, u32[]{:S(2)}) collective-permute-start(f32[136,128]{1,0:T(8,128)S(1)} %constant_dynamic-update-slice_fusion.refs_0_), channel_id=1, source_target_pairs={{0,1},{1,0},{2,3},{3,2},{4,5},{5,4},{6,7},{7,6},{8,9},{9,8},{10,11... | collective-permute-start | bytes 208904 | tf_op jit(solution)/shard_map/ppermute | solution.py:550
  96.7 2.5 %collective-permute-start.16 = (f32[136,128]{1,0:T(8,128)S(1)}, f32[136,128]{1,0:T(8,128)S(1)}, u32[]{:S(2)}, u32[]{:S(2)}) collective-permute-start(f32[136,128]{1,0:T(8,128)S(1)} %constant_dynamic-update-slice_fusion.refs_0_), channel_id=1, source_target_pairs={{0,2},{1,3},{2,0},{3,1},{4,6},{5,7},{6,4},{7,5},{8,10},{9,11},{10,... | collective-permute-start | bytes 208904 | tf_op jit(solution)/shard_map/ppermute | solution.py:550
  99.7 3.7 %collective-permute-done.16.refs_2_ = f32[136,128]{1,0:T(8,128)S(1)} collective-permute-done((f32[136,128]{1,0:T(8,128)S(1)}, f32[136,128]{1,0:T(8,128)S(1)}, u32[]{:S(2)}, u32[]{:S(2)}) %collective-permute-start.16) | collective-permute-done | bytes 69664 | tf_op jit(solution)/shard_map/ppermute | solution.py:550
  103.4 1.9 %collective-permute-done.17.refs_3_ = f32[136,128]{1,0:T(8,128)S(1)} collective-permute-done((f32[136,128]{1,0:T(8,128)S(1)}, f32[136,128]{1,0:T(8,128)S(1)}, u32[]{:S(2)}, u32[]{:S(2)}) %collective-permute-start.17) | collective-permute-done | bytes 69664 | tf_op jit(solution)/shard_map/ppermute | solution.py:550
  (67 shorter events, 13.3 us)
Async XLA Ops:
  5.8 7.3 %collective-permute-start.6 = (bf16[2,1,16,8192]{3,2,1,0:T(8,128)(2,1)}, bf16[2,1,16,8192]{3,2,1,0:T(8,128)(2,1)S(1)}, u32[]{:S(2)}, u32[]{:S(2)}) collective-permute-start(bf16[2,1,16,8192]{3,2,1,0:T(8,128)(2,1)} %get-tuple-element.39), channel_id=1, source_target_pairs={{0,4},{4,0},{8,12},{12,8},{16,20},{20,16},{24,28},{28,24},{1,5},{5... | collective-permute-start | bytes 1572872 | tf_op jit(solution)/shard_map/ppermute | solution.py:644
  6.3 16.4 %collective-permute-start.4 = (bf16[2,1,16,8192]{3,2,1,0:T(8,128)(2,1)S(1)}, bf16[2,1,16,8192]{3,2,1,0:T(8,128)(2,1)S(1)}, u32[]{:S(2)}, u32[]{:S(2)}) collective-permute-start(bf16[2,1,16,8192]{3,2,1,0:T(8,128)(2,1)S(1)} %copy-done.11), channel_id=1, source_target_pairs={{0,24},{4,28},{8,16},{12,20},{16,8},{20,12},{24,0},{28,4},{1,25},{... | collective-permute-start | bytes 1572872 | tf_op jit(solution)/shard_map/ppermute | solution.py:644
  9.8 23.6 %collective-permute-start.5 = (bf16[2,1,16,8192]{3,2,1,0:T(8,128)(2,1)S(1)}, bf16[2,1,16,8192]{3,2,1,0:T(8,128)(2,1)S(1)}, u32[]{:S(2)}, u32[]{:S(2)}) collective-permute-start(bf16[2,1,16,8192]{3,2,1,0:T(8,128)(2,1)S(1)} %copy-done.14), channel_id=1, source_target_pairs={{0,28},{4,24},{8,20},{12,16},{16,12},{20,8},{24,4},{28,0},{1,29},{... | collective-permute-start | bytes 1572872 | tf_op jit(solution)/shard_map/ppermute | solution.py:644
  9.9 35.7 %collective-permute-start.2 = (bf16[2,1,16,8192]{3,2,1,0:T(8,128)(2,1)}, bf16[2,1,16,8192]{3,2,1,0:T(8,128)(2,1)S(1)}, u32[]{:S(2)}, u32[]{:S(2)}) collective-permute-start(bf16[2,1,16,8192]{3,2,1,0:T(8,128)(2,1)} %get-tuple-element.35), channel_id=1, source_target_pairs={{0,8},{4,12},{8,0},{12,4},{16,24},{20,28},{24,16},{28,20},{1,9},{5... | collective-permute-start | bytes 1572872 | tf_op jit(solution)/shard_map/ppermute | solution.py:644
  11.6 34.2 %collective-permute-start.3 = (bf16[2,1,16,8192]{3,2,1,0:T(8,128)(2,1)}, bf16[2,1,16,8192]{3,2,1,0:T(8,128)(2,1)S(1)}, u32[]{:S(2)}, u32[]{:S(2)}) collective-permute-start(bf16[2,1,16,8192]{3,2,1,0:T(8,128)(2,1)} %get-tuple-element.36), channel_id=1, source_target_pairs={{0,16},{4,20},{8,24},{12,28},{16,0},{20,4},{24,8},{28,12},{1,17},{... | collective-permute-start | bytes 1572872 | tf_op jit(solution)/shard_map/ppermute | solution.py:644
  13.1 37.3 %collective-permute-start.7 = (bf16[2,1,8,8192]{3,2,1,0:T(8,128)(2,1)}, bf16[2,1,8,8192]{3,2,1,0:T(8,128)(2,1)S(1)}, u32[]{:S(2)}, u32[]{:S(2)}) collective-permute-start(bf16[2,1,8,8192]{3,2,1,0:T(8,128)(2,1)} %get-tuple-element.40), channel_id=1, source_target_pairs={{0,12},{4,8},{8,4},{12,0},{16,28},{20,24},{24,20},{28,16},{1,13},{... | collective-permute-start | bytes 786440 | tf_op jit(solution)/shard_map/ppermute | solution.py:644
  14.1 19.3 %copy-start.16 = (bf16[2,1,8,8192]{3,2,1,0:T(8,128)(2,1)S(1)}, bf16[2,1,8,8192]{3,2,1,0:T(8,128)(2,1)}, u32[]{:S(2)}) copy-start(bf16[2,1,8,8192]{3,2,1,0:T(8,128)(2,1)} %get-tuple-element.33) | copy-start | bytes 786436
  22.7 27.7 %collective-permute-start.8 = (bf16[2,1,8,8192]{3,2,1,0:T(8,128)(2,1)S(1)}, bf16[2,1,8,8192]{3,2,1,0:T(8,128)(2,1)S(1)}, u32[]{:S(2)}, u32[]{:S(2)}) collective-permute-start(bf16[2,1,8,8192]{3,2,1,0:T(8,128)(2,1)S(1)} %copy-done.17), channel_id=1, source_target_pairs={{0,20},{4,16},{8,28},{12,24},{16,4},{20,0},{24,12},{28,8},{1,21},{... | collective-permute-start | bytes 786440 | tf_op jit(solution)/shard_map/ppermute | solution.py:644
  33.4 22.4 %collective-permute-start = (bf16[2,1,8,8192]{3,2,1,0:T(8,128)(2,1)S(1)}, bf16[2,1,8,8192]{3,2,1,0:T(8,128)(2,1)S(1)}, u32[]{:S(2)}, u32[]{:S(2)}) collective-permute-start(bf16[2,1,8,8192]{3,2,1,0:T(8,128)(2,1)S(1)} %copy-done.16), channel_id=1, source_target_pairs={{0,12},{4,8},{8,4},{12,0},{16,28},{20,24},{24,20},{28,16},{1,13},{... | collective-permute-start | bytes 786440 | tf_op jit(solution)/shard_map/ppermute | solution.py:644
  45.7 10.3 %collective-permute-start.1 = (bf16[2,1,8,8192]{3,2,1,0:T(8,128)(2,1)S(1)}, bf16[2,1,8,8192]{3,2,1,0:T(8,128)(2,1)S(1)}, u32[]{:S(2)}, u32[]{:S(2)}) collective-permute-start(bf16[2,1,8,8192]{3,2,1,0:T(8,128)(2,1)S(1)} %copy-done.15), channel_id=1, source_target_pairs={{0,20},{4,16},{8,28},{12,24},{16,4},{20,0},{24,12},{28,8},{1,21},{... | collective-permute-start | bytes 786440 | tf_op jit(solution)/shard_map/ppermute | solution.py:644
  60.0 46.2 %all-to-all-start = ((f32[32,16,512]{2,1,0:T(8,128)}), f32[32,16,512]{2,1,0:T(8,128)S(1)}, u32[]{:S(2)}, u32[]{:S(2)}) async-start(f32[32,16,512]{2,1,0:T(8,128)} %get-tuple-element.43.lags_ref), calls=%async_computation | async-start | bytes 2097152 | tf_op jit(solution)/shard_map/all_to_all | solution.py:662
  66.2 9.5 %collective-permute-start.10 = (f32[16,8,512]{2,1,0:T(8,128)S(1)}, f32[16,8,512]{2,1,0:T(8,128)S(1)}, u32[]{:S(2)}, u32[]{:S(2)}) collective-permute-start(f32[16,8,512]{2,1,0:T(8,128)S(1)} %get-tuple-element.45), channel_id=1, source_target_pairs={{0,4},{4,0},{8,12},{12,8},{16,20},{20,16},{24,28},{28,24},{1,5},{5... | collective-permute-start | bytes 786440 | tf_op jit(solution)/shard_map/ppermute | solution.py:659
  66.3 9.4 %collective-permute-start.9 = (f32[16,8,512]{2,1,0:T(8,128)S(1)}, f32[16,8,512]{2,1,0:T(8,128)S(1)}, u32[]{:S(2)}, u32[]{:S(2)}) collective-permute-start(f32[16,8,512]{2,1,0:T(8,128)S(1)} %get-tuple-element.44), channel_id=1, source_target_pairs={{0,4},{4,0},{8,12},{12,8},{16,20},{20,16},{24,28},{28,24},{1,5},{5... | collective-permute-start | bytes 786440 | tf_op jit(solution)/shard_map/ppermute | solution.py:659
  76.5 28.7 %copy-start = (f32[64,64]{1,0:T(8,128)S(1)}, f32[64,64]{1,0:T(8,128)}, u32[]{:S(2)}) copy-start(f32[64,64]{1,0:T(8,128)} %refs_6_.3) | copy-start | bytes 49156
  76.5 28.7 %copy-start.1 = (f32[64,33]{0,1:T(8,128)S(1)}, f32[64,33]{0,1:T(8,128)}, u32[]{:S(2)}) copy-start(f32[64,33]{0,1:T(8,128)} %param.32) | copy-start | bytes 25348
  76.5 28.7 %copy-start.2 = (f32[2,64]{1,0:T(2,128)S(1)}, f32[2,64]{1,0:T(2,128)}, u32[]{:S(2)}) copy-start(f32[2,64]{1,0:T(2,128)} %refs_7_.3) | copy-start | bytes 1540
  76.5 28.7 %copy-start.3 = (f32[64]{0:T(128)S(1)}, f32[64]{0:T(128)}, u32[]{:S(2)}) copy-start(f32[64]{0:T(128)} %param.33) | copy-start | bytes 772
  84.8 1.4 %collective-permute-start.11 = (f32[88,128]{1,0:T(8,128)}, f32[88,128]{1,0:T(8,128)S(1)}, u32[]{:S(2)}, u32[]{:S(2)}) collective-permute-start(f32[88,128]{1,0:T(8,128)} %backward.1), channel_id=1, source_target_pairs={{0,4},{4,0},{8,12},{12,8},{16,20},{20,16},{24,28},{28,24},{1,5},{5... | collective-permute-start | bytes 135176 | tf_op jit(solution)/shard_map/ppermute | solution.py:545
  87.1 4.2 %collective-permute-start.12 = (f32[88,128]{1,0:T(8,128)S(1)}, f32[88,128]{1,0:T(8,128)S(1)}, u32[]{:S(2)}, u32[]{:S(2)}) collective-permute-start(f32[88,128]{1,0:T(8,128)S(1)} %add.16), channel_id=1, source_target_pairs={{0,8},{4,12},{8,0},{12,4},{16,24},{20,28},{24,16},{28,20},{1,9},{5... | collective-permute-start | bytes 135176 | tf_op jit(solution)/shard_map/ppermute | solution.py:550
  88.6 4.0 %collective-permute-start.13 = (f32[88,128]{1,0:T(8,128)S(1)}, f32[88,128]{1,0:T(8,128)S(1)}, u32[]{:S(2)}, u32[]{:S(2)}) collective-permute-start(f32[88,128]{1,0:T(8,128)S(1)} %add.16), channel_id=1, source_target_pairs={{0,16},{4,20},{8,24},{12,28},{16,0},{20,4},{24,8},{28,12},{1,17},{... | collective-permute-start | bytes 135176 | tf_op jit(solution)/shard_map/ppermute | solution.py:550
  90.1 4.9 %collective-permute-start.14 = (f32[88,128]{1,0:T(8,128)S(1)}, f32[88,128]{1,0:T(8,128)S(1)}, u32[]{:S(2)}, u32[]{:S(2)}) collective-permute-start(f32[88,128]{1,0:T(8,128)S(1)} %add.16), channel_id=1, source_target_pairs={{0,24},{4,28},{8,16},{12,20},{16,8},{20,12},{24,0},{28,4},{1,25},{... | collective-permute-start | bytes 135176 | tf_op jit(solution)/shard_map/ppermute | solution.py:550
  95.1 4.5 %collective-permute-start.15 = (f32[136,128]{1,0:T(8,128)S(1)}, f32[136,128]{1,0:T(8,128)S(1)}, u32[]{:S(2)}, u32[]{:S(2)}) collective-permute-start(f32[136,128]{1,0:T(8,128)S(1)} %constant_dynamic-update-slice_fusion.refs_0_), channel_id=1, source_target_pairs={{0,1},{1,0},{2,3},{3,2},{4,5},{5,4},{6,7},{7,6},{8,9},{9,8},{10,11... | collective-permute-start | bytes 208904 | tf_op jit(solution)/shard_map/ppermute | solution.py:550
  96.7 6.7 %collective-permute-start.16 = (f32[136,128]{1,0:T(8,128)S(1)}, f32[136,128]{1,0:T(8,128)S(1)}, u32[]{:S(2)}, u32[]{:S(2)}) collective-permute-start(f32[136,128]{1,0:T(8,128)S(1)} %constant_dynamic-update-slice_fusion.refs_0_), channel_id=1, source_target_pairs={{0,2},{1,3},{2,0},{3,1},{4,6},{5,7},{6,4},{7,5},{8,10},{9,11},{10,... | collective-permute-start | bytes 208904 | tf_op jit(solution)/shard_map/ppermute | solution.py:550
  99.1 6.1 %collective-permute-start.17 = (f32[136,128]{1,0:T(8,128)S(1)}, f32[136,128]{1,0:T(8,128)S(1)}, u32[]{:S(2)}, u32[]{:S(2)}) collective-permute-start(f32[136,128]{1,0:T(8,128)S(1)} %constant_dynamic-update-slice_fusion.refs_0_), channel_id=1, source_target_pairs={{0,3},{1,2},{2,1},{3,0},{4,7},{5,6},{6,5},{7,4},{8,11},{9,10},{10,... | collective-permute-start | bytes 208904 | tf_op jit(solution)/shard_map/ppermute | solution.py:550
  (13 other events, 79.4 us)

commit v7 on v6

--- a/solution.py
+++ b/solution.py
@@ -249,12 +249,8 @@
                 out_ref[owner, :, pl.ds(k * LANES, LANES)] = lag_ref[
                     pl.ds(owner * wide_rows + k, channels, stride=2 * rows), :
                 ]
-        skip = (1 - (lax.axis_index("dp") & 1)) * (owners // 2 * wide_rows)
-        for owner in range(owners // 2):
-            for k in range(wide_rows):
-                other_ref[owner, :, pl.ds(k * LANES, LANES)] = lag_ref[
-                    pl.ds(skip + owner * wide_rows + k, channels, stride=2 * rows), :
-                ]
+        half = owners // 2
+        other_ref[...] = out_ref[pl.ds((1 - (lax.axis_index("dp") & 1)) * half, half)]
 
 
 def correlate(pieces, held, scale, owners, lags=None, chunk=0, chunks=1):
@@ -411,7 +407,7 @@
 def backward_body(
     place_ref, second_ref, lags_ref, other_refs, table_ref, layer1_ref, layer2_ref, cos1_ref, cos2_ref,
     decay_ref, output_ref, hidden_ref, freq_ref,
-    out_ref, output_parts, hidden_parts, decay_col, own_ref, sum1_ref, sum3_ref, sum5_ref, *, total, pack,
+    keep_ref, send_ref, output_parts, hidden_parts, decay_col, own_ref, sum1_ref, sum3_ref, sum5_ref, *, total, pack,
 ):
     step = pl.program_id(0)
     owners, own, _ = lags_ref.shape
@@ -459,22 +455,25 @@
             return ref[:rows, :cols] + ref[:rows, cols:] + ref[rows:, :cols]
 
         net = jnp.concatenate([joined(sum3_ref), joined(sum5_ref)], axis=1)
-        out_ref[:hidden] = jnp.concatenate(
-            [net, jnp.zeros((hidden, LANES - net.shape[1]), F32)], axis=1
-        )
+        net = jnp.concatenate([net, jnp.zeros((hidden, LANES - net.shape[1]), F32)], axis=1)
         sums = joined(sum1_ref)
         decay_grad = -jnp.sum(own_ref[...].T * sums[own:], axis=1, keepdims=True)
-        height = out_ref.shape[0] - hidden - own // pack
+        per, half = own // pack, keep_ref.shape[0]
+        summed = half - per // 2
+        height = 2 * summed - hidden
         place = lax.broadcasted_iota(jnp.int32, (height, LANES), 0) * LANES
         place = place + lax.broadcasted_iota(jnp.int32, (height, LANES), 1) - first
         decays = jnp.zeros((height, LANES), F32)
         for c in range(own):
             decays = jnp.where(place == c, decay_grad[c : c + 1], decays)
-        out_ref[pl.ds(hidden, height), :] = decays
-        per = own // pack
         parts = [sums[k * per : (k + 1) * per] for k in range(pack)]
         parts += [jnp.zeros((per, LANES - pack * hidden), F32)] if pack * hidden < LANES else []
-        out_ref[hidden + height :] = jnp.concatenate(parts, axis=1)
+        rows = jnp.concatenate(parts, axis=1)
+        total_rows = jnp.concatenate([net, decays], axis=0)
+        low = jnp.concatenate([total_rows[:summed], rows[: per // 2]], axis=0)
+        high = jnp.concatenate([total_rows[summed:], rows[per // 2 :]], axis=0)
+        keep_ref[...] = jnp.where(upper, high, low)
+        send_ref[...] = jnp.where(upper, low, high)
 
 
 def packing(own, hidden):
@@ -482,7 +481,7 @@
 
 
 def summed_rows(hidden, channels):
-    return hidden + -(-channels // (8 * LANES)) * 8
+    return -(-(hidden + -(-channels // LANES)) // 16) * 8
 
 
 def backward(first, second, lags, others, saved, decay_rate, output_weight, hidden_weight, frequency, total):
@@ -490,7 +489,7 @@
     own = 2 * own
     hidden = hidden_weight.shape[0]
     pack = packing(own, hidden)
-    height = summed_rows(hidden, decay_rate.shape[0]) + own // pack
+    height = summed_rows(hidden, decay_rate.shape[0]) + own // pack // 2
     steps = total // 2 // STEP
     args = (decay_rate[None], output_weight.T, hidden_weight, frequency)
     specs = [
@@ -507,7 +506,7 @@
             num_scalar_prefetch=2,
             grid=(steps,),
             in_specs=specs,
-            out_specs=pl.BlockSpec((height, LANES), lambda i, at, second: (0, 0)),
+            out_specs=[pl.BlockSpec((height, LANES), lambda i, at, second: (0, 0))] * 2,
             scratch_shapes=[
                 pltpu.VMEM((hidden, 3 * own), BF16),
                 pltpu.VMEM((hidden, 3 * hidden), BF16),
@@ -518,7 +517,7 @@
                 pltpu.VMEM((2 * hidden, saved[0].shape[0]), F32),
             ],
         ),
-        out_shape=jax.ShapeDtypeStruct((height, LANES), F32),
+        out_shape=[jax.ShapeDtypeStruct((height, LANES), F32)] * 2,
         cost_estimate=pl.CostEstimate(
             flops=total * hidden * 1000, bytes_accessed=total * hidden * 10, transcendentals=0
         ),
@@ -539,10 +538,10 @@
     return steps
 
 
-def share(both, summed):
+def share(keep, send, summed):
     steps = rounds()
-    size = lax.axis_size("dp")
-    both = both + lax.ppermute(both, "dp", [(i, i ^ 1) for i in range(size)])
+    pair = [(i, i ^ 1) for i in range(lax.axis_size("dp"))]
+    both = keep + lax.ppermute(send, "dp", pair)
     for axis, masks in steps:
         size = lax.axis_size(axis)
         parts = [both]
@@ -550,24 +549,25 @@
             parts.append(lax.ppermute(both, axis, [(i, i ^ mask) for i in range(size)]))
         total = sum(part[:summed] for part in parts)
         both = jnp.concatenate([total, *(part[summed:] for part in parts)], axis=0)
-    return parts
+    return both, lax.ppermute(both, "dp", pair)
 
 
 def finish_kernel(*refs, own, pack):
     steps = rounds()
-    part_refs, refs = refs[: len(steps[-1][1])], refs[len(steps[-1][1]) :]
-    embed_ref, bias_ref, hidden_ref, freq_ref = refs[:4]
-    embed_grad, bias_grad, hidden_grad, frequency_grad, output_grad, decay_grad, rows_ref = refs[4:]
+    mine_ref, theirs_ref, embed_ref, bias_ref, hidden_ref, freq_ref = refs[:6]
+    embed_grad, bias_grad, hidden_grad, frequency_grad, output_grad, decay_grad, rows_ref = refs[6:]
     hidden, features = hidden_ref.shape[0], embed_ref.shape[0]
     summed = summed_rows(hidden, output_grad.shape[1])
-    total = sum(ref[:summed] for ref in part_refs)
+    upper = (lax.axis_index("dp") & 1) != 0
+    low = jnp.where(upper, theirs_ref[...], mine_ref[...])
+    high = jnp.where(upper, mine_ref[...], theirs_ref[...])
+    total = jnp.concatenate([low[:summed], high[:summed]], axis=0)
     net = total[:hidden]
     turned = net.T
     decay_grad[...] = total[hidden : hidden + decay_grad.shape[0]]
-    unit = own // pack
+    unit = own // pack // 2
     count = output_grad.shape[1] // own
     here = {axis: lax.axis_index(axis) for axis in ("dp", "chan")}
-    each = count // len(part_refs)
     for k in range(count):
         there, rest = dict(here), k
         for axis, masks in steps:
@@ -575,9 +575,11 @@
             rest //= len(masks)
         place = there["chan"] * (lax.axis_size("dp") // 2) + (there["dp"] >> 1)
         for n in range(pack):
-            rows_ref[pl.ds(pl.multiple_of(place * own + n * unit, unit), unit), :] = part_refs[
-                k // each
-            ][pl.ds(summed + k % each * unit, unit), n * hidden : (n + 1) * hidden]
+            for m, half in enumerate((low, high)):
+                at = pl.multiple_of(place * own + (2 * n + m) * unit, unit)
+                rows_ref[pl.ds(at, unit), :] = half[
+                    summed + k * unit : summed + (k + 1) * unit, n * hidden : (n + 1) * hidden
+                ]
     output_grad[...] = rows_ref[...].T
     table = turned[hidden:]
     embed = jnp.concatenate([table[features - 1 : features], table[: features - 1]], axis=0)
@@ -591,7 +593,7 @@
     frequency_grad[1:2] = jnp.sum(hidden_ref[...].T * turned[:hidden], axis=0, keepdims=True)
 
 
-def finish(parts, embed_weight, embed_bias, hidden_weight, frequency, channels, own):
+def finish(mine, theirs, embed_weight, embed_bias, hidden_weight, frequency, channels, own):
     hidden, features = embed_weight.shape
     shapes = (
         (features, hidden), (1, hidden), (hidden, hidden), (2, hidden), (hidden, channels),
@@ -603,7 +605,7 @@
         scratch_shapes=[pltpu.VMEM((channels, hidden), F32)],
         compiler_params=pltpu.CompilerParams(vmem_limit_bytes=8 * 2**20),
         name="finish",
-    )(*parts, embed_weight.T, embed_bias[None], hidden_weight, frequency)
+    )(mine, theirs, embed_weight.T, embed_bias[None], hidden_weight, frequency)
     return embed.T, bias[0], hid, freq, output.T, decay.reshape(-1)[:channels]
 
 
@@ -661,13 +663,15 @@
     saved = network(embed_weight, embed_bias, hidden_weight, frequency, total)
     shared = lax.all_to_all(lags, ("dp", "chan"), 0, 0, tiled=True)
     first = at_chan * chan_local + (at_dp & -2) * own
-    both = backward(first, at_dp & 1, lags, others, saved, decay_rate, output_weight, hidden_weight, frequency, total)
-    parts = share(both, summed_rows(hidden, channels))
+    keep, send = backward(
+        first, at_dp & 1, lags, others, saved, decay_rate, output_weight, hidden_weight, frequency, total
+    )
+    mine, theirs = share(keep, send, summed_rows(hidden, channels))
     filter_grad = jnp.swapaxes(shared.reshape(dp, chan, own, -1), 0, 1)
     filter_grad = filter_grad.reshape(channels, -1)
     return (
         filter_grad,
-        *finish(parts, embed_weight, embed_bias, hidden_weight, frequency, channels, 2 * own),
+        *finish(mine, theirs, embed_weight, embed_bias, hidden_weight, frequency, channels, 2 * own),
     )
 
 

time: 108 us -> 122 us (1.13)
  waiting for transfers between devices: 34.7 us -> 51 us
  Pallas kernels: 43.3 us -> 41.1 us
    ppermute x6, waiting for transfers between devices: 10.2 us -> 24.4 us  [share(): parts.append(lax.ppermute(both, axis, [(i, i ^ mask) for i in range(size)]))]
    pallas_call x5, Pallas kernels: 20.1 us -> 18.2 us  [correlate(): pl.pallas_call(functools.partial(correlate_kernel, pieces=len(pieces), he...]
    ppermute x1 -> x2, waiting for transfers between devices: 1.35 us -> 2.48 us  [the longest x1 1.27 us: share(): return (both, lax.ppermute(both, 'dp', pair))]
  transfers between devices with their start and end apart: 19 -> 20, of which waited for: 13 -> 10; matrix products, arithmetic and copies ran while one was open for 1% -> 0% of each run, Pallas kernels for 32% -> 21%
where the time goes in v7:
time: 122 us
  waiting for transfers between devices  51 us (42%)
  Pallas kernels  41.1 us (34%)
  starting transfers between devices  24.7 us (20%)
  local copies, waits for them, and re-layouts  2.98 us (2%)
    ppermute x6, waiting for transfers between devices, share(): parts.append(lax.ppermute(both, axis, [(i, i ^ mask) for i in range(size)]))  24.4 us
    ppermute x9, waiting for transfers between devices, work(): pieces[p, start] = lax.ppermute(sent, 'dp', swap) if p else sent  24.1 us
    pallas_call x5, Pallas kernels, correlate(): pl.pallas_call(functools.partial(correlate_kernel, pieces=len(pieces), he...  18.2 us
    ppermute x9, starting transfers between devices, work(): pieces[p, start] = lax.ppermute(sent, 'dp', swap) if p else sent  9.8 us
    pallas_call x1, Pallas kernels, network(): pl.pallas_call(functools.partial(network_kernel, total=total), grid=(tota...  8.94 us
    ppermute x6, starting transfers between devices, share(): parts.append(lax.ppermute(both, axis, [(i, i ^ mask) for i in range(size)]))  7.94 us
    pallas_call x1, Pallas kernels, backward(): pl.pallas_call(functools.partial(backward_kernel, others=len(others), tot...  7.87 us
    all_to_all x1, starting transfers between devices, work(): shared = lax.all_to_all(lags, ('dp', 'chan'), 0, 0, tiled=True)  6.04 us
  transfers between devices with their start and end apart: 20, of which 10 were waited for; matrix products, arithmetic and copies ran while one was open for 0% of the time, Pallas kernels for 21%

profile of v7, /device:TPU:0, one launch (start us, length us, event | category | flops | bytes accessed | tf_op | source)
XLA Modules:
  0.0 121.5 jit_solution(13820150548644956779)
XLA Ops:
  0.6 2.1 %pick.2 = (bf16[2,1,16,8192]{3,2,1,0:T(8,128)(2,1)}, bf16[2,1,16,8192]{3,2,1,0:T(8,128)(2,1)}) custom-call(bf16[1,128,8192]{2,1,0:T(8,128)(2,1)} %x_ref.3, bf16[1,128,8192]{2,1,0:T(8,128)(2,1)} %g_ref.3), custom_call_target="tpu_custom_call" | custom-call | bytes 2097152 | tf_op jit(solution)/shard_map/pick/pallas_call | solution.py:133
  2.8 3.0 %pick.3 = (bf16[2,1,16,8192]{3,2,1,0:T(8,128)(2,1)}, bf16[2,1,16,8192]{3,2,1,0:T(8,128)(2,1)}, bf16[2,1,16,8192]{3,2,1,0:T(8,128)(2,1)}, bf16[2,1,16,8192]{3,2,1...) custom-call(bf16[1,128,8192]{2,1,0:T(8,128)(2,1)} %x_ref.3, ...), custom_call_target="tpu_custom_call" | custom-call | bytes 6291456 | tf_op jit(solution)/shard_map/pick/pallas_call | solution.py:133
  6.3 3.5 %collective-permute-start.4 = (bf16[2,1,16,8192]{3,2,1,0:T(8,128)(2,1)S(1)}, bf16[2,1,16,8192]{3,2,1,0:T(8,128)(2,1)S(1)}, u32[]{:S(2)}, u32[]{:S(2)}) collective-permute-start(bf16[2,1,16,8192]{3,2,1,0:T(8,128)(2,1)S(1)} %copy-done.12), channel_id=1, source_target_pairs={{0,24},{4,28},{8,16},{12,20},{16,8},{20,12},{24,0},{28,4},{1,25},{... | collective-permute-start | bytes 1572872 | tf_op jit(solution)/shard_map/ppermute | solution.py:646
  9.9 1.6 %collective-permute-start.2 = (bf16[2,1,16,8192]{3,2,1,0:T(8,128)(2,1)}, bf16[2,1,16,8192]{3,2,1,0:T(8,128)(2,1)S(1)}, u32[]{:S(2)}, u32[]{:S(2)}) collective-permute-start(bf16[2,1,16,8192]{3,2,1,0:T(8,128)(2,1)} %get-tuple-element.37), channel_id=1, source_target_pairs={{0,8},{4,12},{8,0},{12,4},{16,24},{20,28},{24,16},{28,20},{1,9},{5... | collective-permute-start | bytes 1572872 | tf_op jit(solution)/shard_map/ppermute | solution.py:646
  11.6 1.5 %collective-permute-start.3 = (bf16[2,1,16,8192]{3,2,1,0:T(8,128)(2,1)}, bf16[2,1,16,8192]{3,2,1,0:T(8,128)(2,1)S(1)}, u32[]{:S(2)}, u32[]{:S(2)}) collective-permute-start(bf16[2,1,16,8192]{3,2,1,0:T(8,128)(2,1)} %get-tuple-element.38), channel_id=1, source_target_pairs={{0,16},{4,20},{8,24},{12,28},{16,0},{20,4},{24,8},{28,12},{1,17},{... | collective-permute-start | bytes 1572872 | tf_op jit(solution)/shard_map/ppermute | solution.py:646
  14.2 4.0 %correlate.5.refs_2_ = f32[16,64,256]{2,1,0:T(8,128)S(1)} custom-call(bf16[2,1,16,8192]{3,2,1,0:T(8,128)(2,1)S(1)} %copy-done.5, bf16[2,1,16,8192]{3,2,1,0:T(8,128)(2,1)S(1)} %collective-permute-done.6.refs_1_, bf16[128,128]{1,0:T(8,128)(2,1)S(1)} %copy-done.11, f32[2,64,128]{2,1,0:T(8,128)S(1)} %copy-done.9, bf16[768,256]{1,0:T(8,128)(2,1)S(1)} %copy-done.6), custom_call_target="tpu_custom_call" | custom-call | flops 2415919104 | bytes 2097152 | tf_op jit(solution)/shard_map/correlate/pallas_call | solution.py:298
  18.2 4.5 %collective-permute-done.4.refs_0_ = bf16[2,1,16,8192]{3,2,1,0:T(8,128)(2,1)S(1)} collective-permute-done((bf16[2,1,16,8192]{3,2,1,0:T(8,128)(2,1)S(1)}, bf16[2,1,16,8192]{3,2,1,0:T(8,128)(2,1)S(1)}, u32[]{:S(2)}, u32[]{:S(2)}) %collective-permute-start.4) | collective-permute-done | bytes 524320 | tf_op jit(solution)/shard_map/ppermute | solution.py:646
  23.3 10.2 %collective-permute-done.5.refs_1_ = bf16[2,1,16,8192]{3,2,1,0:T(8,128)(2,1)S(1)} collective-permute-done((bf16[2,1,16,8192]{3,2,1,0:T(8,128)(2,1)S(1)}, bf16[2,1,16,8192]{3,2,1,0:T(8,128)(2,1)S(1)}, u32[]{:S(2)}, u32[]{:S(2)}) %collective-permute-start.5) | collective-permute-done | bytes 524320 | tf_op jit(solution)/shard_map/ppermute | solution.py:646
  33.4 1.9 %collective-permute-start = (bf16[2,1,8,8192]{3,2,1,0:T(8,128)(2,1)S(1)}, bf16[2,1,8,8192]{3,2,1,0:T(8,128)(2,1)S(1)}, u32[]{:S(2)}, u32[]{:S(2)}) collective-permute-start(bf16[2,1,8,8192]{3,2,1,0:T(8,128)(2,1)S(1)} %copy-done.17), channel_id=1, source_target_pairs={{0,12},{4,8},{8,4},{12,0},{16,28},{20,24},{24,20},{28,16},{1,13},{... | collective-permute-start | bytes 786440 | tf_op jit(solution)/shard_map/ppermute | solution.py:646
  35.3 4.0 %correlate.6.refs_2_ = f32[16,64,256]{2,1,0:T(8,128)S(1)} custom-call(bf16[2,1,16,8192]{3,2,1,0:T(8,128)(2,1)S(1)} %collective-permute-done.4.refs_0_, bf16[2,1,16,8192]{3,2,1,0:T(8,128)(2,1)S(1)} %collective-permute-done.5.refs_1_, f32[16,64,256]{2,1,0:T(8,128)S(1)} %correlate.5.refs_2_, bf16[128,128]{1,0:T(8,128)(2,1)S(1)} %copy-done.11, ...), custom_call_target="tpu_custom_call" | custom-call | flops 2415919104 | bytes 2097152 | tf_op jit(solution)/shard_map/correlate/pallas_call | solution.py:298
  39.3 6.3 %collective-permute-done.2.refs_0_ = bf16[2,1,16,8192]{3,2,1,0:T(8,128)(2,1)S(1)} collective-permute-done((bf16[2,1,16,8192]{3,2,1,0:T(8,128)(2,1)}, bf16[2,1,16,8192]{3,2,1,0:T(8,128)(2,1)S(1)}, u32[]{:S(2)}, u32[]{:S(2)}) %collective-permute-start.2) | collective-permute-done | bytes 524320 | tf_op jit(solution)/shard_map/ppermute | solution.py:646
  45.8 4.0 %correlate.7.refs_2_ = f32[16,64,256]{2,1,0:T(8,128)S(1)} custom-call(bf16[2,1,16,8192]{3,2,1,0:T(8,128)(2,1)S(1)} %collective-permute-done.2.refs_0_, bf16[2,1,16,8192]{3,2,1,0:T(8,128)(2,1)S(1)} %collective-permute-done.3.refs_1_, f32[16,64,256]{2,1,0:T(8,128)S(1)} %correlate.6.refs_2_, bf16[128,128]{1,0:T(8,128)(2,1)S(1)} %copy-done.11, ...), custom_call_target="tpu_custom_call" | custom-call | flops 2415919104 | bytes 2097152 | tf_op jit(solution)/shard_map/correlate/pallas_call | solution.py:298
  50.4 3.1 %correlate.8 = (f32[32,16,512]{2,1,0:T(8,128)S(1)}, f32[16,8,512]{2,1,0:T(8,128)S(1)}) custom-call(bf16[2,1,8,8192]{3,2,1,0:T(8,128)(2,1)S(1)} %collective-permute-done.7.refs_0_, bf16[2,1,8,8192]{3,2,1,0:T(8,128)(2,1)S(1)} %collective-permute-done.8.refs_1_, f32[16,64,256]{2,1,0:T(8,128)S(1)} %correlate.7.refs_2_, bf16[128,128]{1,0:T(8,128)(2,1)S(1)} %copy-done.11, ...), custom_call_target="tpu_custom_call" | custom-call | flops 1207959552 | bytes 1048576 | tf_op jit(solution)/shard_map/correlate/pallas_call | solution.py:298
  53.5 2.3 %collective-permute-done.refs_0_ = bf16[2,1,8,8192]{3,2,1,0:T(8,128)(2,1)S(1)} collective-permute-done((bf16[2,1,8,8192]{3,2,1,0:T(8,128)(2,1)S(1)}, bf16[2,1,8,8192]{3,2,1,0:T(8,128)(2,1)S(1)}, u32[]{:S(2)}, u32[]{:S(2)}) %collective-permute-start) | collective-permute-done | bytes 262176 | tf_op jit(solution)/shard_map/ppermute | solution.py:646
  56.0 3.1 %correlate.9 = (f32[32,16,512]{2,1,0:T(8,128)S(1)}, f32[16,8,512]{2,1,0:T(8,128)S(1)}) custom-call(bf16[2,1,8,8192]{3,2,1,0:T(8,128)(2,1)S(1)} %collective-permute-done.refs_0_, bf16[2,1,8,8192]{3,2,1,0:T(8,128)(2,1)S(1)} %collective-permute-done.1.refs_1_, f32[16,64,256]{2,1,0:T(8,128)S(1)} %correlate.7.refs_2_, ...), custom_call_target="tpu_custom_call", output_to_operand_aliasing={{0}: (3, {})} | custom-call | flops 1207959552 | bytes 1048576 | tf_op jit(solution)/shard_map/correlate/pallas_call | solution.py:298
  59.6 8.9 %network.1 = (bf16[80,8192]{1,0:T(8,128)(2,1)}, bf16[128,8192]{1,0:T(8,128)(2,1)}, bf16[128,8192]{1,0:T(8,128)(2,1)}, f32[64,8192]{1,0:T(8,128)}, f32[64,8192]{1,0:T(8,128)}) custom-call(s32[16,1]{1,0:T(8,128)} %constant.37.clone.factor_ref, f32[33,64]{1,0:T(8,128)} %bitcast.14, f32[1,64]{1,0:T(1,128)} %bitcast.16, f32[64,64]{1,0:T(8,128)} %refs_4_.6, ...), custom_call_target="tpu_custom_call" | custom-call | flops 629145600 | bytes 20971520 | tf_op jit(solution)/shard_map/network/pallas_call | solution.py:384
  69.4 7.9 %backward.1 = (f32[48,128]{1,0:T(8,128)}, f32[48,128]{1,0:T(8,128)}) custom-call(s32[1]{0:T(128)} %bitcast.3.place_ref, s32[1]{0:T(128)} %bitcast.4.second_ref, f32[32,16,512]{2,1,0:T(8,128)} %copy-done, f32[16,8,512]{2,1,0:T(8,128)} %copy-done.14, f32[16,8,512]{2,1,0:T(8,128)} %copy-done.13, bf16[80,8192]{1,0:T(8,128)(2,1)} %get-tuple-element.48.refs_2_, ...), custom_call_target="tpu_custom_call" | custom-call | flops 1048576000 | bytes 10485760 | tf_op jit(solution)/shard_map/backward/pallas_call | solution.py:503
  79.5 1.7 %collective-permute-start.12 = (f32[48,128]{1,0:T(8,128)S(1)}, f32[48,128]{1,0:T(8,128)S(1)}, u32[]{:S(2)}, u32[]{:S(2)}) collective-permute-start(f32[48,128]{1,0:T(8,128)S(1)} %add.25), channel_id=1, source_target_pairs={{0,8},{4,12},{8,0},{12,4},{16,24},{20,28},{24,16},{28,20},{1,9},{5... | collective-permute-start | bytes 73736 | tf_op jit(solution)/shard_map/ppermute | solution.py:549
  81.2 1.5 %collective-permute-start.13 = (f32[48,128]{1,0:T(8,128)S(1)}, f32[48,128]{1,0:T(8,128)S(1)}, u32[]{:S(2)}, u32[]{:S(2)}) collective-permute-start(f32[48,128]{1,0:T(8,128)S(1)} %add.25), channel_id=1, source_target_pairs={{0,16},{4,20},{8,24},{12,28},{16,0},{20,4},{24,8},{28,12},{1,17},{... | collective-permute-start | bytes 73736 | tf_op jit(solution)/shard_map/ppermute | solution.py:549
  83.0 6.0 %all-to-all-start = ((f32[32,16,512]{2,1,0:T(8,128)}), f32[32,16,512]{2,1,0:T(8,128)S(1)}, u32[]{:S(2)}, u32[]{:S(2)}) async-start(f32[32,16,512]{2,1,0:T(8,128)} %copy-done), calls=%async_computation | async-start | bytes 2097152 | tf_op jit(solution)/shard_map/all_to_all | solution.py:664
  89.2 1.8 %collective-permute-start.15 = (f32[72,128]{1,0:T(8,128)S(1)}, f32[72,128]{1,0:T(8,128)S(1)}, u32[]{:S(2)}, u32[]{:S(2)}) collective-permute-start(f32[72,128]{1,0:T(8,128)S(1)} %constant_dynamic-update-slice_fusion), channel_id=1, source_target_pairs={{0,1},{1,0},{2,3},{3,2},{4,5},{5,4},{6,7},{7,6},{8,9},{9,8},{10,11... | collective-permute-start | bytes 110600 | tf_op jit(solution)/shard_map/ppermute | solution.py:549
  91.0 2.4 %collective-permute-start.16 = (f32[72,128]{1,0:T(8,128)S(1)}, f32[72,128]{1,0:T(8,128)S(1)}, u32[]{:S(2)}, u32[]{:S(2)}) collective-permute-start(f32[72,128]{1,0:T(8,128)S(1)} %constant_dynamic-update-slice_fusion), channel_id=1, source_target_pairs={{0,2},{1,3},{2,0},{3,1},{4,6},{5,7},{6,4},{7,5},{8,10},{9,11},{10,... | collective-permute-start | bytes 110600 | tf_op jit(solution)/shard_map/ppermute | solution.py:549
  93.6 14.2 %collective-permute-done.15 = f32[72,128]{1,0:T(8,128)S(1)} collective-permute-done((f32[72,128]{1,0:T(8,128)S(1)}, f32[72,128]{1,0:T(8,128)S(1)}, u32[]{:S(2)}, u32[]{:S(2)}) %collective-permute-start.15) | collective-permute-done | bytes 36896 | tf_op jit(solution)/shard_map/ppermute | solution.py:549
  107.8 10.2 %collective-permute-done.16 = f32[72,128]{1,0:T(8,128)S(1)} collective-permute-done((f32[72,128]{1,0:T(8,128)S(1)}, f32[72,128]{1,0:T(8,128)S(1)}, u32[]{:S(2)}, u32[]{:S(2)}) %collective-permute-start.16) | collective-permute-done | bytes 36896 | tf_op jit(solution)/shard_map/ppermute | solution.py:549
  (79 shorter events, 10.7 us)
Async XLA Ops:
  5.8 7.3 %collective-permute-start.6 = (bf16[2,1,16,8192]{3,2,1,0:T(8,128)(2,1)}, bf16[2,1,16,8192]{3,2,1,0:T(8,128)(2,1)S(1)}, u32[]{:S(2)}, u32[]{:S(2)}) collective-permute-start(bf16[2,1,16,8192]{3,2,1,0:T(8,128)(2,1)} %get-tuple-element.41), channel_id=1, source_target_pairs={{0,4},{4,0},{8,12},{12,8},{16,20},{20,16},{24,28},{28,24},{1,5},{5... | collective-permute-start | bytes 1572872 | tf_op jit(solution)/shard_map/ppermute | solution.py:646
  6.3 16.4 %collective-permute-start.4 = (bf16[2,1,16,8192]{3,2,1,0:T(8,128)(2,1)S(1)}, bf16[2,1,16,8192]{3,2,1,0:T(8,128)(2,1)S(1)}, u32[]{:S(2)}, u32[]{:S(2)}) collective-permute-start(bf16[2,1,16,8192]{3,2,1,0:T(8,128)(2,1)S(1)} %copy-done.12), channel_id=1, source_target_pairs={{0,24},{4,28},{8,16},{12,20},{16,8},{20,12},{24,0},{28,4},{1,25},{... | collective-permute-start | bytes 1572872 | tf_op jit(solution)/shard_map/ppermute | solution.py:646
  9.8 23.6 %collective-permute-start.5 = (bf16[2,1,16,8192]{3,2,1,0:T(8,128)(2,1)S(1)}, bf16[2,1,16,8192]{3,2,1,0:T(8,128)(2,1)S(1)}, u32[]{:S(2)}, u32[]{:S(2)}) collective-permute-start(bf16[2,1,16,8192]{3,2,1,0:T(8,128)(2,1)S(1)} %copy-done.15), channel_id=1, source_target_pairs={{0,28},{4,24},{8,20},{12,16},{16,12},{20,8},{24,4},{28,0},{1,29},{... | collective-permute-start | bytes 1572872 | tf_op jit(solution)/shard_map/ppermute | solution.py:646
  9.9 35.7 %collective-permute-start.2 = (bf16[2,1,16,8192]{3,2,1,0:T(8,128)(2,1)}, bf16[2,1,16,8192]{3,2,1,0:T(8,128)(2,1)S(1)}, u32[]{:S(2)}, u32[]{:S(2)}) collective-permute-start(bf16[2,1,16,8192]{3,2,1,0:T(8,128)(2,1)} %get-tuple-element.37), channel_id=1, source_target_pairs={{0,8},{4,12},{8,0},{12,4},{16,24},{20,28},{24,16},{28,20},{1,9},{5... | collective-permute-start | bytes 1572872 | tf_op jit(solution)/shard_map/ppermute | solution.py:646
  11.6 34.2 %collective-permute-start.3 = (bf16[2,1,16,8192]{3,2,1,0:T(8,128)(2,1)}, bf16[2,1,16,8192]{3,2,1,0:T(8,128)(2,1)S(1)}, u32[]{:S(2)}, u32[]{:S(2)}) collective-permute-start(bf16[2,1,16,8192]{3,2,1,0:T(8,128)(2,1)} %get-tuple-element.38), channel_id=1, source_target_pairs={{0,16},{4,20},{8,24},{12,28},{16,0},{20,4},{24,8},{28,12},{1,17},{... | collective-permute-start | bytes 1572872 | tf_op jit(solution)/shard_map/ppermute | solution.py:646
  13.1 37.3 %collective-permute-start.7 = (bf16[2,1,8,8192]{3,2,1,0:T(8,128)(2,1)}, bf16[2,1,8,8192]{3,2,1,0:T(8,128)(2,1)S(1)}, u32[]{:S(2)}, u32[]{:S(2)}) collective-permute-start(bf16[2,1,8,8192]{3,2,1,0:T(8,128)(2,1)} %get-tuple-element.42), channel_id=1, source_target_pairs={{0,12},{4,8},{8,4},{12,0},{16,28},{20,24},{24,20},{28,16},{1,13},{... | collective-permute-start | bytes 786440 | tf_op jit(solution)/shard_map/ppermute | solution.py:646
  22.7 27.7 %collective-permute-start.8 = (bf16[2,1,8,8192]{3,2,1,0:T(8,128)(2,1)S(1)}, bf16[2,1,8,8192]{3,2,1,0:T(8,128)(2,1)S(1)}, u32[]{:S(2)}, u32[]{:S(2)}) collective-permute-start(bf16[2,1,8,8192]{3,2,1,0:T(8,128)(2,1)S(1)} %copy-done.18), channel_id=1, source_target_pairs={{0,20},{4,16},{8,28},{12,24},{16,4},{20,0},{24,12},{28,8},{1,21},{... | collective-permute-start | bytes 786440 | tf_op jit(solution)/shard_map/ppermute | solution.py:646
  33.4 22.4 %collective-permute-start = (bf16[2,1,8,8192]{3,2,1,0:T(8,128)(2,1)S(1)}, bf16[2,1,8,8192]{3,2,1,0:T(8,128)(2,1)S(1)}, u32[]{:S(2)}, u32[]{:S(2)}) collective-permute-start(bf16[2,1,8,8192]{3,2,1,0:T(8,128)(2,1)S(1)} %copy-done.17), channel_id=1, source_target_pairs={{0,12},{4,8},{8,4},{12,0},{16,28},{20,24},{24,20},{28,16},{1,13},{... | collective-permute-start | bytes 786440 | tf_op jit(solution)/shard_map/ppermute | solution.py:646
  45.7 10.3 %collective-permute-start.1 = (bf16[2,1,8,8192]{3,2,1,0:T(8,128)(2,1)S(1)}, bf16[2,1,8,8192]{3,2,1,0:T(8,128)(2,1)S(1)}, u32[]{:S(2)}, u32[]{:S(2)}) collective-permute-start(bf16[2,1,8,8192]{3,2,1,0:T(8,128)(2,1)S(1)} %copy-done.16), channel_id=1, source_target_pairs={{0,20},{4,16},{8,28},{12,24},{16,4},{20,0},{24,12},{28,8},{1,21},{... | collective-permute-start | bytes 786440 | tf_op jit(solution)/shard_map/ppermute | solution.py:646
  59.1 9.5 %collective-permute-start.10 = (f32[16,8,512]{2,1,0:T(8,128)S(1)}, f32[16,8,512]{2,1,0:T(8,128)S(1)}, u32[]{:S(2)}, u32[]{:S(2)}) collective-permute-start(f32[16,8,512]{2,1,0:T(8,128)S(1)} %get-tuple-element.47), channel_id=1, source_target_pairs={{0,4},{4,0},{8,12},{12,8},{16,20},{20,16},{24,28},{28,24},{1,5},{5... | collective-permute-start | bytes 786440 | tf_op jit(solution)/shard_map/ppermute | solution.py:661
  59.3 9.3 %collective-permute-start.9 = (f32[16,8,512]{2,1,0:T(8,128)S(1)}, f32[16,8,512]{2,1,0:T(8,128)S(1)}, u32[]{:S(2)}, u32[]{:S(2)}) collective-permute-start(f32[16,8,512]{2,1,0:T(8,128)S(1)} %get-tuple-element.46), channel_id=1, source_target_pairs={{0,4},{4,0},{8,12},{12,8},{16,20},{20,16},{24,28},{28,24},{1,5},{5... | collective-permute-start | bytes 786440 | tf_op jit(solution)/shard_map/ppermute | solution.py:661
  77.3 42.2 %copy-start.1 = (f32[64,64]{1,0:T(8,128)S(1)}, f32[64,64]{1,0:T(8,128)}, u32[]{:S(2)}) copy-start(f32[64,64]{1,0:T(8,128)} %refs_4_.6) | copy-start | bytes 49156
  77.3 42.2 %copy-start.2 = (f32[64,33]{0,1:T(8,128)S(1)}, f32[64,33]{0,1:T(8,128)}, u32[]{:S(2)}) copy-start(f32[64,33]{0,1:T(8,128)} %param.32) | copy-start | bytes 25348
  77.3 42.2 %copy-start.3 = (f32[2,64]{1,0:T(2,128)S(1)}, f32[2,64]{1,0:T(2,128)}, u32[]{:S(2)}) copy-start(f32[2,64]{1,0:T(2,128)} %refs_5_.5) | copy-start | bytes 1540
  77.3 42.2 %copy-start.4 = (f32[64]{0:T(128)S(1)}, f32[64]{0:T(128)}, u32[]{:S(2)}) copy-start(f32[64]{0:T(128)} %param.33) | copy-start | bytes 772
  77.3 1.5 %collective-permute-start.11 = (f32[48,128]{1,0:T(8,128)}, f32[48,128]{1,0:T(8,128)S(1)}, u32[]{:S(2)}, u32[]{:S(2)}) collective-permute-start(f32[48,128]{1,0:T(8,128)} %get-tuple-element.54), channel_id=1, source_target_pairs={{0,4},{4,0},{8,12},{12,8},{16,20},{20,16},{24,28},{28,24},{1,5},{5... | collective-permute-start | bytes 73736 | tf_op jit(solution)/shard_map/ppermute | solution.py:544
  79.5 9.5 %collective-permute-start.12 = (f32[48,128]{1,0:T(8,128)S(1)}, f32[48,128]{1,0:T(8,128)S(1)}, u32[]{:S(2)}, u32[]{:S(2)}) collective-permute-start(f32[48,128]{1,0:T(8,128)S(1)} %add.25), channel_id=1, source_target_pairs={{0,8},{4,12},{8,0},{12,4},{16,24},{20,28},{24,16},{28,20},{1,9},{5... | collective-permute-start | bytes 73736 | tf_op jit(solution)/shard_map/ppermute | solution.py:549
  81.2 7.9 %collective-permute-start.13 = (f32[48,128]{1,0:T(8,128)S(1)}, f32[48,128]{1,0:T(8,128)S(1)}, u32[]{:S(2)}, u32[]{:S(2)}) collective-permute-start(f32[48,128]{1,0:T(8,128)S(1)} %add.25), channel_id=1, source_target_pairs={{0,16},{4,20},{8,24},{12,28},{16,0},{20,4},{24,8},{28,12},{1,17},{... | collective-permute-start | bytes 73736 | tf_op jit(solution)/shard_map/ppermute | solution.py:549
  82.7 6.4 %collective-permute-start.14 = (f32[48,128]{1,0:T(8,128)S(1)}, f32[48,128]{1,0:T(8,128)S(1)}, u32[]{:S(2)}, u32[]{:S(2)}) collective-permute-start(f32[48,128]{1,0:T(8,128)S(1)} %add.25), channel_id=1, source_target_pairs={{0,24},{4,28},{8,16},{12,20},{16,8},{20,12},{24,0},{28,4},{1,25},{... | collective-permute-start | bytes 73736 | tf_op jit(solution)/shard_map/ppermute | solution.py:549
  83.0 37.4 %all-to-all-start = ((f32[32,16,512]{2,1,0:T(8,128)}), f32[32,16,512]{2,1,0:T(8,128)S(1)}, u32[]{:S(2)}, u32[]{:S(2)}) async-start(f32[32,16,512]{2,1,0:T(8,128)} %copy-done), calls=%async_computation | async-start | bytes 2097152 | tf_op jit(solution)/shard_map/all_to_all | solution.py:664
  89.2 18.6 %collective-permute-start.15 = (f32[72,128]{1,0:T(8,128)S(1)}, f32[72,128]{1,0:T(8,128)S(1)}, u32[]{:S(2)}, u32[]{:S(2)}) collective-permute-start(f32[72,128]{1,0:T(8,128)S(1)} %constant_dynamic-update-slice_fusion), channel_id=1, source_target_pairs={{0,1},{1,0},{2,3},{3,2},{4,5},{5,4},{6,7},{7,6},{8,9},{9,8},{10,11... | collective-permute-start | bytes 110600 | tf_op jit(solution)/shard_map/ppermute | solution.py:549
  91.0 27.0 %collective-permute-start.16 = (f32[72,128]{1,0:T(8,128)S(1)}, f32[72,128]{1,0:T(8,128)S(1)}, u32[]{:S(2)}, u32[]{:S(2)}) collective-permute-start(f32[72,128]{1,0:T(8,128)S(1)} %constant_dynamic-update-slice_fusion), channel_id=1, source_target_pairs={{0,2},{1,3},{2,0},{3,1},{4,6},{5,7},{6,4},{7,5},{8,10},{9,11},{10,... | collective-permute-start | bytes 110600 | tf_op jit(solution)/shard_map/ppermute | solution.py:549
  93.4 24.6 %collective-permute-start.17 = (f32[72,128]{1,0:T(8,128)S(1)}, f32[72,128]{1,0:T(8,128)S(1)}, u32[]{:S(2)}, u32[]{:S(2)}) collective-permute-start(f32[72,128]{1,0:T(8,128)S(1)} %constant_dynamic-update-slice_fusion), channel_id=1, source_target_pairs={{0,3},{1,2},{2,1},{3,0},{4,7},{5,6},{6,5},{7,4},{8,11},{9,10},{10,... | collective-permute-start | bytes 110600 | tf_op jit(solution)/shard_map/ppermute | solution.py:549
  118.1 1.3 %collective-permute-start.18 = (f32[168,128]{1,0:T(8,128)S(1)}, f32[168,128]{1,0:T(8,128)S(1)}, u32[]{:S(2)}, u32[]{:S(2)}) collective-permute-start(f32[168,128]{1,0:T(8,128)S(1)} %constant_dynamic-update-slice_fusion.5.refs_0_), channel_id=1, source_target_pairs={{0,4},{4,0},{8,12},{12,8},{16,20},{20,16},{24,28},{28,24},{1,5},{5... | collective-permute-start | bytes 258056 | tf_op jit(solution)/shard_map/ppermute | solution.py:552
  (15 other events, 108.3 us)

commit v8 on v7

--- a/solution.py
+++ b/solution.py
@@ -65,6 +65,23 @@
 def wide(values, axis):
     high, low = split(values)
     return jnp.concatenate([high, high, low], axis=axis)
+
+
+def thirds(values):
+    high, rest = values.astype(BF16), values
+    rest = rest - high.astype(F32)
+    middle = rest.astype(BF16)
+    return high, middle, (rest - middle.astype(F32)).astype(BF16)
+
+
+def narrow_exact(values, axis):
+    high, middle, low = thirds(values)
+    return jnp.concatenate([high, high, middle, middle, high, low], axis=axis)
+
+
+def wide_exact(values, axis):
+    high, middle, low = thirds(values)
+    return jnp.concatenate([high, middle, high, middle, low, high], axis=axis)
 
 
 def dot_lanes(a, b):
@@ -349,8 +366,8 @@
             ],
             axis=0,
         )
-        embed_parts[...] = narrow(embed.T, 1)
-        hidden_parts[...] = narrow(hidden_ref[...], 1)
+        embed_parts[...] = narrow_exact(embed.T, 1)
+        hidden_parts[...] = narrow_exact(hidden_ref[...], 1)
         for k in range(2):
             freq_cols[k] = column(freq_ref[k : k + 1, :])
 
@@ -363,10 +380,10 @@
     extra = jnp.where(row == 0, scaled, jnp.where(row == 1, 1.0, 0.0))
     table = jnp.concatenate([sine, cosine, extra], axis=0)
     table_ref[...] = stacked(table, 0)
-    first, cos1 = sine_cosine(freq_cols[0] * dot(embed_parts[...], wide(table, 0)))
+    first, cos1 = sine_cosine(freq_cols[0] * dot(embed_parts[...], wide_exact(table, 0)))
     first_ref[...] = stacked(first, 0)
     cos1_ref[...] = cos1
-    second, cos2 = sine_cosine(freq_cols[1] * dot(hidden_parts[...], wide(first, 0)))
+    second, cos2 = sine_cosine(freq_cols[1] * dot(hidden_parts[...], wide_exact(first, 0)))
     second_ref[...] = stacked(second, 0)
     cos2_ref[...] = cos2
 
@@ -388,8 +405,8 @@
         out_specs=[pl.BlockSpec((h, STEP), lambda i: (0, i)) for h, _ in heights],
         out_shape=[jax.ShapeDtypeStruct((h, total // 2), t) for h, t in heights],
         scratch_shapes=[
-            pltpu.VMEM((hidden, 3 * depth), BF16),
-            pltpu.VMEM((hidden, 3 * hidden), BF16),
+            pltpu.VMEM((hidden, 6 * depth), BF16),
+            pltpu.VMEM((hidden, 6 * hidden), BF16),
             pltpu.VMEM((2, hidden, 1), F32),
         ],
         cost_estimate=pl.CostEstimate(

time: 122 us -> 123 us (level)
  no operation moved by 1% of the time
where the time goes in v8:
time: 123 us; the launch traced here: 122 us
  waiting for transfers between devices  51 us (41%)
  Pallas kernels  41.6 us (34%)
  starting transfers between devices  24.7 us (20%)
  local copies, waits for them, and re-layouts  2.98 us (2%)
    ppermute x6, waiting for transfers between devices, share(): parts.append(lax.ppermute(both, axis, [(i, i ^ mask) for i in range(size)]))  24.4 us
    ppermute x9, waiting for transfers between devices, work(): pieces[p, start] = lax.ppermute(sent, 'dp', swap) if p else sent  24.1 us
    pallas_call x5, Pallas kernels, correlate(): pl.pallas_call(functools.partial(correlate_kernel, pieces=len(pieces), he...  18.2 us
    ppermute x9, starting transfers between devices, work(): pieces[p, start] = lax.ppermute(sent, 'dp', swap) if p else sent  9.8 us
    pallas_call x1, Pallas kernels, network(): pl.pallas_call(functools.partial(network_kernel, total=total), grid=(tota...  9.5 us
    ppermute x6, starting transfers between devices, share(): parts.append(lax.ppermute(both, axis, [(i, i ^ mask) for i in range(size)]))  7.94 us
    pallas_call x1, Pallas kernels, backward(): pl.pallas_call(functools.partial(backward_kernel, others=len(others), tot...  7.87 us
    all_to_all x1, starting transfers between devices, work(): shared = lax.all_to_all(lags, ('dp', 'chan'), 0, 0, tiled=True)  6.04 us
  transfers between devices with their start and end apart: 20, of which 10 were waited for; matrix products, arithmetic and copies ran while one was open for 0% of the time, Pallas kernels for 21%

profile of v8, /device:TPU:0, one launch (start us, length us, event | category | flops | bytes accessed | tf_op | source)
XLA Modules:
  0.0 122.1 jit_solution(4279622953841777738)
XLA Ops:
  0.6 2.1 %pick.2 = (bf16[2,1,16,8192]{3,2,1,0:T(8,128)(2,1)}, bf16[2,1,16,8192]{3,2,1,0:T(8,128)(2,1)}) custom-call(bf16[1,128,8192]{2,1,0:T(8,128)(2,1)} %x_ref.3, bf16[1,128,8192]{2,1,0:T(8,128)(2,1)} %g_ref.3), custom_call_target="tpu_custom_call" | custom-call | bytes 2097152 | tf_op jit(solution)/shard_map/pick/pallas_call | solution.py:150
  2.8 3.0 %pick.3 = (bf16[2,1,16,8192]{3,2,1,0:T(8,128)(2,1)}, bf16[2,1,16,8192]{3,2,1,0:T(8,128)(2,1)}, bf16[2,1,16,8192]{3,2,1,0:T(8,128)(2,1)}, bf16[2,1,16,8192]{3,2,1...) custom-call(bf16[1,128,8192]{2,1,0:T(8,128)(2,1)} %x_ref.3, ...), custom_call_target="tpu_custom_call" | custom-call | bytes 6291456 | tf_op jit(solution)/shard_map/pick/pallas_call | solution.py:150
  6.3 3.5 %collective-permute-start.4 = (bf16[2,1,16,8192]{3,2,1,0:T(8,128)(2,1)S(1)}, bf16[2,1,16,8192]{3,2,1,0:T(8,128)(2,1)S(1)}, u32[]{:S(2)}, u32[]{:S(2)}) collective-permute-start(bf16[2,1,16,8192]{3,2,1,0:T(8,128)(2,1)S(1)} %copy-done.12), channel_id=1, source_target_pairs={{0,24},{4,28},{8,16},{12,20},{16,8},{20,12},{24,0},{28,4},{1,25},{... | collective-permute-start | bytes 1572872 | tf_op jit(solution)/shard_map/ppermute | solution.py:663
  9.9 1.6 %collective-permute-start.2 = (bf16[2,1,16,8192]{3,2,1,0:T(8,128)(2,1)}, bf16[2,1,16,8192]{3,2,1,0:T(8,128)(2,1)S(1)}, u32[]{:S(2)}, u32[]{:S(2)}) collective-permute-start(bf16[2,1,16,8192]{3,2,1,0:T(8,128)(2,1)} %get-tuple-element.37), channel_id=1, source_target_pairs={{0,8},{4,12},{8,0},{12,4},{16,24},{20,28},{24,16},{28,20},{1,9},{5... | collective-permute-start | bytes 1572872 | tf_op jit(solution)/shard_map/ppermute | solution.py:663
  11.6 1.5 %collective-permute-start.3 = (bf16[2,1,16,8192]{3,2,1,0:T(8,128)(2,1)}, bf16[2,1,16,8192]{3,2,1,0:T(8,128)(2,1)S(1)}, u32[]{:S(2)}, u32[]{:S(2)}) collective-permute-start(bf16[2,1,16,8192]{3,2,1,0:T(8,128)(2,1)} %get-tuple-element.38), channel_id=1, source_target_pairs={{0,16},{4,20},{8,24},{12,28},{16,0},{20,4},{24,8},{28,12},{1,17},{... | collective-permute-start | bytes 1572872 | tf_op jit(solution)/shard_map/ppermute | solution.py:663
  14.2 4.0 %correlate.5.refs_2_ = f32[16,64,256]{2,1,0:T(8,128)S(1)} custom-call(bf16[2,1,16,8192]{3,2,1,0:T(8,128)(2,1)S(1)} %copy-done.5, bf16[2,1,16,8192]{3,2,1,0:T(8,128)(2,1)S(1)} %collective-permute-done.6.refs_1_, bf16[128,128]{1,0:T(8,128)(2,1)S(1)} %copy-done.11, f32[2,64,128]{2,1,0:T(8,128)S(1)} %copy-done.9, bf16[768,256]{1,0:T(8,128)(2,1)S(1)} %copy-done.6), custom_call_target="tpu_custom_call" | custom-call | flops 2415919104 | bytes 2097152 | tf_op jit(solution)/shard_map/correlate/pallas_call | solution.py:315
  18.2 4.5 %collective-permute-done.4.refs_0_ = bf16[2,1,16,8192]{3,2,1,0:T(8,128)(2,1)S(1)} collective-permute-done((bf16[2,1,16,8192]{3,2,1,0:T(8,128)(2,1)S(1)}, bf16[2,1,16,8192]{3,2,1,0:T(8,128)(2,1)S(1)}, u32[]{:S(2)}, u32[]{:S(2)}) %collective-permute-start.4) | collective-permute-done | bytes 524320 | tf_op jit(solution)/shard_map/ppermute | solution.py:663
  23.3 10.2 %collective-permute-done.5.refs_1_ = bf16[2,1,16,8192]{3,2,1,0:T(8,128)(2,1)S(1)} collective-permute-done((bf16[2,1,16,8192]{3,2,1,0:T(8,128)(2,1)S(1)}, bf16[2,1,16,8192]{3,2,1,0:T(8,128)(2,1)S(1)}, u32[]{:S(2)}, u32[]{:S(2)}) %collective-permute-start.5) | collective-permute-done | bytes 524320 | tf_op jit(solution)/shard_map/ppermute | solution.py:663
  33.4 1.9 %collective-permute-start = (bf16[2,1,8,8192]{3,2,1,0:T(8,128)(2,1)S(1)}, bf16[2,1,8,8192]{3,2,1,0:T(8,128)(2,1)S(1)}, u32[]{:S(2)}, u32[]{:S(2)}) collective-permute-start(bf16[2,1,8,8192]{3,2,1,0:T(8,128)(2,1)S(1)} %copy-done.17), channel_id=1, source_target_pairs={{0,12},{4,8},{8,4},{12,0},{16,28},{20,24},{24,20},{28,16},{1,13},{... | collective-permute-start | bytes 786440 | tf_op jit(solution)/shard_map/ppermute | solution.py:663
  35.3 4.0 %correlate.6.refs_2_ = f32[16,64,256]{2,1,0:T(8,128)S(1)} custom-call(bf16[2,1,16,8192]{3,2,1,0:T(8,128)(2,1)S(1)} %collective-permute-done.4.refs_0_, bf16[2,1,16,8192]{3,2,1,0:T(8,128)(2,1)S(1)} %collective-permute-done.5.refs_1_, f32[16,64,256]{2,1,0:T(8,128)S(1)} %correlate.5.refs_2_, bf16[128,128]{1,0:T(8,128)(2,1)S(1)} %copy-done.11, ...), custom_call_target="tpu_custom_call" | custom-call | flops 2415919104 | bytes 2097152 | tf_op jit(solution)/shard_map/correlate/pallas_call | solution.py:315
  39.3 6.3 %collective-permute-done.2.refs_0_ = bf16[2,1,16,8192]{3,2,1,0:T(8,128)(2,1)S(1)} collective-permute-done((bf16[2,1,16,8192]{3,2,1,0:T(8,128)(2,1)}, bf16[2,1,16,8192]{3,2,1,0:T(8,128)(2,1)S(1)}, u32[]{:S(2)}, u32[]{:S(2)}) %collective-permute-start.2) | collective-permute-done | bytes 524320 | tf_op jit(solution)/shard_map/ppermute | solution.py:663
  45.8 4.0 %correlate.7.refs_2_ = f32[16,64,256]{2,1,0:T(8,128)S(1)} custom-call(bf16[2,1,16,8192]{3,2,1,0:T(8,128)(2,1)S(1)} %collective-permute-done.2.refs_0_, bf16[2,1,16,8192]{3,2,1,0:T(8,128)(2,1)S(1)} %collective-permute-done.3.refs_1_, f32[16,64,256]{2,1,0:T(8,128)S(1)} %correlate.6.refs_2_, bf16[128,128]{1,0:T(8,128)(2,1)S(1)} %copy-done.11, ...), custom_call_target="tpu_custom_call" | custom-call | flops 2415919104 | bytes 2097152 | tf_op jit(solution)/shard_map/correlate/pallas_call | solution.py:315
  50.4 3.1 %correlate.8 = (f32[32,16,512]{2,1,0:T(8,128)S(1)}, f32[16,8,512]{2,1,0:T(8,128)S(1)}) custom-call(bf16[2,1,8,8192]{3,2,1,0:T(8,128)(2,1)S(1)} %collective-permute-done.7.refs_0_, bf16[2,1,8,8192]{3,2,1,0:T(8,128)(2,1)S(1)} %collective-permute-done.8.refs_1_, f32[16,64,256]{2,1,0:T(8,128)S(1)} %correlate.7.refs_2_, bf16[128,128]{1,0:T(8,128)(2,1)S(1)} %copy-done.11, ...), custom_call_target="tpu_custom_call" | custom-call | flops 1207959552 | bytes 1048576 | tf_op jit(solution)/shard_map/correlate/pallas_call | solution.py:315
  53.5 2.3 %collective-permute-done.refs_0_ = bf16[2,1,8,8192]{3,2,1,0:T(8,128)(2,1)S(1)} collective-permute-done((bf16[2,1,8,8192]{3,2,1,0:T(8,128)(2,1)S(1)}, bf16[2,1,8,8192]{3,2,1,0:T(8,128)(2,1)S(1)}, u32[]{:S(2)}, u32[]{:S(2)}) %collective-permute-start) | collective-permute-done | bytes 262176 | tf_op jit(solution)/shard_map/ppermute | solution.py:663
  56.0 3.1 %correlate.9 = (f32[32,16,512]{2,1,0:T(8,128)S(1)}, f32[16,8,512]{2,1,0:T(8,128)S(1)}) custom-call(bf16[2,1,8,8192]{3,2,1,0:T(8,128)(2,1)S(1)} %collective-permute-done.refs_0_, bf16[2,1,8,8192]{3,2,1,0:T(8,128)(2,1)S(1)} %collective-permute-done.1.refs_1_, f32[16,64,256]{2,1,0:T(8,128)S(1)} %correlate.7.refs_2_, ...), custom_call_target="tpu_custom_call", output_to_operand_aliasing={{0}: (3, {})} | custom-call | flops 1207959552 | bytes 1048576 | tf_op jit(solution)/shard_map/correlate/pallas_call | solution.py:315
  59.6 9.5 %network.1 = (bf16[80,8192]{1,0:T(8,128)(2,1)}, bf16[128,8192]{1,0:T(8,128)(2,1)}, bf16[128,8192]{1,0:T(8,128)(2,1)}, f32[64,8192]{1,0:T(8,128)}, f32[64,8192]{1,0:T(8,128)}) custom-call(s32[16,1]{1,0:T(8,128)} %constant.37.clone.factor_ref, f32[33,64]{1,0:T(8,128)} %bitcast.14, f32[1,64]{1,0:T(1,128)} %bitcast.16, f32[64,64]{1,0:T(8,128)} %refs_4_.6, ...), custom_call_target="tpu_custom_call" | custom-call | flops 629145600 | bytes 20971520 | tf_op jit(solution)/shard_map/network/pallas_call | solution.py:401
  70.0 7.9 %backward.1 = (f32[48,128]{1,0:T(8,128)}, f32[48,128]{1,0:T(8,128)}) custom-call(s32[1]{0:T(128)} %bitcast.3.place_ref, s32[1]{0:T(128)} %bitcast.4.second_ref, f32[32,16,512]{2,1,0:T(8,128)} %copy-done, f32[16,8,512]{2,1,0:T(8,128)} %copy-done.14, f32[16,8,512]{2,1,0:T(8,128)} %copy-done.13, bf16[80,8192]{1,0:T(8,128)(2,1)} %get-tuple-element.48.refs_2_, ...), custom_call_target="tpu_custom_call" | custom-call | flops 1048576000 | bytes 10485760 | tf_op jit(solution)/shard_map/backward/pallas_call | solution.py:520
  80.1 1.7 %collective-permute-start.12 = (f32[48,128]{1,0:T(8,128)S(1)}, f32[48,128]{1,0:T(8,128)S(1)}, u32[]{:S(2)}, u32[]{:S(2)}) collective-permute-start(f32[48,128]{1,0:T(8,128)S(1)} %add.25), channel_id=1, source_target_pairs={{0,8},{4,12},{8,0},{12,4},{16,24},{20,28},{24,16},{28,20},{1,9},{5... | collective-permute-start | bytes 73736 | tf_op jit(solution)/shard_map/ppermute | solution.py:566
  81.8 1.5 %collective-permute-start.13 = (f32[48,128]{1,0:T(8,128)S(1)}, f32[48,128]{1,0:T(8,128)S(1)}, u32[]{:S(2)}, u32[]{:S(2)}) collective-permute-start(f32[48,128]{1,0:T(8,128)S(1)} %add.25), channel_id=1, source_target_pairs={{0,16},{4,20},{8,24},{12,28},{16,0},{20,4},{24,8},{28,12},{1,17},{... | collective-permute-start | bytes 73736 | tf_op jit(solution)/shard_map/ppermute | solution.py:566
  83.6 6.0 %all-to-all-start = ((f32[32,16,512]{2,1,0:T(8,128)}), f32[32,16,512]{2,1,0:T(8,128)S(1)}, u32[]{:S(2)}, u32[]{:S(2)}) async-start(f32[32,16,512]{2,1,0:T(8,128)} %copy-done), calls=%async_computation | async-start | bytes 2097152 | tf_op jit(solution)/shard_map/all_to_all | solution.py:681
  89.7 1.8 %collective-permute-start.15 = (f32[72,128]{1,0:T(8,128)S(1)}, f32[72,128]{1,0:T(8,128)S(1)}, u32[]{:S(2)}, u32[]{:S(2)}) collective-permute-start(f32[72,128]{1,0:T(8,128)S(1)} %constant_dynamic-update-slice_fusion), channel_id=1, source_target_pairs={{0,1},{1,0},{2,3},{3,2},{4,5},{5,4},{6,7},{7,6},{8,9},{9,8},{10,11... | collective-permute-start | bytes 110600 | tf_op jit(solution)/shard_map/ppermute | solution.py:566
  91.6 2.4 %collective-permute-start.16 = (f32[72,128]{1,0:T(8,128)S(1)}, f32[72,128]{1,0:T(8,128)S(1)}, u32[]{:S(2)}, u32[]{:S(2)}) collective-permute-start(f32[72,128]{1,0:T(8,128)S(1)} %constant_dynamic-update-slice_fusion), channel_id=1, source_target_pairs={{0,2},{1,3},{2,0},{3,1},{4,6},{5,7},{6,4},{7,5},{8,10},{9,11},{10,... | collective-permute-start | bytes 110600 | tf_op jit(solution)/shard_map/ppermute | solution.py:566
  94.2 14.2 %collective-permute-done.15 = f32[72,128]{1,0:T(8,128)S(1)} collective-permute-done((f32[72,128]{1,0:T(8,128)S(1)}, f32[72,128]{1,0:T(8,128)S(1)}, u32[]{:S(2)}, u32[]{:S(2)}) %collective-permute-start.15) | collective-permute-done | bytes 36896 | tf_op jit(solution)/shard_map/ppermute | solution.py:566
  108.4 10.2 %collective-permute-done.16 = f32[72,128]{1,0:T(8,128)S(1)} collective-permute-done((f32[72,128]{1,0:T(8,128)S(1)}, f32[72,128]{1,0:T(8,128)S(1)}, u32[]{:S(2)}, u32[]{:S(2)}) %collective-permute-start.16) | collective-permute-done | bytes 36896 | tf_op jit(solution)/shard_map/ppermute | solution.py:566
  (79 shorter events, 10.7 us)
Async XLA Ops:
  5.8 7.3 %collective-permute-start.6 = (bf16[2,1,16,8192]{3,2,1,0:T(8,128)(2,1)}, bf16[2,1,16,8192]{3,2,1,0:T(8,128)(2,1)S(1)}, u32[]{:S(2)}, u32[]{:S(2)}) collective-permute-start(bf16[2,1,16,8192]{3,2,1,0:T(8,128)(2,1)} %get-tuple-element.41), channel_id=1, source_target_pairs={{0,4},{4,0},{8,12},{12,8},{16,20},{20,16},{24,28},{28,24},{1,5},{5... | collective-permute-start | bytes 1572872 | tf_op jit(solution)/shard_map/ppermute | solution.py:663
  6.3 16.4 %collective-permute-start.4 = (bf16[2,1,16,8192]{3,2,1,0:T(8,128)(2,1)S(1)}, bf16[2,1,16,8192]{3,2,1,0:T(8,128)(2,1)S(1)}, u32[]{:S(2)}, u32[]{:S(2)}) collective-permute-start(bf16[2,1,16,8192]{3,2,1,0:T(8,128)(2,1)S(1)} %copy-done.12), channel_id=1, source_target_pairs={{0,24},{4,28},{8,16},{12,20},{16,8},{20,12},{24,0},{28,4},{1,25},{... | collective-permute-start | bytes 1572872 | tf_op jit(solution)/shard_map/ppermute | solution.py:663
  9.8 23.6 %collective-permute-start.5 = (bf16[2,1,16,8192]{3,2,1,0:T(8,128)(2,1)S(1)}, bf16[2,1,16,8192]{3,2,1,0:T(8,128)(2,1)S(1)}, u32[]{:S(2)}, u32[]{:S(2)}) collective-permute-start(bf16[2,1,16,8192]{3,2,1,0:T(8,128)(2,1)S(1)} %copy-done.15), channel_id=1, source_target_pairs={{0,28},{4,24},{8,20},{12,16},{16,12},{20,8},{24,4},{28,0},{1,29},{... | collective-permute-start | bytes 1572872 | tf_op jit(solution)/shard_map/ppermute | solution.py:663
  9.9 35.7 %collective-permute-start.2 = (bf16[2,1,16,8192]{3,2,1,0:T(8,128)(2,1)}, bf16[2,1,16,8192]{3,2,1,0:T(8,128)(2,1)S(1)}, u32[]{:S(2)}, u32[]{:S(2)}) collective-permute-start(bf16[2,1,16,8192]{3,2,1,0:T(8,128)(2,1)} %get-tuple-element.37), channel_id=1, source_target_pairs={{0,8},{4,12},{8,0},{12,4},{16,24},{20,28},{24,16},{28,20},{1,9},{5... | collective-permute-start | bytes 1572872 | tf_op jit(solution)/shard_map/ppermute | solution.py:663
  11.6 34.2 %collective-permute-start.3 = (bf16[2,1,16,8192]{3,2,1,0:T(8,128)(2,1)}, bf16[2,1,16,8192]{3,2,1,0:T(8,128)(2,1)S(1)}, u32[]{:S(2)}, u32[]{:S(2)}) collective-permute-start(bf16[2,1,16,8192]{3,2,1,0:T(8,128)(2,1)} %get-tuple-element.38), channel_id=1, source_target_pairs={{0,16},{4,20},{8,24},{12,28},{16,0},{20,4},{24,8},{28,12},{1,17},{... | collective-permute-start | bytes 1572872 | tf_op jit(solution)/shard_map/ppermute | solution.py:663
  13.1 37.3 %collective-permute-start.7 = (bf16[2,1,8,8192]{3,2,1,0:T(8,128)(2,1)}, bf16[2,1,8,8192]{3,2,1,0:T(8,128)(2,1)S(1)}, u32[]{:S(2)}, u32[]{:S(2)}) collective-permute-start(bf16[2,1,8,8192]{3,2,1,0:T(8,128)(2,1)} %get-tuple-element.42), channel_id=1, source_target_pairs={{0,12},{4,8},{8,4},{12,0},{16,28},{20,24},{24,20},{28,16},{1,13},{... | collective-permute-start | bytes 786440 | tf_op jit(solution)/shard_map/ppermute | solution.py:663
  22.7 27.7 %collective-permute-start.8 = (bf16[2,1,8,8192]{3,2,1,0:T(8,128)(2,1)S(1)}, bf16[2,1,8,8192]{3,2,1,0:T(8,128)(2,1)S(1)}, u32[]{:S(2)}, u32[]{:S(2)}) collective-permute-start(bf16[2,1,8,8192]{3,2,1,0:T(8,128)(2,1)S(1)} %copy-done.18), channel_id=1, source_target_pairs={{0,20},{4,16},{8,28},{12,24},{16,4},{20,0},{24,12},{28,8},{1,21},{... | collective-permute-start | bytes 786440 | tf_op jit(solution)/shard_map/ppermute | solution.py:663
  33.4 22.4 %collective-permute-start = (bf16[2,1,8,8192]{3,2,1,0:T(8,128)(2,1)S(1)}, bf16[2,1,8,8192]{3,2,1,0:T(8,128)(2,1)S(1)}, u32[]{:S(2)}, u32[]{:S(2)}) collective-permute-start(bf16[2,1,8,8192]{3,2,1,0:T(8,128)(2,1)S(1)} %copy-done.17), channel_id=1, source_target_pairs={{0,12},{4,8},{8,4},{12,0},{16,28},{20,24},{24,20},{28,16},{1,13},{... | collective-permute-start | bytes 786440 | tf_op jit(solution)/shard_map/ppermute | solution.py:663
  45.7 10.3 %collective-permute-start.1 = (bf16[2,1,8,8192]{3,2,1,0:T(8,128)(2,1)S(1)}, bf16[2,1,8,8192]{3,2,1,0:T(8,128)(2,1)S(1)}, u32[]{:S(2)}, u32[]{:S(2)}) collective-permute-start(bf16[2,1,8,8192]{3,2,1,0:T(8,128)(2,1)S(1)} %copy-done.16), channel_id=1, source_target_pairs={{0,20},{4,16},{8,28},{12,24},{16,4},{20,0},{24,12},{28,8},{1,21},{... | collective-permute-start | bytes 786440 | tf_op jit(solution)/shard_map/ppermute | solution.py:663
  59.1 10.1 %collective-permute-start.10 = (f32[16,8,512]{2,1,0:T(8,128)S(1)}, f32[16,8,512]{2,1,0:T(8,128)S(1)}, u32[]{:S(2)}, u32[]{:S(2)}) collective-permute-start(f32[16,8,512]{2,1,0:T(8,128)S(1)} %get-tuple-element.47), channel_id=1, source_target_pairs={{0,4},{4,0},{8,12},{12,8},{16,20},{20,16},{24,28},{28,24},{1,5},{5... | collective-permute-start | bytes 786440 | tf_op jit(solution)/shard_map/ppermute | solution.py:678
  59.3 9.8 %collective-permute-start.9 = (f32[16,8,512]{2,1,0:T(8,128)S(1)}, f32[16,8,512]{2,1,0:T(8,128)S(1)}, u32[]{:S(2)}, u32[]{:S(2)}) collective-permute-start(f32[16,8,512]{2,1,0:T(8,128)S(1)} %get-tuple-element.46), channel_id=1, source_target_pairs={{0,4},{4,0},{8,12},{12,8},{16,20},{20,16},{24,28},{28,24},{1,5},{5... | collective-permute-start | bytes 786440 | tf_op jit(solution)/shard_map/ppermute | solution.py:678
  77.8 42.2 %copy-start.1 = (f32[64,64]{1,0:T(8,128)S(1)}, f32[64,64]{1,0:T(8,128)}, u32[]{:S(2)}) copy-start(f32[64,64]{1,0:T(8,128)} %refs_4_.6) | copy-start | bytes 49156
  77.8 42.2 %copy-start.2 = (f32[64,33]{0,1:T(8,128)S(1)}, f32[64,33]{0,1:T(8,128)}, u32[]{:S(2)}) copy-start(f32[64,33]{0,1:T(8,128)} %param.32) | copy-start | bytes 25348
  77.9 42.2 %copy-start.3 = (f32[2,64]{1,0:T(2,128)S(1)}, f32[2,64]{1,0:T(2,128)}, u32[]{:S(2)}) copy-start(f32[2,64]{1,0:T(2,128)} %refs_5_.5) | copy-start | bytes 1540
  77.9 42.2 %copy-start.4 = (f32[64]{0:T(128)S(1)}, f32[64]{0:T(128)}, u32[]{:S(2)}) copy-start(f32[64]{0:T(128)} %param.33) | copy-start | bytes 772
  77.9 1.5 %collective-permute-start.11 = (f32[48,128]{1,0:T(8,128)}, f32[48,128]{1,0:T(8,128)S(1)}, u32[]{:S(2)}, u32[]{:S(2)}) collective-permute-start(f32[48,128]{1,0:T(8,128)} %get-tuple-element.54), channel_id=1, source_target_pairs={{0,4},{4,0},{8,12},{12,8},{16,20},{20,16},{24,28},{28,24},{1,5},{5... | collective-permute-start | bytes 73736 | tf_op jit(solution)/shard_map/ppermute | solution.py:561
  80.1 9.5 %collective-permute-start.12 = (f32[48,128]{1,0:T(8,128)S(1)}, f32[48,128]{1,0:T(8,128)S(1)}, u32[]{:S(2)}, u32[]{:S(2)}) collective-permute-start(f32[48,128]{1,0:T(8,128)S(1)} %add.25), channel_id=1, source_target_pairs={{0,8},{4,12},{8,0},{12,4},{16,24},{20,28},{24,16},{28,20},{1,9},{5... | collective-permute-start | bytes 73736 | tf_op jit(solution)/shard_map/ppermute | solution.py:566
  81.8 7.9 %collective-permute-start.13 = (f32[48,128]{1,0:T(8,128)S(1)}, f32[48,128]{1,0:T(8,128)S(1)}, u32[]{:S(2)}, u32[]{:S(2)}) collective-permute-start(f32[48,128]{1,0:T(8,128)S(1)} %add.25), channel_id=1, source_target_pairs={{0,16},{4,20},{8,24},{12,28},{16,0},{20,4},{24,8},{28,12},{1,17},{... | collective-permute-start | bytes 73736 | tf_op jit(solution)/shard_map/ppermute | solution.py:566
  83.3 6.4 %collective-permute-start.14 = (f32[48,128]{1,0:T(8,128)S(1)}, f32[48,128]{1,0:T(8,128)S(1)}, u32[]{:S(2)}, u32[]{:S(2)}) collective-permute-start(f32[48,128]{1,0:T(8,128)S(1)} %add.25), channel_id=1, source_target_pairs={{0,24},{4,28},{8,16},{12,20},{16,8},{20,12},{24,0},{28,4},{1,25},{... | collective-permute-start | bytes 73736 | tf_op jit(solution)/shard_map/ppermute | solution.py:566
  83.6 37.4 %all-to-all-start = ((f32[32,16,512]{2,1,0:T(8,128)}), f32[32,16,512]{2,1,0:T(8,128)S(1)}, u32[]{:S(2)}, u32[]{:S(2)}) async-start(f32[32,16,512]{2,1,0:T(8,128)} %copy-done), calls=%async_computation | async-start | bytes 2097152 | tf_op jit(solution)/shard_map/all_to_all | solution.py:681
  89.7 18.6 %collective-permute-start.15 = (f32[72,128]{1,0:T(8,128)S(1)}, f32[72,128]{1,0:T(8,128)S(1)}, u32[]{:S(2)}, u32[]{:S(2)}) collective-permute-start(f32[72,128]{1,0:T(8,128)S(1)} %constant_dynamic-update-slice_fusion), channel_id=1, source_target_pairs={{0,1},{1,0},{2,3},{3,2},{4,5},{5,4},{6,7},{7,6},{8,9},{9,8},{10,11... | collective-permute-start | bytes 110600 | tf_op jit(solution)/shard_map/ppermute | solution.py:566
  91.6 27.0 %collective-permute-start.16 = (f32[72,128]{1,0:T(8,128)S(1)}, f32[72,128]{1,0:T(8,128)S(1)}, u32[]{:S(2)}, u32[]{:S(2)}) collective-permute-start(f32[72,128]{1,0:T(8,128)S(1)} %constant_dynamic-update-slice_fusion), channel_id=1, source_target_pairs={{0,2},{1,3},{2,0},{3,1},{4,6},{5,7},{6,4},{7,5},{8,10},{9,11},{10,... | collective-permute-start | bytes 110600 | tf_op jit(solution)/shard_map/ppermute | solution.py:566
  94.0 24.6 %collective-permute-start.17 = (f32[72,128]{1,0:T(8,128)S(1)}, f32[72,128]{1,0:T(8,128)S(1)}, u32[]{:S(2)}, u32[]{:S(2)}) collective-permute-start(f32[72,128]{1,0:T(8,128)S(1)} %constant_dynamic-update-slice_fusion), channel_id=1, source_target_pairs={{0,3},{1,2},{2,1},{3,0},{4,7},{5,6},{6,5},{7,4},{8,11},{9,10},{10,... | collective-permute-start | bytes 110600 | tf_op jit(solution)/shard_map/ppermute | solution.py:566
  118.7 1.3 %collective-permute-start.18 = (f32[168,128]{1,0:T(8,128)S(1)}, f32[168,128]{1,0:T(8,128)S(1)}, u32[]{:S(2)}, u32[]{:S(2)}) collective-permute-start(f32[168,128]{1,0:T(8,128)S(1)} %constant_dynamic-update-slice_fusion.5.refs_0_), channel_id=1, source_target_pairs={{0,4},{4,0},{8,12},{12,8},{16,20},{20,16},{24,28},{28,24},{1,5},{5... | collective-permute-start | bytes 258056 | tf_op jit(solution)/shard_map/ppermute | solution.py:569
  (15 other events, 108.8 us)
